TPU v7x, 32 devices: a whole 2x2x4 slice. The times are simulated.
32 devices in a mesh: wshard: 8 (over z, x), seq: 4 (over y, core).
Axes of the slice: x: 2, y: 2, z: 4, core: 2. Of those that a mesh axis runs over, the one named last changes fastest.
Arguments:
- hidden: bfloat16 [8, 2048, 1536], P('wshard', 'seq'), may hold values from -6 to 6
- segments: int32 [8, 2048], P('wshard'), may hold values from 0 to 3, never falling along the last dimension, each value on 1 to 1024 neighbouring positions
- norm_gain: bfloat16 [1536], P('wshard'), may hold values from 0.099609375 to 1.8984375
- in_weight: bfloat16 [1536, 6448], P('wshard'), may hold values from -0.15625 to 0.15625
- conv_weight: float32 [4, 3328], replicated, may hold values from -3 to 3
- conv_bias: float32 [3328], replicated, may hold values from -3 to 3
- step_bias: float32 [48], replicated, may hold values from -6 to -2
- decay_log: float32 [48], replicated, may hold values from 0 to 2.5
- skip_scale: float32 [48], replicated, may hold values from 0.5 to 1.5
- gate_gain: bfloat16 [3072], P('wshard'), may hold values from 0.099609375 to 1.8984375
- out_weight: bfloat16 [3072, 1536], P('wshard'), may hold values from -0.109375 to 0.109375
- cotangent: bfloat16 [8, 2048, 1536], P('wshard', 'seq'), may hold values from -6 to 6
Outputs:
- layer_output: float32 [8, 2048, 1536], P('wshard', 'seq')
- hidden_grad: float32 [8, 2048, 1536], P('wshard', 'seq')
- norm_gain_grad: float32 [1536], P('wshard')
- in_weight_grad: float32 [1536, 6448], P('wshard')
- conv_weight_grad: float32 [4, 3328], replicated
- conv_bias_grad: float32 [3328], replicated
- step_bias_grad: float32 [48], replicated
- decay_log_grad: float32 [48], replicated
- skip_scale_grad: float32 [48], replicated
- gate_gain_grad: float32 [3072], P('wshard')
- out_weight_grad: float32 [3072, 1536], P('wshard')
Inputs may be any that keep to these rules, and one draw needn't show every extreme that they name: `segments`: within each sequence document numbers never fall; each document spans 1 to 1024 consecutive tokens, one of them exactly that many.
All inputs are finite; a program needn't handle non-finite values.
Results may differ from a plain program's by a relative error of at most 0.011.
Values may be sent and summed in bfloat16 or wider, within the bound.
A program may use at most 256 MiB of HBM per device.

v0:
```python
import jax
import jax.numpy as jnp
from jax import lax
from jax.sharding import PartitionSpec as P

D = 1536
H = 48
P_SIZE = 64
N = 128
STRETCH = 256
E = 3072


eps = 1e-05
precise = lax.Precision.HIGHEST


def causal_conv(values, kernel, offsets, seg_ids):
    tap_count = kernel.shape[0]
    length_here = values.shape[0]
    padded = jnp.pad(values, ((tap_count - 1, 0), (0, 0)))
    seg_padded = jnp.concatenate([jnp.full((tap_count - 1,), -1, jnp.int32), seg_ids])
    summed = jnp.zeros_like(values) + offsets[None, :]
    for offset in range(tap_count):
        same_doc = (seg_padded[offset : offset + length_here] == seg_ids).astype(values.dtype)
        summed = (
            summed
            + kernel[offset][None, :] * padded[offset : offset + length_here] * same_doc[:, None]
        )
    return jax.nn.silu(summed)


def block_step(state, pieces):
    x_block, b_block, c_block, rate_block, step_block, seg_block, seg_before = pieces
    block_len = x_block.shape[0]
    cumul = jnp.cumsum(rate_block, axis=0)
    causal = jnp.arange(block_len)[:, None] >= jnp.arange(block_len)[None, :]
    allowed = (causal & (seg_block[:, None] == seg_block[None, :]))[:, :, None]
    spread = cumul[:, None, :] - cumul[None, :, :]
    decay = jnp.where(allowed, jnp.exp(jnp.where(allowed, spread, 0.0)), 0.0)
    affinity = jnp.dot(c_block, b_block.T, precision=precise)
    weighted = affinity[:, :, None] * decay * step_block[None, :, :]
    within = jnp.einsum("ijh,jhp->ihp", weighted, x_block, precision=precise)
    carried = (seg_block == seg_before).astype(rate_block.dtype)
    entering = (
        jnp.einsum("in,hnp->ihp", c_block, state, precision=precise)
        * (jnp.exp(cumul) * carried[:, None])[:, :, None]
    )
    last_cum = cumul[block_len - 1]
    same_last = (seg_block == seg_block[block_len - 1]).astype(rate_block.dtype)
    to_end = jnp.exp(last_cum[None, :] - cumul) * same_last[:, None] * step_block
    retained = jnp.exp(last_cum) * (seg_block[block_len - 1] == seg_before).astype(rate_block.dtype)
    new_state = state * retained[:, None, None] + jnp.einsum(
        "jn,jh,jhp->hnp", b_block, to_end, x_block, precision=precise
    )
    return (new_state, within + entering)


def state_scan(x_heads, b_vals, c_vals, decay_rates, step_sizes, seg_ids):
    length_here, head_count, head_dim = x_heads.shape
    blocks = length_here // STRETCH
    seg_blocks = seg_ids.reshape(blocks, STRETCH)
    seg_prior = jnp.concatenate([jnp.full((1,), -1, jnp.int32), seg_blocks[:-1, STRETCH - 1]])
    start_state = jnp.zeros((head_count, b_vals.shape[1], head_dim), x_heads.dtype)
    pieces = (
        x_heads.reshape(blocks, STRETCH, head_count, head_dim),
        b_vals.reshape(blocks, STRETCH, b_vals.shape[1]),
        c_vals.reshape(blocks, STRETCH, c_vals.shape[1]),
        decay_rates.reshape(blocks, STRETCH, head_count),
        step_sizes.reshape(blocks, STRETCH, head_count),
        seg_blocks,
        seg_prior,
    )
    _, results = lax.scan(jax.checkpoint(block_step), start_state, pieces)
    return results.reshape(length_here, head_count, head_dim)


def mixer(
    x_raw,
    bc_raw,
    dt_raw,
    conv_weight,
    conv_bias,
    step_bias,
    decay_log,
    skip_scale,
    seg_ids,
    head_start,
    chan_start,
):
    channels = x_raw.shape[1]
    head_count = dt_raw.shape[1]
    head_dim = channels // head_count
    state_dim = bc_raw.shape[1] // 2
    inner_width = conv_weight.shape[1] - 2 * state_dim
    x_conv = causal_conv(
        x_raw,
        lax.dynamic_slice_in_dim(conv_weight, chan_start, channels, 1),
        lax.dynamic_slice_in_dim(conv_bias, chan_start, channels, 0),
        seg_ids,
    )
    bc_conv = causal_conv(bc_raw, conv_weight[:, inner_width:], conv_bias[inner_width:], seg_ids)
    x_heads = x_conv.reshape(-1, head_count, head_dim)
    step_sizes = jax.nn.softplus(
        dt_raw + lax.dynamic_slice_in_dim(step_bias, head_start, head_count, 0)[None, :]
    )
    decay_rates = -jnp.exp(lax.dynamic_slice_in_dim(decay_log, head_start, head_count, 0))
    scanned = state_scan(
        x_heads,
        bc_conv[:, :state_dim],
        bc_conv[:, state_dim:],
        step_sizes * decay_rates[None, :],
        step_sizes,
        seg_ids,
    )
    skipped = (
        scanned
        + lax.dynamic_slice_in_dim(skip_scale, head_start, head_count, 0)[None, :, None] * x_heads
    )
    return skipped.reshape(-1, channels)


def pre_norm(hidden_rows, gain_full):
    scale = lax.rsqrt(jnp.mean(hidden_rows * hidden_rows, axis=-1, keepdims=True) + eps)
    return hidden_rows * scale * gain_full[None, :]


def gated_norm(mixed_rows, gate_part, gain_full):
    gated = mixed_rows * jax.nn.silu(gate_part)
    gate_scale = lax.rsqrt(jnp.mean(gated * gated, axis=-1, keepdims=True) + eps)
    return gated * gate_scale * gain_full[None, :]


def over_rows(left, right):
    return lax.dot_general(
        left, right, (((0,), (0,)), ((), ())), preferred_element_type=jnp.float32
    )


def shards(
    hidden,
    segments,
    norm_gain,
    in_weight,
    conv_weight,
    conv_bias,
    step_bias,
    decay_log,
    skip_scale,
    gate_gain,
    out_weight,
    cotangent,
):
    seq_count, piece_len, _ = hidden.shape
    row_count = seq_count * piece_len
    group_heads = H // lax.axis_size("seq")
    head_start = lax.axis_index("seq") * group_heads
    chan_start = head_start * P_SIZE
    in_full, norm_full, out_full, gate_full = (
        lax.all_gather(in_weight, "wshard", axis=0, tiled=True),
        lax.all_gather(norm_gain, "wshard", axis=0, tiled=True),
        lax.all_gather(out_weight, "wshard", axis=0, tiled=True),
        lax.all_gather(gate_gain, "wshard", axis=0, tiled=True),
    )
    hidden_rows = hidden.astype(jnp.float32).reshape(row_count, D)
    normed_low = pre_norm(hidden_rows, norm_full.astype(jnp.float32)).astype(jnp.bfloat16)
    projected = jnp.dot(normed_low, in_full, preferred_element_type=jnp.float32)
    gate_part = projected[:, :E]
    x_low = projected[:, E : 2 * E].astype(jnp.bfloat16).reshape(seq_count, piece_len, E)
    bc_low = (
        projected[:, 2 * E : 2 * E + 2 * N]
        .astype(jnp.bfloat16)
        .reshape(seq_count, piece_len, 2 * N)
    )
    dt_low = projected[:, 2 * E + 2 * N :].astype(jnp.bfloat16).reshape(seq_count, piece_len, H)
    x_heads, dt_heads = (
        lax.all_to_all(x_low, "seq", split_axis=2, concat_axis=1, tiled=True),
        lax.all_to_all(dt_low, "seq", split_axis=2, concat_axis=1, tiled=True),
    )
    bc_whole = lax.all_gather(bc_low, "seq", axis=1, tiled=True)

    def mixer_all(x_in, bc_in, dt_in, kernel, offsets, bias_in, log_in, skip_in):

        def one_seq(items):
            x_seq, bc_seq, dt_seq, seg_seq = items
            return mixer(
                x_seq,
                bc_seq,
                dt_seq,
                kernel,
                offsets,
                bias_in,
                log_in,
                skip_in,
                seg_seq,
                head_start,
                chan_start,
            )

        return lax.map(one_seq, (x_in, bc_in, dt_in, segments))

    mixed_heads, mixer_pull = jax.vjp(
        mixer_all,
        x_heads.astype(jnp.float32),
        bc_whole.astype(jnp.float32),
        dt_heads.astype(jnp.float32),
        conv_weight,
        conv_bias,
        step_bias,
        decay_log,
        skip_scale,
    )
    mixed_pieces = lax.all_to_all(
        mixed_heads.astype(jnp.bfloat16), "seq", split_axis=1, concat_axis=2, tiled=True
    )
    mixed_rows = mixed_pieces.reshape(row_count, E).astype(jnp.float32)
    gated_low = gated_norm(mixed_rows, gate_part, gate_full.astype(jnp.float32)).astype(
        jnp.bfloat16
    )
    layer_output = hidden_rows + jnp.dot(gated_low, out_full, preferred_element_type=jnp.float32)
    cot_rows = cotangent.reshape(row_count, D)
    d_gated = lax.dot_general(
        cot_rows, out_full, (((1,), (1,)), ((), ())), preferred_element_type=jnp.float32
    )
    _, gate_pull = jax.vjp(gated_norm, mixed_rows, gate_part, gate_full.astype(jnp.float32))
    d_mixed, d_gate_part, gate_gain_term = gate_pull(d_gated)
    d_mixed_heads = lax.all_to_all(
        d_mixed.astype(jnp.bfloat16).reshape(seq_count, piece_len, E),
        "seq",
        split_axis=2,
        concat_axis=1,
        tiled=True,
    )
    d_x_heads, d_bc_whole, d_dt_heads, kernel_sum, offset_sum, bias_sum, log_sum, skip_sum = (
        mixer_pull(d_mixed_heads.astype(jnp.float32))
    )
    conv_weight_grad, conv_bias_grad, step_bias_grad, decay_log_grad, skip_scale_grad = lax.psum(
        (kernel_sum, offset_sum, bias_sum, log_sum, skip_sum), ("wshard", "seq")
    )
    d_x_low = d_x_heads.astype(jnp.bfloat16)
    d_dt_low = d_dt_heads.astype(jnp.bfloat16)
    d_x_pieces, d_dt_pieces = (
        lax.all_to_all(d_x_low, "seq", split_axis=1, concat_axis=2, tiled=True),
        lax.all_to_all(d_dt_low, "seq", split_axis=1, concat_axis=2, tiled=True),
    )
    d_bc_pieces = lax.psum_scatter(
        d_bc_whole.astype(jnp.bfloat16), "seq", scatter_dimension=1, tiled=True
    )
    d_gate_low = d_gate_part.astype(jnp.bfloat16)
    d_projected = jnp.concatenate(
        [
            d_gate_low,
            d_x_pieces.reshape(row_count, E),
            d_bc_pieces.reshape(row_count, 2 * N),
            d_dt_pieces.reshape(row_count, H),
        ],
        axis=1,
    )
    d_normed = lax.dot_general(
        d_projected, in_full, (((1,), (1,)), ((), ())), preferred_element_type=jnp.float32
    )
    _, norm_pull = jax.vjp(pre_norm, hidden_rows, norm_full.astype(jnp.float32))
    hidden_term, norm_gain_term = norm_pull(d_normed)
    hidden_grad = (cot_rows.astype(jnp.float32) + hidden_term).reshape(seq_count, piece_len, D)
    in_weight_term = over_rows(normed_low, d_projected)
    out_weight_term = over_rows(gated_low, cot_rows)
    shard_sums = (
        lax.psum_scatter(in_weight_term, "wshard", scatter_dimension=0, tiled=True),
        lax.psum_scatter(norm_gain_term, "wshard", scatter_dimension=0, tiled=True),
        lax.psum_scatter(out_weight_term, "wshard", scatter_dimension=0, tiled=True),
        lax.psum_scatter(gate_gain_term, "wshard", scatter_dimension=0, tiled=True),
    )
    in_weight_grad, norm_gain_grad, out_weight_grad, gate_gain_grad = (
        lax.psum(shard_sums[0].astype(jnp.bfloat16), "seq").astype(jnp.float32),
        lax.psum(shard_sums[1].astype(jnp.bfloat16), "seq").astype(jnp.float32),
        lax.psum(shard_sums[2].astype(jnp.bfloat16), "seq").astype(jnp.float32),
        lax.psum(shard_sums[3].astype(jnp.bfloat16), "seq").astype(jnp.float32),
    )
    return (
        layer_output.reshape(seq_count, piece_len, D),
        hidden_grad,
        norm_gain_grad,
        in_weight_grad,
        conv_weight_grad,
        conv_bias_grad,
        step_bias_grad,
        decay_log_grad,
        skip_scale_grad,
        gate_gain_grad,
        out_weight_grad,
    )


def solution(mesh):
    in_specs = (
        P("wshard", "seq", None),
        P("wshard", None),
        P("wshard"),
        P("wshard", None),
        P(),
        P(),
        P(),
        P(),
        P(),
        P("wshard"),
        P("wshard", None),
        P("wshard", "seq", None),
    )
    out_specs = (
        P("wshard", "seq", None),
        P("wshard", "seq", None),
        P("wshard"),
        P("wshard", None),
        P(),
        P(),
        P(),
        P(),
        P(),
        P("wshard"),
        P("wshard", None),
    )
    return jax.shard_map(shards, mesh=mesh, in_specs=in_specs, out_specs=out_specs, check_vma=False)
```

profile of v0, /device:TPU:0, one launch (start us, length us, event | category | flops | bytes accessed | tf_op | source)
XLA Modules:
  0.0 2986.6 jit_solution(9371011800629736709)
XLA Ops:
  10.8 47.5 %all-reduce.24 = bf16[1536]{0:T(1024)(128)(2,1)S(1)} all-reduce(bf16[1536]{0:T(1024)(128)(2,1)S(1)} %dynamic-update-slice.15), channel_id=1, replica_groups=mesh['wshard'=8,'seq'=4] {'wshard'}, use_global_device_ids=true, to_apply=%add.24 | all-reduce | flops 1536 | bytes 6144
  60.7 336.6 %all-gather.6.cloned.1.call-done = bf16[1536,6448]{1,0:T(8,128)(2,1)} async-done(((bf16[192,6448]{1,0:T(8,128)(2,1)}), bf16[1536,6448]{1,0:T(8,128)(2,1)}) %all-gather.6.cloned.1.call-update) | async-done | bytes 19808272 | tf_op jit(solution)/shard_map/all_gather | solution.py:160
  427.4 27.4 copy.490
  454.8 20.3 reduce.35
  576.7 312.3 %while.143 = (s32[]{:T(128)}, f32[12,128,64]{1,2,0:T(8,128)S(1)}, f32[8,256,12,64]{1,0,3,2:T(8,128)}, f32[8,12,128,64]{2,3,1,0:T(8,128)}, f32[8,256,12]{1,2,0:T(...) while((s32[]{:T(128)}, f32[12,128,64]{1,2,0:T(8,128)S(1)}, ...), condition=%wide.region_4.5_spmd.clone, body=%wide.region_1.4_spmd.clone.sunk | while | flops 1314042880 | bytes 11014881 | solution.py:74
  594.0 18.5 dynamic_update_slice.219
  633.0 18.5 dynamic_update_slice.219
  909.8 44.7 %copy.489 = bf16[1,2048,768]{2,0,1:T(2,128)(2,1)} copy(bf16[1,2048,768]{2,1,0:T(8,128)(2,1)S(1)} %fusion.107) | data formatting | bytes 6291456 | tf_op jit(solution)/shard_map/convert_element_type | solution.py:214
  954.5 31.6 %reduce.36 = bf16[2048,768]{1,0:T(8,128)(2,1)S(1)} reduce(bf16[2048,1,768]{2,1,0:T(2,128)(2,1)} %bitcast.482, bf16[]{:T(256)} %broadcast.726), dimensions={1}, to_apply=%bitcast.320.reduce_sub_computation | reduce | bytes 6291458
  992.3 25.9 all-gather.1
  1074.9 27.4 copy.488
  1102.3 20.4 reduce.37
  1130.0 36.8 %all-to-all-done.3 = bf16[4,2,196608]{2,1,0:T(2,128)(2,1)S(1)} async-done(((bf16[4,2,196608]{2,1,0:T(2,128)(2,1)}), bf16[4,2,196608]{2,1,0:T(2,128)(2,1)S(1)}, u32[]{:S(2)}, u32[]{:S(2)}) %all-to-all-start.3) | async-done | bytes 3145760 | tf_op jit(solution)/shard_map/all_to_all | solution.py:227
  1200.2 566.3 %while.144 = (s32[]{:T(128)}, f32[12,128,64]{1,2,0:T(8,128)S(1)}, f32[8,256,12,64]{1,0,3,2:T(8,128)}, f32[8,256,128]{2,1,0:T(8,128)}, f32[8,256,128]{2,1,0:T(8,1...) while((s32[]{:T(128)}, f32[12,128,64]{1,2,0:T(8,128)S(1)}, ...), condition=%wide.region_19.20_spmd.clone, body=%wide.region_7.19_spmd.clone.sunk | while | flops 3038930944 | bytes 28993192 | solution.py:74
  1832.9 20.7 multiply_reduce_fusion.7
  1865.5 44.8 %copy.487 = bf16[1,2048,768]{2,0,1:T(2,128)(2,1)} copy(bf16[1,2048,768]{2,1,0:T(8,128)(2,1)S(1)} %fusion.111) | data formatting | bytes 6291456 | tf_op jit(solution)/shard_map/convert_element_type | solution.py:240
  1910.3 31.6 %reduce.39 = bf16[2048,768]{1,0:T(8,128)(2,1)S(1)} reduce(bf16[2048,1,768]{2,1,0:T(2,128)(2,1)} %bitcast.476, bf16[]{:T(256)} %broadcast.726), dimensions={1}, to_apply=%bitcast.318.reduce_sub_computation | reduce | bytes 6291458
  1953.4 31.6 %all-to-all-done.4 = bf16[4,2,196608]{2,1,0:T(2,128)(2,1)S(1)} async-done(((bf16[4,2,196608]{2,1,0:T(2,128)(2,1)}), bf16[4,2,196608]{2,1,0:T(2,128)(2,1)S(1)}, u32[]{:S(2)}, u32[]{:S(2)}) %all-to-all-start.4) | async-done | bytes 3145760 | tf_op jit(solution)/shard_map/all_to_all | solution.py:243
  1999.1 21.1 fusion.120
  2021.5 100.1 %reduce-scatter.8.cloned.1.call-done = f32[384,1536]{1,0:T(8,128)} async-done(((f32[3072,1536]{1,0:T(8,128)}), f32[384,1536]{1,0:T(8,128)}) %reduce-scatter.8.cloned.1.call-update) | async-done | bytes 2359312 | tf_op jit(solution)/shard_map/reduce_scatter | solution.py:270
  2124.4 640.7 %reduce-scatter.6.cloned.1.call-done = f32[192,6448]{1,0:T(8,128)} async-done(((f32[1536,6448]{1,0:T(8,128)}), f32[192,6448]{1,0:T(8,128)}) %reduce-scatter.6.cloned.1.call-update) | async-done | bytes 4952080 | tf_op jit(solution)/shard_map/reduce_scatter | solution.py:268
  2783.2 26.7 fusion.104
  2814.4 35.0 %all-reduce.28 = (bf16[1536]{0:T(1024)(128)(2,1)S(1)}, bf16[3072]{0:T(1024)(128)(2,1)S(1)}) all-reduce(f32[1536]{0:T(1024)S(1)} %get-tuple-element.1746, f32[3072]{0:T(1024)S(1)} %copy-done.45), channel_id=4, replica_groups=mesh['wshard'=8,'seq'=4] {'wshard'}, use_global_device_ids=true, to_apply=%region_23.24.clone | all-reduce | flops 4608 | bytes 27648
  2862.5 111.0 %all-reduce.34.cloned.1.call-done = (f32[4,3328]{1,0:T(4,128)}, f32[3328]{0:T(1024)}, f32[48]{0:T(128)}, f32[48]{0:T(128)}, f32[48]{0:T(128)}) async-done(((f32[4,3328]{1,0:T(4,128)}, f32[3328]{0:T(1024)}, f32[48]{0:T(128)}, f32[48]{0:T(128)}, f32[48]{0:T(128)}), (f32[4,3328]{1,0:T(4,128)}, f32[3328]{0:T(1024)}, f32[48]{0:T(128)}, f32[48]{0:T(128)}, f32[48]{0:T(128)})) %all-reduce.34.cloned.1.call-update) | async-done | bytes 67152 | tf_op jit(solution)/shard_map/psum | solution.py:237
  (1048 shorter events, 1227.1 us)
Async XLA Ops:
  7.2 390.1 %all-gather.6.cloned.1.call-start = ((), (), s32[]{:S(2)}) async-start(), calls=%async_computation.9 | async-start | bytes 22560768 | tf_op jit(solution)/shard_map/all_gather | solution.py:160
  7.9 495.7 %all-gather.10.cloned.1.call-start = ((), (), s32[]{:S(2)}) async-start(), calls=%async_computation.14 | async-start | bytes 1310720 | tf_op jit(solution)/shard_map/all_gather | solution.py:180
  58.3 356.3 %copy-start.39 = (f32[1536]{0:T(1024)}, f32[1536]{0:T(1024)S(1)}, u32[]{:S(2)}) copy-start(f32[1536]{0:T(1024)S(1)} %convert_element_type.262) | copy-start | bytes 18436
  60.7 354.0 %copy-start.50 = (f32[512]{0:T(512)}, f32[512]{0:T(512)S(1)}, u32[]{:S(2)}) copy-start(f32[512]{0:T(512)S(1)} %fusion.144) | copy-start | bytes 6148
  418.1 636.5 %all-gather.8.cloned.1.call-start = ((), (), s32[]{:S(2)}) async-start(), calls=%async_computation.10 | async-start | bytes 10616832 | tf_op jit(solution)/shard_map/all_gather | solution.py:162
  421.8 56.8 %all-to-all-start = ((bf16[4,2,3072]{2,1,0:T(2,128)(2,1)}), bf16[4,2,3072]{2,1,0:T(2,128)(2,1)S(1)}, u32[]{:S(2)}, u32[]{:S(2)}) async-start(bf16[4,2,3072]{2,1,0:T(2,128)(2,1)} %reshape.1078), calls=%async_computation | async-start | bytes 98304 | tf_op jit(solution)/shard_map/all_to_all | solution.py:178
  478.7 41.1 %all-to-all-start.1 = ((bf16[4,2,196608]{2,1,0:T(2,128)(2,1)}), bf16[4,2,196608]{2,1,0:T(2,128)(2,1)S(1)}, u32[]{:S(2)}, u32[]{:S(2)}) async-start(bf16[4,2,196608]{2,1,0:T(2,128)(2,1)} %reshape.1080), calls=%async_computation.1 | async-start | bytes 6291456 | tf_op jit(solution)/shard_map/all_to_all | solution.py:177
  495.9 42.0 %copy-start.15 = (f32[2048]{0:T(1024)}, f32[2048]{0:T(1024)S(1)}, u32[]{:S(2)}) copy-start(f32[2048]{0:T(1024)S(1)} %get-tuple-element.1868) | copy-start | bytes 24580
  495.9 42.0 %copy-start.17 = (f32[2048]{0:T(1024)}, f32[2048]{0:T(1024)S(1)}, u32[]{:S(2)}) copy-start(f32[2048]{0:T(1024)S(1)} %get-tuple-element.1869) | copy-start | bytes 24580
  988.5 40.6 %all-to-all-start.2 = ((bf16[4,2,196608]{2,1,0:T(2,128)(2,1)}), bf16[4,2,196608]{2,1,0:T(2,128)(2,1)S(1)}, u32[]{:S(2)}, u32[]{:S(2)}) async-start(bf16[4,2,196608]{2,1,0:T(2,128)(2,1)} %reshape.1082), calls=%async_computation.2 | async-start | bytes 6291456 | tf_op jit(solution)/shard_map/all_to_all | solution.py:213
  1018.2 49.3 %copy-start.21 = (f32[8,1,384]{2,1,0:T(1,128)}, f32[8,1,384]{2,1,0:T(1,128)S(1)}, u32[]{:S(2)}) copy-start(f32[8,1,384]{2,1,0:T(1,128)S(1)} %convert_element_type.323) | copy-start | bytes 36868
  1126.3 40.6 %all-to-all-start.3 = ((bf16[4,2,196608]{2,1,0:T(2,128)(2,1)}), bf16[4,2,196608]{2,1,0:T(2,128)(2,1)S(1)}, u32[]{:S(2)}, u32[]{:S(2)}) async-start(bf16[4,2,196608]{2,1,0:T(2,128)(2,1)} %reshape.1084), calls=%async_computation.3 | async-start | bytes 6291456 | tf_op jit(solution)/shard_map/all_to_all | solution.py:227
  1130.0 869.1 %reduce-scatter.4.cloned.1.call-start = ((), (), s32[]{:S(2)}) async-start(), calls=%async_computation.11 | async-start | bytes 1310720 | tf_op jit(solution)/shard_map/reduce_scatter | solution.py:246
  1779.9 341.7 %reduce-scatter.8.cloned.1.call-start = ((), (), s32[]{:S(2)}) async-start(), calls=%async_computation.13 | async-start | bytes 21233664 | tf_op jit(solution)/shard_map/reduce_scatter | solution.py:270
  1808.2 24.7 copy-start.36
  1829.6 114.8 %all-to-all-start.5 = ((bf16[4,2,3072]{2,1,0:T(2,128)(2,1)}), bf16[4,2,3072]{2,1,0:T(2,128)(2,1)S(1)}, u32[]{:S(2)}, u32[]{:S(2)}) async-start(bf16[4,2,3072]{2,1,0:T(2,128)(2,1)} %reshape.1086), calls=%async_computation.6 | async-start | bytes 98304 | tf_op jit(solution)/shard_map/all_to_all | solution.py:244
  1832.8 20.8 copy-start.28
  1832.9 20.8 copy-start.30
  1944.3 40.7 %all-to-all-start.4 = ((bf16[4,2,196608]{2,1,0:T(2,128)(2,1)}), bf16[4,2,196608]{2,1,0:T(2,128)(2,1)S(1)}, u32[]{:S(2)}, u32[]{:S(2)}) async-start(bf16[4,2,196608]{2,1,0:T(2,128)(2,1)} %reshape.1088), calls=%async_computation.4 | async-start | bytes 6291456 | tf_op jit(solution)/shard_map/all_to_all | solution.py:243
  1948.0 817.1 %reduce-scatter.6.cloned.1.call-start = ((), (), s32[]{:S(2)}) async-start(), calls=%async_computation.12 | async-start | bytes 45121536 | tf_op jit(solution)/shard_map/reduce_scatter | solution.py:268
  2020.1 836.2 %all-reduce.36.cloned.1.call-start = ((), (), s32[]{:S(2)}) async-start(), calls=%async_computation.16 | async-start | bytes 7372800 | tf_op jit(solution)/shard_map/psum | solution.py:274
  2769.3 204.2 %all-reduce.34.cloned.1.call-start = ((), (), s32[]{:S(2)}) async-start(), calls=%async_computation.15 | async-start | bytes 142336 | tf_op jit(solution)/shard_map/psum | solution.py:237
  2783.2 26.7 copy-start.43
  2783.2 26.7 copy-start.9
  (68 other events, 515.5 us)
Sparse Core Ops, SparseCore 0:
  9.5 387.7 all-gather.5
  418.2 17.2 all-gather.9
  437.7 137.6 all-gather.7
  1780.0 23.9 reduce-scatter.3
  1808.2 313.3 reduce-scatter.7
  2125.9 639.1 reduce-scatter.5
  2769.3 76.7 all-reduce.35
  2853.6 119.8 all-reduce.33
where the time goes:
time: 3010 us; the launch traced here: 2990 us
  waiting for transfers between devices  1270 us (42%)
  local copies, waits for them, and re-layouts  850 us (28%)
  other arithmetic  352 us (12%)
  matrix products  335 us (11%)
  blocking collectives  114 us (4%)
    reduce_scatter x1, waiting for transfers between devices, shards(): lax.psum_scatter(in_weight_term, 'wshard', scatter_dimension=0, tiled=True)  641 us
    all_gather x1, waiting for transfers between devices, shards(): lax.all_gather(in_weight, 'wshard', axis=0, tiled=True)  337 us
    dynamic_update_slice x48, local copies, waits for them, and re-layouts, state_scan(): _, results = lax.scan(jax.checkpoint(block_step), start_state, pieces)  322 us
    dot_general x24, matrix products, block_step(): within = jnp.einsum('ijh,jhp->ihp', weighted, x_block, precision=precise)  124 us
    unnamed x10, other arithmetic  117 us
    psum x1, waiting for transfers between devices, shards(): lax.psum((kernel_sum, offset_sum, bias_sum, log_sum, skip_sum), ('wshard'...  111 us
    reduce_scatter x1, waiting for transfers between devices, shards(): lax.psum_scatter(out_weight_term, 'wshard', scatter_dimension=0, tiled=True)  100 us
    unnamed x157, local copies, waits for them, and re-layouts  93.5 us
  transfers between devices with their start and end apart: 14, of which 8 were waited for; matrix products, arithmetic and copies ran while one was open for 28% of the time, Pallas kernels for 0%

commit v1 on v0

v1 whole, which is shorter than its diff:
```python
import jax
import jax.numpy as jnp
from jax import lax
from jax.experimental import pallas as pl
from jax.experimental.pallas import tpu as pltpu
from jax.sharding import PartitionSpec as P

D = 1536
H = 48
P_SIZE = 64
N = 128
E = 3072

eps = 1e-05
f32, bf16 = jnp.float32, jnp.bfloat16
Q = 128
NEG = -1e30


def dot(a, b):
    return jnp.dot(a, b, preferred_element_type=f32)


def dot_nt(a, b):
    return lax.dot_general(a, b, (((1,), (1,)), ((), ())), preferred_element_type=f32)


def dot3(tri, v):
    hi = v.astype(bf16)
    rest = v - hi.astype(f32)
    mid = rest.astype(bf16)
    low = (rest - mid.astype(f32)).astype(bf16)
    return dot(tri, hi) + dot(tri, mid) + dot(tri, low)


def sigmoid(v):
    return 1.0 / (1.0 + jnp.exp(-v))


def spread_col(v, col):
    return jnp.broadcast_to(v[:, col : col + 1], (Q, 128))


def softplus(v):
    return jnp.maximum(v, 0.0) + jnp.log1p(jnp.exp(-jnp.abs(v)))


def chunk_masks(segc, segr):
    row = lax.broadcasted_iota(jnp.int32, (Q, Q), 0)
    col = lax.broadcasted_iota(jnp.int32, (Q, Q), 1)
    return row, col, segc == segr


def conv_pre(useen, flags, wk, bias, lanes):
    now = useen[8 : 8 + Q, lanes]
    pre = bias[:, lanes] + wk[3:4, lanes] * now
    shifted = [now]
    for j in (1, 2, 3):
        moved = useen[8 - j : 8 - j + Q, lanes] * flags[j]
        shifted.append(moved)
        pre = pre + wk[3 - j : 4 - j, lanes] * moved
    return pre, shifted


def fwd_kernel(u_ref, dt_ref, tok_ref, segc_ref, segr_ref, wk_ref, bias_ref, head_ref, skip_ref,
               mixed_ref, save_ref, state, useen, act):
    step_no = pl.program_id(0)
    width = u_ref.shape[1]
    xw = width - 256
    pairs = xw // 128

    @pl.when(step_no == 0)
    def _():
        state[...] = jnp.zeros_like(state)
        useen[0:8, :] = jnp.zeros((8, width), f32)

    useen[8 : 8 + Q, :] = u_ref[...].astype(f32)
    flags = [None] + [spread_col(tok_ref[...], j) for j in range(3)]
    carried = spread_col(tok_ref[...], 3)
    samelast = spread_col(tok_ref[...], 4)
    for p in range(width // 128):
        lanes = slice(128 * p, 128 * p + 128)
        pre, _ = conv_pre(useen, flags, wk_ref, bias_ref, lanes)
        act[:, lanes] = pre * sigmoid(pre)
    tail = useen[Q : Q + 8, :]
    useen[0:8, :] = tail

    step = softplus(dt_ref[...].astype(f32) + head_ref[0:1, :])
    row = lax.broadcasted_iota(jnp.int32, (Q, Q), 0)
    col = lax.broadcasted_iota(jnp.int32, (Q, Q), 1)
    tri = jnp.where(row >= col, 1.0, 0.0).astype(bf16)
    decay = dot3(tri, step * head_ref[1:2, :])
    decay_t = decay.T
    madd = jnp.where((row >= col) & (segc_ref[...] == segr_ref[0]), 0.0, NEG)
    b_now = act[:, xw : xw + 128]
    c_low = act[:, xw + 128 : xw + 256].astype(bf16)
    gram = dot_nt(c_low, b_now.astype(bf16))
    b_t = b_now.T.astype(bf16)
    left = lax.broadcasted_iota(jnp.int32, (Q, 128), 1) < 64
    for p in range(pairs):
        lanes = slice(128 * p, 128 * p + 128)
        d0, d1 = spread_col(decay, 2 * p), spread_col(decay, 2 * p + 1)
        dp = jnp.where(left, d0, d1)
        sp = jnp.where(left, spread_col(step, 2 * p), spread_col(step, 2 * p + 1))
        xs = act[:, lanes]
        xp = xs * sp
        m0 = gram * jnp.exp(d0 - decay_t[2 * p : 2 * p + 1, :] + madd)
        m1 = gram * jnp.exp(d1 - decay_t[2 * p + 1 : 2 * p + 2, :] + madd)
        both = jnp.concatenate([m0.astype(bf16), m1.astype(bf16)], axis=1)
        stacked = jnp.concatenate(
            [jnp.where(left, xp, 0.0).astype(bf16), jnp.where(left, 0.0, xp).astype(bf16)], axis=0
        )
        st = state[:, lanes]
        st_low = st.astype(bf16)
        save_ref[0, :, lanes] = st_low
        y = dot(both, stacked) + dot(c_low, st_low) * (jnp.exp(dp) * carried)
        mixed_ref[:, lanes] = (y + skip_ref[:, lanes] * xs).astype(bf16)
        last = dp[Q - 1 : Q, :]
        to_end = (xp * (jnp.exp(last - dp) * samelast)).astype(bf16)
        state[:, lanes] = st * (jnp.exp(last) * carried[Q - 1 : Q, :]) + dot(b_t, to_end)


def mixer_fwd(u, dt, tok, segc, segr, wk, bias, head, skip):
    length, width = u.shape
    xw = width - 256
    n = length // Q
    whole = lambda shape: pl.BlockSpec(shape, lambda i: (0,) * len(shape))
    return pl.pallas_call(
        fwd_kernel,
        grid=(n,),
        in_specs=[
            pl.BlockSpec((Q, width), lambda i: (i, 0)),
            pl.BlockSpec((Q, 128), lambda i: (i, 0)),
            pl.BlockSpec((Q, 8), lambda i: (i, 0)),
            pl.BlockSpec((Q, 1), lambda i: (i, 0)),
            pl.BlockSpec((1, 1, Q), lambda i: (i, 0, 0)),
            whole((4, width)),
            whole((1, width)),
            whole((2, 128)),
            whole((1, xw)),
        ],
        out_specs=[
            pl.BlockSpec((Q, xw), lambda i: (i, 0)),
            pl.BlockSpec((1, 128, xw), lambda i: (i, 0, 0)),
        ],
        out_shape=[
            jax.ShapeDtypeStruct((length, xw), bf16),
            jax.ShapeDtypeStruct((n, 128, xw), bf16),
        ],
        scratch_shapes=[
            pltpu.VMEM((128, xw), f32),
            pltpu.VMEM((Q + 8, width), f32),
            pltpu.VMEM((Q, width), f32),
        ],
        compiler_params=pltpu.CompilerParams(vmem_limit_bytes=48 * 2**20),
        name="mixer_forward",
    )(u, dt, tok, segc, segr, wk, bias, head, skip)


def bwd_kernel(u_ref, halo_ref, dt_ref, tok_ref, segc_ref, segr_ref, wk_ref, bias_ref, head_ref, skip_ref,
               save_ref, dy_ref, spot_ref,
               du_ref, ddt_ref, wgrad_ref, hgrad_ref, sgrad_ref,
               dstate, useen, act, slope, dpre, keep_y, keep_x, prod_a, prod_b, rows_a, held):
    step_no = pl.program_id(0)
    width = u_ref.shape[1]
    xw = width - 256
    pairs = xw // 128

    @pl.when(step_no == 0)
    def _():
        dstate[...] = jnp.zeros_like(dstate)
        dpre[Q : Q + 8, :] = jnp.zeros((8, width), f32)
        wgrad_ref[...] = jnp.zeros_like(wgrad_ref)
        hgrad_ref[...] = jnp.zeros_like(hgrad_ref)
        sgrad_ref[...] = jnp.zeros_like(sgrad_ref)
        rows_a[...] = jnp.zeros_like(rows_a)

    useen[0:8, :] = halo_ref[...].astype(f32)[8:16, :]
    useen[8 : 8 + Q, :] = u_ref[...].astype(f32)
    tok = tok_ref[...]
    flags = [None] + [spread_col(tok, j) for j in range(3)]
    carried = spread_col(tok, 3)
    samelast = spread_col(tok, 4)
    for p in range(width // 128):
        lanes = slice(128 * p, 128 * p + 128)
        pre, _ = conv_pre(useen, flags, wk_ref, bias_ref, lanes)
        sg = sigmoid(pre)
        act[:, lanes] = pre * sg
        slope[:, lanes] = sg * (1.0 + pre * (1.0 - sg))

    raw = dt_ref[...].astype(f32) + head_ref[0:1, :]
    step = softplus(raw)
    rate = head_ref[1:2, :]
    row = lax.broadcasted_iota(jnp.int32, (Q, Q), 0)
    col = lax.broadcasted_iota(jnp.int32, (Q, Q), 1)
    tri = jnp.where(row >= col, 1.0, 0.0).astype(bf16)
    upper = jnp.where(row <= col, 1.0, 0.0).astype(bf16)
    below = jnp.where(row > col, 1.0, 0.0).astype(bf16)
    decay = dot3(tri, step * rate)
    decay_t = decay.T
    madd = jnp.where((row <= col) & (segc_ref[...] == segr_ref[0]), 0.0, NEG)
    b_now, c_now = act[:, xw : xw + 128], act[:, xw + 128 : xw + 256]
    b_low, c_low = b_now.astype(bf16), c_now.astype(bf16)
    c_t = c_now.T.astype(bf16)
    gram = dot_nt(b_low, c_low)
    left = lax.broadcasted_iota(jnp.int32, (Q, 128), 1) < 64
    lane = lax.broadcasted_iota(jnp.int32, (Q, 128), 1)
    dgram = jnp.zeros((Q, Q), f32)
    cols_b = jnp.zeros((Q, 128), f32)
    for p in range(pairs):
        lanes = slice(128 * p, 128 * p + 128)
        d0, d1 = spread_col(decay, 2 * p), spread_col(decay, 2 * p + 1)
        dp = jnp.where(left, d0, d1)
        sp = jnp.where(left, spread_col(step, 2 * p), spread_col(step, 2 * p + 1))
        xs = act[:, lanes]
        xp = xs * sp
        dy_low = dy_ref[:, lanes]
        dy = dy_low.astype(f32)
        stacked = jnp.concatenate(
            [jnp.where(left, dy, 0.0).astype(bf16), jnp.where(left, 0.0, dy).astype(bf16)], axis=0
        )
        pair = dot_nt(xp.astype(bf16), stacked)
        mts = []
        for k, dk in ((0, d0), (1, d1)):
            h = 2 * p + k
            e = jnp.exp(decay_t[h : h + 1, :] - dk + madd)
            f = e * pair[:, 128 * k : 128 * k + 128]
            dgram = dgram + f
            w = gram * f
            mts.append((gram * e).astype(bf16))
            rows_a[h : h + 1, :] = jnp.sum(w, axis=0, keepdims=True)
            cols_b = jnp.where(lane == h, jnp.sum(w, axis=1, keepdims=True), cols_b)
        within = dot(jnp.concatenate(mts, axis=1), stacked)
        grow = jnp.exp(dp) * carried
        dy_in = dy * grow
        dy_in_low = dy_in.astype(bf16)
        keep_y[:, lanes] = dy_in_low
        st = save_ref[0, :, lanes]
        prod_a[:, lanes] = (dy_in * dot(c_low, st)).astype(bf16)
        last = dp[Q - 1 : Q, :]
        fade = jnp.exp(last - dp) * samelast
        ds = dstate[:, lanes]
        ds_low = ds.astype(bf16)
        xe = xp * fade
        keep_x[:, lanes] = xe.astype(bf16)
        later = dot(b_low, ds_low)
        prod_b[:, lanes] = (xe * later).astype(bf16)
        retain = jnp.exp(last) * carried[Q - 1 : Q, :]
        held[0:1, lanes] = jnp.sum(ds * st.astype(f32), axis=0, keepdims=True) * retain
        dxs = sp * (within + later * fade) + skip_ref[:, lanes] * dy
        skp = xs * dy
        sgrad_ref[:, lanes] += jnp.sum(skp.reshape(Q // 8, 8, 128), axis=0)
        dpre[0:Q, lanes] = dxs * slope[:, lanes]
        dstate[:, lanes] = ds * retain + dot(c_t, dy_in_low)
        if p == 0:
            db_in, dc_in = dot_nt(keep_x[:, lanes], ds_low), dot_nt(dy_in_low, st)
        else:
            db_in, dc_in = db_in + dot_nt(keep_x[:, lanes], ds_low), dc_in + dot_nt(dy_in_low, st)

    dg_low = dgram.astype(bf16)
    db = dot(dg_low, c_low) + db_in
    dc = dot(dgram.T.astype(bf16), b_low) + dc_in
    dpre[0:Q, xw : xw + 128] = db * slope[:, xw : xw + 128]
    dpre[0:Q, xw + 128 : xw + 256] = dc * slope[:, xw + 128 : xw + 256]

    spot = spot_ref[...]
    a_in = dot(prod_a[...], spot)
    b_in = dot(prod_b[...], spot)
    hv = jnp.broadcast_to(held[0:1, :], (8, xw))
    h_hi = hv.astype(bf16)
    h_lo = (hv - h_hi.astype(f32)).astype(bf16)
    through = (dot(h_hi, spot) + dot(h_lo, spot))[0:1, :]
    a_own = rows_a[...].T
    cross = dot3(upper, a_own - cols_b + a_in) + dot3(below, b_in) + through
    total = cols_b + b_in
    sg = sigmoid(raw)
    ratio = jnp.where(step > 1e-30, sg / jnp.maximum(step, 1e-30), 1.0)
    draw = total * ratio + rate * cross * sg
    ddt_ref[...] = draw.astype(bf16)
    hgrad_ref[0:8, :] += jnp.sum(draw.reshape(Q // 8, 8, 128), axis=0)
    hgrad_ref[8:16, :] += jnp.sum((step * cross).reshape(Q // 8, 8, 128), axis=0)

    for p in range(width // 128):
        lanes = slice(128 * p, 128 * p + 128)
        own = dpre[0:Q, lanes]
        du = wk_ref[3:4, lanes] * own
        wgrad_ref[24:32, lanes] += jnp.sum((own * useen[8 : 8 + Q, lanes]).reshape(Q // 8, 8, 128), axis=0)
        wgrad_ref[32:40, lanes] += jnp.sum(own.reshape(Q // 8, 8, 128), axis=0)
        for j in (1, 2, 3):
            du = du + wk_ref[3 - j : 4 - j, lanes] * (dpre[j : j + Q, lanes] * spread_col(tok, 4 + j))
            moved = own * (useen[8 - j : 8 - j + Q, lanes] * flags[j])
            k = 3 - j
            wgrad_ref[8 * k : 8 * k + 8, lanes] += jnp.sum(moved.reshape(Q // 8, 8, 128), axis=0)
        du_ref[:, lanes] = du.astype(bf16)
    first = dpre[0:8, :]
    dpre[Q : Q + 8, :] = first


def mixer_bwd(u, dt, tok, segc, segr, wk, bias, head, skip, save, dy, spot):
    length, width = u.shape
    xw = width - 256
    n = length // Q
    whole = lambda shape: pl.BlockSpec(shape, lambda i: (0,) * len(shape))
    back = lambda i: (n - 1 - i, 0)
    return pl.pallas_call(
        bwd_kernel,
        grid=(n,),
        in_specs=[
            pl.BlockSpec((Q, width), back),
            pl.BlockSpec((16, width), lambda i: (jnp.maximum((n - 1 - i) * (Q // 16) - 1, 0), 0)),
            pl.BlockSpec((Q, 128), back),
            pl.BlockSpec((Q, 8), back),
            pl.BlockSpec((Q, 1), back),
            pl.BlockSpec((1, 1, Q), lambda i: (n - 1 - i, 0, 0)),
            whole((4, width)),
            whole((1, width)),
            whole((2, 128)),
            whole((1, xw)),
            pl.BlockSpec((1, 128, xw), lambda i: (n - 1 - i, 0, 0)),
            pl.BlockSpec((Q, xw), back),
            whole((xw, 128)),
        ],
        out_specs=[
            pl.BlockSpec((Q, width), back),
            pl.BlockSpec((Q, 128), back),
            whole((40, width)),
            whole((16, 128)),
            whole((8, xw)),
        ],
        out_shape=[
            jax.ShapeDtypeStruct((length, width), bf16),
            jax.ShapeDtypeStruct((length, 128), bf16),
            jax.ShapeDtypeStruct((40, width), f32),
            jax.ShapeDtypeStruct((16, 128), f32),
            jax.ShapeDtypeStruct((8, xw), f32),
        ],
        scratch_shapes=[
            pltpu.VMEM((128, xw), f32),
            pltpu.VMEM((Q + 8, width), f32),
            pltpu.VMEM((Q, width), f32),
            pltpu.VMEM((Q, width), f32),
            pltpu.VMEM((Q + 8, width), f32),
            pltpu.VMEM((Q, xw), bf16),
            pltpu.VMEM((Q, xw), bf16),
            pltpu.VMEM((Q, xw), bf16),
            pltpu.VMEM((Q, xw), bf16),
            pltpu.VMEM((128, 128), f32),
            pltpu.VMEM((8, xw), f32),
        ],
        compiler_params=pltpu.CompilerParams(vmem_limit_bytes=48 * 2**20),
        name="mixer_backward",
    )(u, u, dt, tok, segc, segr, wk, bias, head, skip, save, dy, spot)


def token_facts(seg):
    length = seg.shape[0]
    facts = []
    for j in (1, 2, 3):
        before = jnp.concatenate([jnp.full((j,), -1, jnp.int32), seg[:-j]])
        facts.append(before == seg)
    by = seg.reshape(length // Q, Q)
    ends = by[:, Q - 1]
    prior = jnp.concatenate([jnp.full((1,), -1, jnp.int32), ends[:-1]])
    facts.append((by == prior[:, None]).reshape(length))
    facts.append((by == ends[:, None]).reshape(length))
    for j in (1, 2, 3):
        after = jnp.concatenate([seg[j:], jnp.full((j,), -1, jnp.int32)])
        facts.append(after == seg)
    return jnp.stack(facts, axis=1).astype(f32)


def over_rows(left, right):
    return lax.dot_general(
        left, right, (((0,), (0,)), ((), ())), preferred_element_type=jnp.float32
    )


def own_columns(weight, group, groups):
    heads = H // groups
    wide = heads * P_SIZE
    dt = lax.dynamic_slice_in_dim(weight, 2 * E + 2 * N + group * heads, heads, 1)
    return jnp.concatenate(
        [
            lax.dynamic_slice_in_dim(weight, group * wide, wide, 1),
            lax.dynamic_slice_in_dim(weight, E + group * wide, wide, 1),
            weight[:, 2 * E : 2 * E + 2 * N],
            jnp.pad(dt, ((0, 0), (0, 128 - heads))),
        ],
        axis=1,
    )


def shards(
    hidden,
    segments,
    norm_gain,
    in_weight,
    conv_weight,
    conv_bias,
    step_bias,
    decay_log,
    skip_scale,
    gate_gain,
    out_weight,
    cotangent,
):
    group = lax.axis_index("seq")
    groups = lax.axis_size("seq")
    heads = H // groups
    wide = heads * P_SIZE
    piece = hidden.shape[1]
    length = segments.shape[1]
    hidden_own, cot_own = hidden[0], cotangent[0]
    hidden_all = lax.all_gather(hidden_own, "seq", axis=0, tiled=True)
    in_gain = norm_gain.astype(f32)[:, None]
    in_scaled = (in_weight.astype(f32) * in_gain).astype(bf16)
    in_own = lax.all_gather(own_columns(in_scaled, group, groups), "wshard", axis=0, tiled=True)
    out_gain = gate_gain.astype(f32)[:, None]
    out_scaled = (out_weight.astype(f32) * out_gain).astype(bf16)
    out_cols = lax.all_to_all(out_scaled, "wshard", split_axis=1, concat_axis=0, tiled=True)
    out_own = lax.all_gather(
        lax.dynamic_slice_in_dim(out_cols, group * wide, wide, 0), "wshard", axis=1, tiled=True
    )
    cot_all = lax.all_gather(cot_own, "seq", axis=0, tiled=True)

    hidden_wide = hidden_all.astype(f32)
    scale = lax.rsqrt(jnp.mean(hidden_wide * hidden_wide, axis=-1, keepdims=True) + eps)
    gate = jnp.dot(hidden_all, in_own[:, :wide], preferred_element_type=f32) * scale
    u = (
        jnp.dot(hidden_all, in_own[:, wide : 2 * wide + 2 * N], preferred_element_type=f32) * scale
    ).astype(bf16)
    dt = (
        jnp.dot(hidden_all, in_own[:, 2 * wide + 2 * N :], preferred_element_type=f32) * scale
    ).astype(bf16)

    seg = segments[0]
    tok = token_facts(seg)
    segc, segr = seg[:, None], seg.reshape(length // Q, 1, Q)
    own_chan = lambda v: jnp.concatenate(
        [lax.dynamic_slice_in_dim(v, group * wide, wide, v.ndim - 1), v[..., E:]], axis=-1
    )
    own_head = lambda v: lax.dynamic_slice_in_dim(v, group * heads, heads, 0)
    taps, bias = own_chan(conv_weight), own_chan(conv_bias)[None]
    rate = -jnp.exp(own_head(decay_log))
    head = jnp.pad(jnp.stack([own_head(step_bias), rate]), ((0, 0), (0, 128 - heads)))
    skip = jnp.repeat(own_head(skip_scale), P_SIZE)[None]
    spot = (jnp.arange(wide)[:, None] // P_SIZE == jnp.arange(128)[None]).astype(bf16)
    mixed, save = mixer_fwd(u, dt, tok, segc, segr, taps, bias, head, skip)

    mixed_wide = mixed.astype(f32)
    sg = jax.nn.sigmoid(gate)
    silu = gate * sg
    g = mixed_wide * silu
    g_low = g.astype(bf16)
    a = lax.dot_general(cot_all, out_own, (((1,), (1,)), ((), ())), preferred_element_type=f32)
    sums = lax.psum(jnp.stack([jnp.sum(g * g, axis=1), jnp.sum(a * g, axis=1)]), "seq")
    r = lax.rsqrt(sums[0] / E + eps)[:, None]
    pull = (r * r * r) * (sums[1] / E)[:, None]
    d_g = r * a - g * pull
    gate_gain_part = jnp.sum(a * (g * r), axis=0)
    d_mixed = (d_g * silu).astype(bf16)
    d_gate = (d_g * mixed_wide * (sg * (1.0 + gate * (1.0 - sg))) * scale).astype(bf16)
    partial = (jnp.dot(g_low, out_own, preferred_element_type=f32) * r).astype(bf16)
    out_sum = lax.psum_scatter(partial, "seq", scatter_dimension=0, tiled=True)
    layer_output = hidden_own.astype(f32) + out_sum.astype(f32)
    cot_r = (cot_all.astype(f32) * r).astype(bf16)
    out_part = over_rows(g_low, cot_r).astype(bf16)
    out_part = lax.psum_scatter(out_part, "wshard", scatter_dimension=1, tiled=True)
    out_part = lax.all_gather(out_part, "seq", axis=0, tiled=True)
    out_part = lax.all_to_all(out_part, "wshard", split_axis=0, concat_axis=1, tiled=True)
    out_weight_grad = out_part.astype(f32) * out_gain

    du, ddt, taps_sum, head_sum, skip_sum = mixer_bwd(
        u, dt, tok, segc, segr, taps, bias, head, skip, save, d_mixed, spot
    )
    du = (du.astype(f32) * scale).astype(bf16)
    ddt = (ddt.astype(f32) * scale).astype(bf16)
    d_proj = jnp.concatenate([d_gate, du, ddt], axis=1)
    in_part = over_rows(hidden_all, d_proj).astype(bf16)
    b_part = lax.dot_general(
        d_proj, in_own, (((1,), (1,)), ((), ())), preferred_element_type=f32
    ).astype(bf16)
    b_sum = lax.psum_scatter(b_part, "seq", scatter_dimension=0, tiled=True).astype(f32)
    own_wide = hidden_own.astype(f32)
    own_scale = lax.rsqrt(jnp.mean(own_wide * own_wide, axis=-1, keepdims=True) + eps)
    hidden_grad = (
        cot_own.astype(f32)
        + b_sum
        - own_wide * (own_scale * own_scale) * jnp.mean(b_sum * own_wide, axis=-1, keepdims=True)
    )
    norm_part = jnp.sum(b_sum * own_wide, axis=0)

    in_part = lax.psum_scatter(in_part, "wshard", scatter_dimension=0, tiled=True)
    in_all = lax.all_gather(in_part, "seq", axis=0, tiled=False).astype(f32)
    side = lambda lo, hi: jnp.concatenate([in_all[i, :, lo:hi] for i in range(groups)], axis=1)
    in_weight_grad = (
        jnp.concatenate(
            [
                side(0, wide),
                side(wide, 2 * wide),
                jnp.sum(in_all[:, :, 2 * wide : 2 * wide + 2 * N], axis=0),
                side(2 * wide + 2 * N, 2 * wide + 2 * N + heads),
            ],
            axis=1,
        )
        * in_gain
    )

    taps_sum = jnp.sum(taps_sum.reshape(5, 8, -1), axis=1)
    head_sum = jnp.sum(head_sum.reshape(2, 8, -1), axis=1)[:, :heads]
    head_sum = head_sum * jnp.stack([jnp.ones_like(rate), rate])
    skip_sum = jnp.sum(skip_sum, axis=0).reshape(heads, P_SIZE).sum(axis=1)
    place = lambda v, size, at: lax.dynamic_update_slice_in_dim(
        jnp.zeros(v.shape[:-1] + (size,), f32), v, at, v.ndim - 1
    )
    chan_sums = jnp.concatenate([place(taps_sum[:, :wide], E, group * wide), taps_sum[:, wide:]], axis=1)
    flat = jnp.concatenate(
        [
            chan_sums.reshape(-1),
            place(jnp.concatenate([head_sum, skip_sum[None]]), H, group * heads).reshape(-1),
            place(gate_gain_part, E, group * wide),
            norm_part,
        ]
    )
    flat = lax.psum(flat, ("wshard", "seq"))
    channels = E + 2 * N
    chan_sums = flat[: 5 * channels].reshape(5, channels)
    at = 5 * channels
    head_sums = flat[at : at + 3 * H].reshape(3, H)
    at = at + 3 * H
    shard = lax.axis_index("wshard")
    gate_rows, norm_rows = out_weight.shape[0], in_weight.shape[0]
    gate_gain_grad = lax.dynamic_slice_in_dim(flat[at : at + E], shard * gate_rows, gate_rows, 0) / gate_gain.astype(f32)
    norm_gain_grad = lax.dynamic_slice_in_dim(flat[at + E :], shard * norm_rows, norm_rows, 0) / norm_gain.astype(f32)
    return (
        layer_output[None],
        hidden_grad[None],
        norm_gain_grad,
        in_weight_grad,
        chan_sums[:4],
        chan_sums[4],
        head_sums[0],
        head_sums[1],
        head_sums[2],
        gate_gain_grad,
        out_weight_grad,
    )


def solution(mesh):
    in_specs = (
        P("wshard", "seq", None),
        P("wshard", None),
        P("wshard"),
        P("wshard", None),
        P(),
        P(),
        P(),
        P(),
        P(),
        P("wshard"),
        P("wshard", None),
        P("wshard", "seq", None),
    )
    out_specs = (
        P("wshard", "seq", None),
        P("wshard", "seq", None),
        P("wshard"),
        P("wshard", None),
        P(),
        P(),
        P(),
        P(),
        P(),
        P("wshard"),
        P("wshard", None),
    )
    return jax.shard_map(shards, mesh=mesh, in_specs=in_specs, out_specs=out_specs, check_vma=False)
```

time: 3010 us -> 842 us (0.28)
  local copies, waits for them, and re-layouts: 850 us -> 35.7 us
  waiting for transfers between devices: 1270 us -> 547 us
  other arithmetic: 352 us -> 48.1 us
  matrix products: 335 us -> 96.2 us
  blocking collectives: 114 us -> 10.5 us
  Pallas kernels: 0 us -> 66.4 us
    reduce_scatter x3 -> x4, waiting for transfers between devices: 741 us -> 185 us  [the longest x1 114 us: shards(): lax.psum_scatter(in_part, 'wshard', scatter_dimension=0, tiled=True)]
    dynamic_update_slice x48 -> x3, local copies, waits for them, and re-layouts: 322 us -> 0.46 us  [shards(): lax.dynamic_update_slice_in_dim(jnp.zeros(v.shape[:-1] + (size,), f32), v...]
    dot_general x100 -> x6, matrix products: 282 us -> 64.9 us  [the longest x1 18.3 us: shards(): lax.dot_general(d_proj, in_own, (((1,), (1,)), ((), ())), preferred_eleme...]
    convert_element_type x12 -> x0, local copies, waits for them, and re-layouts: 127 us -> none  [the longest x1 44.8 us: shards(): d_x_low = d_x_heads.astype(jnp.bfloat16)]
    all_gather x3 -> x6, waiting for transfers between devices: 337 us -> 212 us  [the longest x1 87.4 us: shards(): lax.all_gather(own_columns(in_scaled, group, groups), 'wshard', axis=0, t...]
    unnamed x10 -> x0, other arithmetic: 117 us -> none
    unnamed x2 -> x0, blocking collectives: 82.5 us -> none
    unnamed x157 -> x43, local copies, waits for them, and re-layouts: 93.5 us -> 15.5 us
  transfers between devices with their start and end apart: 14 -> 13, of which waited for: 8 -> 11; matrix products, arithmetic and copies ran while one was open for 28% -> 15% of each run, Pallas kernels for 0% -> 6%
where the time goes in v1:
time: 842 us; the launch traced here: 831 us
  waiting for transfers between devices  547 us (65%)
  matrix products  96.2 us (11%)
  Pallas kernels  66.4 us (8%)
  other arithmetic  48.1 us (6%)
  local copies, waits for them, and re-layouts  35.7 us (4%)
  between operations  14.8 us (2%)
  starting transfers between devices  12.4 us (1%)
  blocking collectives  10.5 us (1%)
    psum x1, waiting for transfers between devices, shards(): flat = lax.psum(flat, ('wshard', 'seq'))  120 us
    reduce_scatter x1, waiting for transfers between devices, shards(): lax.psum_scatter(in_part, 'wshard', scatter_dimension=0, tiled=True)  114 us
    all_gather x1, waiting for transfers between devices, shards(): lax.all_gather(own_columns(in_scaled, group, groups), 'wshard', axis=0, t...  87.4 us
    reduce_scatter x1, waiting for transfers between devices, shards(): out_sum = lax.psum_scatter(partial, 'seq', scatter_dimension=0, tiled=True)  55 us
    all_gather x1, waiting for transfers between devices, shards(): lax.all_gather(lax.dynamic_slice_in_dim(out_cols, group * wide, wide, 0),...  50.8 us
    all_gather x1, waiting for transfers between devices, shards(): cot_all = lax.all_gather(cot_own, 'seq', axis=0, tiled=True)  46.5 us
    pallas_call x1, Pallas kernels, mixer_bwd(): pl.pallas_call(bwd_kernel, grid=(n,), in_specs=[pl.BlockSpec((Q, width),...  45.7 us
    dot_general x2, matrix products, over_rows(): lax.dot_general(left, right, (((0,), (0,)), ((), ())), preferred_element_...  31.2 us
  transfers between devices with their start and end apart: 13, of which 11 were waited for; matrix products, arithmetic and copies ran while one was open for 15% of the time, Pallas kernels for 6%

profile of v1, /device:TPU:0, one launch (start us, length us, event | category | flops | bytes accessed | tf_op | source)
XLA Modules:
  0.0 831.2 jit_solution(770625255697684732)
XLA Ops:
  11.6 7.3 all-to-all-start
  18.9 28.5 %all-to-all-done = bf16[384,8,192]{0,2,1:T(8,128)(2,1)S(1)} async-done(((bf16[384,8,192]{0,2,1:T(8,128)(2,1)}), bf16[384,8,192]{0,2,1:T(8,128)(2,1)S(1)}, u32[]{:S(2)}, u32[]{:S(2)}) %all-to-all-start) | async-done | bytes 1179680 | tf_op jit(solution)/shard_map/all_to_all | solution.py:420
  62.8 50.8 %all-gather.12.cloned.1.call-done = bf16[768,1536]{0,1:T(8,128)(2,1)} async-done(((bf16[768,192]{0,1:T(8,128)(2,1)}), bf16[768,1536]{0,1:T(8,128)(2,1)}) %all-gather.12.cloned.1.call-update) | async-done | bytes 2359312 | tf_op jit(solution)/shard_map/all_gather | solution.py:421
  113.6 46.5 %all-gather.18.cloned.1.call-done = bf16[1,2048,1536]{2,1,0:T(8,128)(2,1)} async-done(((bf16[1,512,1536]{2,1,0:T(8,128)(2,1)}), bf16[1,2048,1536]{2,1,0:T(8,128)(2,1)}) %all-gather.18.cloned.1.call-update) | async-done | bytes 6291472 | tf_op jit(solution)/shard_map/all_gather | solution.py:424
  160.1 9.5 %fusion.9 = f32[768,2048]{0,1:T(8,128)} fusion(bf16[768,1536]{0,1:T(8,128)(2,1)} %all-gather.12.cloned.1.call-done, bf16[1,2048,1536]{2,1,0:T(8,128)(2,1)} %all-gather.18.cloned.1.call-done), kind=kOutput, calls=%fused_computation.22 | convolution fusion | flops 4831838208 | bytes 14942208 | tf_op jit(solution)/shard_map/dot_general | solution.py:455
  169.6 87.4 %all-gather.10.cloned.1.call-done = bf16[1536,1920]{1,0:T(8,128)(2,1)} async-done(((bf16[192,1920]{1,0:T(8,128)(2,1)}), bf16[1536,1920]{1,0:T(8,128)(2,1)}) %all-gather.10.cloned.1.call-update) | async-done | bytes 5898256 | tf_op jit(solution)/shard_map/all_gather | solution.py:417
  261.7 10.1 %fusion.24.u_ref.halo_ref = bf16[2048,1024]{1,0:T(8,128)(2,1)} fusion(f32[2048]{0:T(1024)S(1)} %add_rsqrt_fusion, bf16[1,2048,1536]{2,1,0:T(8,128)(2,1)S(1)} %copy-done.4, bf16[1536,1920]{1,0:T(8,128)(2,1)} %all-gather.10.cloned.1.call-done), kind=kOutput, calls=%fused_computation.47 | convolution fusion | flops 6446645248 | bytes 13639680 | tf_op jit(solution)/shard_map/dot_general | solution.py:430
  271.8 20.6 %mixer_forward.1 = (bf16[2048,768]{1,0:T(8,128)(2,1)S(1)}, bf16[16,128,768]{2,1,0:T(8,128)(2,1)}) custom-call(bf16[2048,1024]{1,0:T(8,128)(2,1)} %fusion.24.u_ref.halo_ref, bf16[2048,128]{1,0:T(8,128)(2,1)S(1)} %fusion.43.dt_ref, f32[2048,8]{1,0:T(8,128)S(1)} %convert_element_type.122.tok_ref, s32[2048,1]{1,0:T(8,128)S(1)} %copy.86.segc_ref, ...), custom_call_target="tpu_custom_call" | custom-call | tf_op jit(solution)/shard_map/mixer_forward/pallas_call | solution.py:128
  292.4 12.0 %multiply_reduce_fusion.1 = (f32[2048]{0:T(1024)S(1)}, f32[2048]{0:T(1024)S(1)}, f32[768,2048]{0,1:T(8,128)}) fusion(bf16[2048,768]{1,0:T(8,128)(2,1)S(1)} %get-tuple-element.18, f32[2048]{0:T(1024)S(1)} %add_rsqrt_fusion, f32[768,2048]{0,1:T(8,128)} %fusion.9, bf16[1536,1920]{1,0:T(8,128)(2,1)} %all-gather.10.cloned.1.call-done, ...), kind=kOutput, calls=%fused_computation.41 | convolution fusion | flops 4849135616 | bytes 24403968 | tf_op jit(solution)/shard_map/dot_general | solution.py:428
  304.4 10.5 %psum.14 = f32[2,2048]{1,0:T(2,128)S(1)} all-reduce(f32[2,2048]{1,0:T(2,128)S(1)} %pad_maximum_fusion.5), channel_id=1, replica_groups=mesh['wshard'=8,'seq'=4] {'seq'}, use_global_device_ids=true, to_apply=%region_3.4 | all-reduce | flops 4096 | bytes 32768 | tf_op jit(solution)/shard_map/psum | solution.py:456
  314.9 13.2 %fusion.27 = bf16[768,1536]{0,1:T(8,128)(2,1)} fusion(bf16[1,2048,1536]{2,1,0:T(8,128)(2,1)} %all-gather.18.cloned.1.call-done, f32[2048]{0:T(1024)S(1)} %bitcast.187, bf16[2048,768]{1,0:T(8,128)(2,1)} %copy-done, f32[768,2048]{0,1:T(8,128)} %get-tuple-element.101, f32[2048]{0:T(1024)S(1)} %add_rsqrt_fusion), kind=kOutput, calls=%fused_computation.49 | convolution fusion | flops 4855037952 | bytes 18104320 | tf_op jit(solution)/shard_map/dot_general | solution.py:373
  328.6 12.0 %fusion.3 = (bf16[2048,768]{1,0:T(8,128)(2,1)}, bf16[2048,768]{1,0:T(8,128)(2,1)}, f32[768]{0:T(1024)S(1)}) fusion(bf16[2048,768]{1,0:T(8,128)(2,1)} %copy-done, f32[768,2048]{0,1:T(8,128)} %get-tuple-element.101, f32[2048]{0:T(1024)S(1)} %add_rsqrt_fusion, f32[2048]{0:T(1024)S(1)} %fusion.52, f32[768,2048]{0,1:T(8,128)} %fusion.9, f32[2048]{0:T(1024)S(1)} %bitcast.189), kind=kLoop, calls=%fused_computation.13 | loop fusion | flops 36175104 | bytes 22047744 | tf_op jit(solution)/shard_map/convert_element_type | solution.py:462
  340.6 45.7 %mixer_backward.1 = (bf16[2048,1024]{1,0:T(8,128)(2,1)}, bf16[2048,128]{1,0:T(8,128)(2,1)S(1)}, f32[40,1024]{1,0:T(8,128)S(1)}, f32[16,128]{1,0:T(8,128)S(1)}, f32[8,768]{1,0:T(8,128)S(1)}) custom-call(bf16[2048,1024]{1,0:T(8,128)(2,1)} %fusion.24.u_ref.halo_ref, bf16[2048,1024]{1,0:T(8,128)(2,1)} %fusion.24.u_ref.halo_ref, ...), custom_call_target="tpu_custom_call" | custom-call | tf_op jit(solution)/shard_map/mixer_backward/pallas_call | solution.py:305
  395.7 18.3 %convolution_convert_fusion.1 = bf16[2048,1536]{1,0:T(8,128)(2,1)} fusion(bf16[1536,1920]{1,0:T(8,128)(2,1)} %all-gather.10.cloned.1.call-done, bf16[2048,128]{1,0:T(8,128)(2,1)} %multiply_convert_fusion.10, bf16[2048,1024]{1,0:T(8,128)(2,1)} %multiply_convert_fusion.2, bf16[2048,768]{1,0:T(8,128)(2,1)S(1)} %copy-done.6), kind=kOutput, calls=%fused_computation.9 | convolution fusion | flops 12106334208 | bytes 20054016 | tf_op jit(solution)/shard_map/dot_general | solution.py:480
  414.3 18.0 %fusion = bf16[1536,1920]{0,1:T(8,128)(2,1)} fusion(bf16[1,2048,1536]{2,1,0:T(8,128)(2,1)} %all-gather.16.cloned.1.call-done, bf16[2048,128]{1,0:T(8,128)(2,1)} %multiply_convert_fusion.10, bf16[2048,1024]{1,0:T(8,128)(2,1)} %multiply_convert_fusion.2, bf16[2048,768]{1,0:T(8,128)(2,1)S(1)} %copy-done.6), kind=kOutput, calls=%fused_computation.10 | convolution fusion | flops 12106137600 | bytes 20054016 | tf_op jit(solution)/shard_map/dot_general | solution.py:373
  432.3 8.7 %copy.99 = bf16[1536,1920]{1,0:T(8,128)(2,1)} copy(bf16[1536,1920]{0,1:T(8,128)(2,1)} %fusion) | data formatting | bytes 11796480
  442.8 10.4 %multiply_convert_fusion.1 = bf16[2048,1536]{1,0:T(8,128)(2,1)} fusion(bf16[768,1536]{0,1:T(8,128)(2,1)} %all-gather.12.cloned.1.call-done, f32[2048]{0:T(1024)S(1)} %bitcast.190, bf16[2048,768]{1,0:T(8,128)(2,1)S(1)} %copy-done.1, f32[768,2048]{0,1:T(8,128)} %get-tuple-element.101, f32[2048]{0:T(1024)S(1)} %add_rsqrt_fusion), kind=kOutput, calls=%fused_computation.1 | convolution fusion | flops 4850712576 | bytes 18104320 | tf_op jit(solution)/shard_map/dot_general | solution.py:463
  461.0 13.6 %reduce-scatter.9.cloned.1.call-done = bf16[512,1536]{1,0:T(8,128)(2,1)} async-done(((bf16[2048,1536]{1,0:T(8,128)(2,1)}), bf16[512,1536]{1,0:T(8,128)(2,1)}) %reduce-scatter.9.cloned.1.call-update) | async-done | bytes 1572880 | tf_op jit(solution)/shard_map/reduce_scatter | solution.py:483
  477.6 113.7 %reduce-scatter.13.cloned.1.call-done = bf16[192,1920]{1,0:T(8,128)(2,1)} async-done(((bf16[1536,1920]{1,0:T(8,128)(2,1)}), bf16[192,1920]{1,0:T(8,128)(2,1)}) %reduce-scatter.13.cloned.1.call-update) | async-done | bytes 737296 | tf_op jit(solution)/shard_map/reduce_scatter | solution.py:493
  597.2 55.0 %reduce-scatter.7.cloned.1.call-done = bf16[512,1536]{1,0:T(8,128)(2,1)} async-done(((bf16[2048,1536]{1,0:T(8,128)(2,1)}), bf16[512,1536]{1,0:T(8,128)(2,1)}) %reduce-scatter.7.cloned.1.call-update) | async-done | bytes 1572880 | tf_op jit(solution)/shard_map/reduce_scatter | solution.py:464
  652.2 5.5 fusion.29
  657.7 120.0 %all-reduce.9.cloned.1.call-done = f32[21392]{0:T(1024)} async-done(((f32[21392]{0:T(1024)}), f32[21392]{0:T(1024)}) %all-reduce.9.cloned.1.call-update) | async-done | bytes 85584 | tf_op jit(solution)/shard_map/psum | solution.py:525
  784.7 23.9 %all-gather.20.cloned.1.call-done = bf16[768,1920]{1,0:T(8,128)(2,1)} async-done(((bf16[192,1920]{1,0:T(8,128)(2,1)}), bf16[768,1920]{1,0:T(8,128)(2,1)}) %all-gather.20.cloned.1.call-update) | async-done | bytes 2949136 | tf_op jit(solution)/shard_map/all_gather | solution.py:494
  813.8 5.3 concatenate.79
  (156 shorter events, 70.0 us)
Async XLA Ops:
  7.2 51.5 %all-gather.16.cloned.1.call-start = ((), (), s32[]{:S(2)}) async-start(), calls=%async_computation.13 | async-start | bytes 7864320 | tf_op jit(solution)/shard_map/all_gather | solution.py:414
  8.6 38.8 %copy-start.7 = (f32[384]{0:T(512)}, f32[384]{0:T(512)S(1)}, u32[]{:S(2)}) copy-start(f32[384]{0:T(512)S(1)} %convert_element_type.126) | copy-start | bytes 4612
  8.6 40.6 %copy-start.16 = (bf16[192]{0:T(256)(128)(2,1)S(1)}, bf16[192]{0:T(256)(128)(2,1)}, u32[]{:S(2)}) copy-start(bf16[192]{0:T(256)(128)(2,1)} %param.14) | copy-start | bytes 1156
  11.6 35.8 %all-to-all-start = ((bf16[384,8,192]{0,2,1:T(8,128)(2,1)}), bf16[384,8,192]{0,2,1:T(8,128)(2,1)S(1)}, u32[]{:S(2)}, u32[]{:S(2)}) async-start(bf16[384,8,192]{0,2,1:T(8,128)(2,1)} %bitcast.22), calls=%async_computation | async-start | bytes 2359296 | tf_op jit(solution)/shard_map/all_to_all | solution.py:420
  18.8 94.7 %all-gather.12.cloned.1.call-start = ((), (), s32[]{:S(2)}) async-start(), calls=%async_computation.7 | async-start | bytes 2654208 | tf_op jit(solution)/shard_map/all_gather | solution.py:421
  48.4 111.7 %all-gather.18.cloned.1.call-start = ((), (), s32[]{:S(2)}) async-start(), calls=%async_computation.14 | async-start | bytes 7864320 | tf_op jit(solution)/shard_map/all_gather | solution.py:424
  49.2 207.8 %all-gather.10.cloned.1.call-start = ((), (), s32[]{:S(2)}) async-start(), calls=%async_computation.6 | async-start | bytes 6635520 | tf_op jit(solution)/shard_map/all_gather | solution.py:417
  49.3 6.2 copy-start.9
  49.3 6.3 slice-start
  52.9 342.7 %reduce-scatter.11.cloned.1.call-start = ((), (), s32[]{:S(2)}) async-start(), calls=%async_computation.11 | async-start | bytes 2654208 | tf_op jit(solution)/shard_map/reduce_scatter | solution.py:468
  292.4 12.0 %copy-start = (bf16[2048,768]{1,0:T(8,128)(2,1)}, bf16[2048,768]{1,0:T(8,128)(2,1)S(1)}, u32[]{:S(2)}) copy-start(bf16[2048,768]{1,0:T(8,128)(2,1)S(1)} %get-tuple-element.18) | copy-start | bytes 9437188
  328.2 126.1 %all-gather.14.cloned.1.call-start = ((), (), s32[]{:S(2)}) async-start(), calls=%async_computation.12 | async-start | bytes 1474560 | tf_op jit(solution)/shard_map/all_gather | solution.py:469
  386.3 9.3 %copy-start.6 = (bf16[2048,768]{1,0:T(8,128)(2,1)S(1)}, bf16[2048,768]{1,0:T(8,128)(2,1)}, u32[]{:S(2)}) copy-start(bf16[2048,768]{1,0:T(8,128)(2,1)} %get-tuple-element.63) | copy-start | bytes 9437188
  395.6 78.9 %reduce-scatter.9.cloned.1.call-start = ((), (), s32[]{:S(2)}) async-start(), calls=%async_computation.9 | async-start | bytes 7864320 | tf_op jit(solution)/shard_map/reduce_scatter | solution.py:483
  414.0 177.3 %reduce-scatter.13.cloned.1.call-start = ((), (), s32[]{:S(2)}) async-start(), calls=%async_computation.16 | async-start | bytes 6635520 | tf_op jit(solution)/shard_map/reduce_scatter | solution.py:493
  441.0 211.2 %reduce-scatter.7.cloned.1.call-start = ((), (), s32[]{:S(2)}) async-start(), calls=%async_computation.8 | async-start | bytes 7864320 | tf_op jit(solution)/shard_map/reduce_scatter | solution.py:464
  453.3 21.3 %copy-start.3 = (bf16[1,512,1536]{2,1,0:T(8,128)(2,1)S(1)}, bf16[1,512,1536]{2,1,0:T(8,128)(2,1)}, u32[]{:S(2)}) copy-start(bf16[1,512,1536]{2,1,0:T(8,128)(2,1)} %param.12) | copy-start | bytes 4718596
  453.3 138.0 %copy-start.8 = (f32[384]{0:T(512)S(1)}, f32[384]{0:T(512)}, u32[]{:S(2)}) copy-start(f32[384]{0:T(512)} %copy-done.7) | copy-start | bytes 4612
  456.7 134.6 %all-to-all-start.1 = ((bf16[8,384,192]{1,2,0:T(8,128)(2,1)}), bf16[8,384,192]{1,2,0:T(8,128)(2,1)}, u32[]{:S(2)}, u32[]{:S(2)}) async-start(bf16[8,384,192]{1,2,0:T(8,128)(2,1)} %bitcast.174), calls=%async_computation.4 | async-start | bytes 2359296 | tf_op jit(solution)/shard_map/all_to_all | solution.py:470
  460.9 191.3 %copy-start.5 = (bf16[1,512,1536]{2,1,0:T(8,128)(2,1)S(1)}, bf16[1,512,1536]{2,1,0:T(8,128)(2,1)}, u32[]{:S(2)}) copy-start(bf16[1,512,1536]{2,1,0:T(8,128)(2,1)} %param.23) | copy-start | bytes 4718596
  460.9 316.7 %all-reduce.9.cloned.1.call-start = ((), (), s32[]{:S(2)}) async-start(), calls=%async_computation.10 | async-start | bytes 172032 | tf_op jit(solution)/shard_map/psum | solution.py:525
  477.5 331.1 %all-gather.20.cloned.1.call-start = ((), (), s32[]{:S(2)}) async-start(), calls=%async_computation.15 | async-start | bytes 3686400 | tf_op jit(solution)/shard_map/all_gather | solution.py:494
  597.2 184.8 %copy-start.17 = (bf16[192]{0:T(256)(128)(2,1)S(1)}, bf16[192]{0:T(256)(128)(2,1)}, u32[]{:S(2)}) copy-start(bf16[192]{0:T(256)(128)(2,1)} %param.14) | copy-start | bytes 1156
  597.2 185.5 %copy-start.11 = (bf16[384]{0:T(512)(128)(2,1)S(1)}, bf16[384]{0:T(512)(128)(2,1)}, u32[]{:S(2)}) copy-start(bf16[384]{0:T(512)(128)(2,1)} %param.21) | copy-start | bytes 2308
  (10 other events, 51.6 us)
Sparse Core Ops, SparseCore 0:
  9.6 49.0 all-gather.15
  61.4 52.0 all-gather.11
  115.1 44.9 all-gather.17
  162.7 94.2 all-gather.9
  328.3 67.2 reduce-scatter.10
  397.0 16.5 all-gather.13
  416.2 58.3 reduce-scatter.8
  478.7 112.5 reduce-scatter.12
  594.0 58.1 reduce-scatter.6
  658.2 119.4 all-reduce.8
  779.2 29.3 all-gather.19

commit v2 on v1

--- a/solution.py
+++ b/solution.py
@@ -1,3 +1,5 @@
+import functools
+
 import jax
 import jax.numpy as jnp
 from jax import lax
@@ -62,19 +64,61 @@
     return pre, shifted
 
 
-def fwd_kernel(u_ref, dt_ref, tok_ref, segc_ref, segr_ref, wk_ref, bias_ref, head_ref, skip_ref,
-               mixed_ref, save_ref, state, useen, act):
+class NoTraffic:
+    inputs, outputs, scratch, collective_id = (), (), (), None
+
+    def __init__(self, *refs):
+        pass
+
+    def step(self, i, last):
+        pass
+
+
+def fwd_kernel(traffic, hid_ref, main_ref, bc_ref, wdt_ref, tok_ref, segc_ref, segr_ref, wk_ref, bias_ref, head_ref, skip_ref, *rest):
+    n_in, n_out = len(traffic.inputs), len(traffic.outputs)
+    extra_in, rest = rest[:n_in], rest[n_in:]
+    u_ref, dt_ref, gate_ref, scale_ref, mixed_ref, save_ref = rest[:6]
+    extra_out, rest = rest[6 : 6 + n_out], rest[6 + n_out :]
+    state, useen, act, next_u, next_dt = rest[:5]
     step_no = pl.program_id(0)
-    width = u_ref.shape[1]
+    traffic(*extra_in, *extra_out, *rest[5:]).step(step_no, pl.num_programs(0) - 1)
+    width = wk_ref.shape[1]
     xw = width - 256
     pairs = xw // 128
 
     @pl.when(step_no == 0)
+    def _():
+        next_u[...] = jnp.zeros_like(next_u)
+        next_dt[...] = jnp.zeros_like(next_dt)
+
+    @pl.when(step_no <= 1)
     def _():
         state[...] = jnp.zeros_like(state)
         useen[0:8, :] = jnp.zeros((8, width), f32)
 
-    useen[8 : 8 + Q, :] = u_ref[...].astype(f32)
+    useen[8 : 8 + Q, :] = next_u[...]
+    dt_now = next_dt[...]
+
+    low = hid_ref[...]
+    total = jnp.zeros((Q, 128), f32)
+    for k in range(low.shape[1] // 128):
+        part = low[:, 128 * k : 128 * k + 128].astype(f32)
+        total = total + part * part
+    scale = lax.rsqrt(jnp.sum(total, axis=1, keepdims=True) / low.shape[1] + eps)
+    scale_ref[...] = scale
+    for k in range(xw // 256):
+        gate_ref[:, 256 * k : 256 * k + 256] = dot(low, main_ref[:, 256 * k : 256 * k + 256]) * scale
+    for k in range(xw // 256):
+        got = (dot(low, main_ref[:, xw + 256 * k : xw + 256 * k + 256]) * scale).astype(bf16)
+        u_ref[:, 256 * k : 256 * k + 256] = got
+        next_u[:, 256 * k : 256 * k + 256] = got.astype(f32)
+    got = (dot(low, bc_ref[...]) * scale).astype(bf16)
+    u_ref[:, xw : xw + 256] = got
+    next_u[:, xw : xw + 256] = got.astype(f32)
+    got = (dot(low, wdt_ref[...]) * scale).astype(bf16)
+    dt_ref[...] = got
+    next_dt[...] = got.astype(f32)
+
     flags = [None] + [spread_col(tok_ref[...], j) for j in range(3)]
     carried = spread_col(tok_ref[...], 3)
     samelast = spread_col(tok_ref[...], 4)
@@ -85,7 +129,7 @@
     tail = useen[Q : Q + 8, :]
     useen[0:8, :] = tail
 
-    step = softplus(dt_ref[...].astype(f32) + head_ref[0:1, :])
+    step = softplus(dt_now + head_ref[0:1, :])
     row = lax.broadcasted_iota(jnp.int32, (Q, Q), 0)
     col = lax.broadcasted_iota(jnp.int32, (Q, Q), 1)
     tri = jnp.where(row >= col, 1.0, 0.0).astype(bf16)
@@ -120,48 +164,76 @@
         state[:, lanes] = st * (jnp.exp(last) * carried[Q - 1 : Q, :]) + dot(b_t, to_end)
 
 
-def mixer_fwd(u, dt, tok, segc, segr, wk, bias, head, skip):
-    length, width = u.shape
+def mixer_fwd(traffic, extra, hid, main, bc, wdt, tok, segc, segr, wk, bias, head, skip):
+    length, depth = hid.shape
+    width = wk.shape[1]
     xw = width - 256
     n = length // Q
-    whole = lambda shape: pl.BlockSpec(shape, lambda i: (0,) * len(shape))
+    whole = lambda shape: pl.BlockSpec(shape, lambda i: (0,) * len(shape), pipeline_mode=pl.Buffered(1))
+    ahead = lambda i: (jnp.minimum(i, n - 1), 0)
+    now = lambda i: (jnp.maximum(i - 1, 0), 0)
+    now3 = lambda i: (jnp.maximum(i - 1, 0), 0, 0)
     return pl.pallas_call(
-        fwd_kernel,
-        grid=(n,),
+        functools.partial(fwd_kernel, traffic),
+        grid=(n + 1,),
         in_specs=[
-            pl.BlockSpec((Q, width), lambda i: (i, 0)),
-            pl.BlockSpec((Q, 128), lambda i: (i, 0)),
-            pl.BlockSpec((Q, 8), lambda i: (i, 0)),
-            pl.BlockSpec((Q, 1), lambda i: (i, 0)),
-            pl.BlockSpec((1, 1, Q), lambda i: (i, 0, 0)),
+            pl.BlockSpec((Q, depth), ahead),
+            whole(main.shape),
+            whole(bc.shape),
+            whole(wdt.shape),
+            pl.BlockSpec((Q, 8), now),
+            pl.BlockSpec((Q, 1), now),
+            pl.BlockSpec((1, 1, Q), now3),
             whole((4, width)),
             whole((1, width)),
             whole((2, 128)),
             whole((1, xw)),
-        ],
+        ]
+        + [pl.BlockSpec(memory_space=pl.ANY)] * len(extra),
         out_specs=[
-            pl.BlockSpec((Q, xw), lambda i: (i, 0)),
-            pl.BlockSpec((1, 128, xw), lambda i: (i, 0, 0)),
-        ],
+            pl.BlockSpec((Q, width), ahead),
+            pl.BlockSpec((Q, 128), ahead),
+            pl.BlockSpec((Q, xw), ahead),
+            pl.BlockSpec((Q, 1), ahead),
+            pl.BlockSpec((Q, xw), now),
+            pl.BlockSpec((1, 128, xw), now3),
+        ]
+        + [pl.BlockSpec(memory_space=pl.ANY)] * len(traffic.outputs),
         out_shape=[
+            jax.ShapeDtypeStruct((length, width), bf16),
+            jax.ShapeDtypeStruct((length, 128), bf16),
+            jax.ShapeDtypeStruct((length, xw), f32),
+            jax.ShapeDtypeStruct((length, 1), f32),
             jax.ShapeDtypeStruct((length, xw), bf16),
             jax.ShapeDtypeStruct((n, 128, xw), bf16),
+            *traffic.outputs,
         ],
         scratch_shapes=[
             pltpu.VMEM((128, xw), f32),
             pltpu.VMEM((Q + 8, width), f32),
             pltpu.VMEM((Q, width), f32),
+            pltpu.VMEM((Q, width), f32),
+            pltpu.VMEM((Q, 128), f32),
+            *traffic.scratch,
         ],
-        compiler_params=pltpu.CompilerParams(vmem_limit_bytes=48 * 2**20),
+        compiler_params=pltpu.CompilerParams(
+            vmem_limit_bytes=48 * 2**20,
+            collective_id=traffic.collective_id,
+            has_side_effects=traffic.collective_id is not None,
+        ),
         name="mixer_forward",
-    )(u, dt, tok, segc, segr, wk, bias, head, skip)
-
-
-def bwd_kernel(u_ref, halo_ref, dt_ref, tok_ref, segc_ref, segr_ref, wk_ref, bias_ref, head_ref, skip_ref,
-               save_ref, dy_ref, spot_ref,
-               du_ref, ddt_ref, wgrad_ref, hgrad_ref, sgrad_ref,
-               dstate, useen, act, slope, dpre, keep_y, keep_x, prod_a, prod_b, rows_a, held):
+    )(hid, main, bc, wdt, tok, segc, segr, wk, bias, head, skip, *extra)
+
+
+def bwd_kernel(traffic, u_ref, halo_ref, dt_ref, tok_ref, segc_ref, segr_ref, wk_ref, bias_ref, head_ref, skip_ref,
+               save_ref, dy_ref, spot_ref, *rest):
+    n_in, n_out = len(traffic.inputs), len(traffic.outputs)
+    extra_in, rest = rest[:n_in], rest[n_in:]
+    du_ref, ddt_ref, wgrad_ref, hgrad_ref, sgrad_ref = rest[:5]
+    extra_out, rest = rest[5 : 5 + n_out], rest[5 + n_out :]
+    dstate, useen, act, slope, dpre, keep_y, keep_x, prod_a, prod_b, rows_a, held = rest[:11]
     step_no = pl.program_id(0)
+    traffic(*extra_in, *extra_out, *rest[11:]).step(step_no, pl.num_programs(0) - 1)
     width = u_ref.shape[1]
     xw = width - 256
     pairs = xw // 128
@@ -296,14 +368,14 @@
     dpre[Q : Q + 8, :] = first
 
 
-def mixer_bwd(u, dt, tok, segc, segr, wk, bias, head, skip, save, dy, spot):
+def mixer_bwd(traffic, extra, u, dt, tok, segc, segr, wk, bias, head, skip, save, dy, spot):
     length, width = u.shape
     xw = width - 256
     n = length // Q
     whole = lambda shape: pl.BlockSpec(shape, lambda i: (0,) * len(shape))
     back = lambda i: (n - 1 - i, 0)
     return pl.pallas_call(
-        bwd_kernel,
+        functools.partial(bwd_kernel, traffic),
         grid=(n,),
         in_specs=[
             pl.BlockSpec((Q, width), back),
@@ -319,20 +391,23 @@
             pl.BlockSpec((1, 128, xw), lambda i: (n - 1 - i, 0, 0)),
             pl.BlockSpec((Q, xw), back),
             whole((xw, 128)),
-        ],
+        ]
+        + [pl.BlockSpec(memory_space=pl.ANY)] * len(extra),
         out_specs=[
             pl.BlockSpec((Q, width), back),
             pl.BlockSpec((Q, 128), back),
             whole((40, width)),
             whole((16, 128)),
             whole((8, xw)),
-        ],
+        ]
+        + [pl.BlockSpec(memory_space=pl.ANY)] * len(traffic.outputs),
         out_shape=[
             jax.ShapeDtypeStruct((length, width), bf16),
             jax.ShapeDtypeStruct((length, 128), bf16),
             jax.ShapeDtypeStruct((40, width), f32),
             jax.ShapeDtypeStruct((16, 128), f32),
             jax.ShapeDtypeStruct((8, xw), f32),
+            *traffic.outputs,
         ],
         scratch_shapes=[
             pltpu.VMEM((128, xw), f32),
@@ -346,10 +421,15 @@
             pltpu.VMEM((Q, xw), bf16),
             pltpu.VMEM((128, 128), f32),
             pltpu.VMEM((8, xw), f32),
+            *traffic.scratch,
         ],
-        compiler_params=pltpu.CompilerParams(vmem_limit_bytes=48 * 2**20),
+        compiler_params=pltpu.CompilerParams(
+            vmem_limit_bytes=48 * 2**20,
+            collective_id=traffic.collective_id,
+            has_side_effects=traffic.collective_id is not None,
+        ),
         name="mixer_backward",
-    )(u, u, dt, tok, segc, segr, wk, bias, head, skip, save, dy, spot)
+    )(u, u, dt, tok, segc, segr, wk, bias, head, skip, save, dy, spot, *extra)
 
 
 def token_facts(seg):
@@ -369,25 +449,824 @@
     return jnp.stack(facts, axis=1).astype(f32)
 
 
+MESH = pl.DeviceIdType.MESH
+ANY = pl.ANY
+PARTS = 4
+
+
+def remote(src, dst, send_sem, recv_sem, device):
+    return pltpu.make_async_remote_copy(
+        src_ref=src, dst_ref=dst, send_sem=send_sem, recv_sem=recv_sem, device_id=device, device_id_type=MESH
+    )
+
+
+class Place:
+    def __init__(self):
+        self.w, self.s = lax.axis_index("wshard"), lax.axis_index("seq")
+        self.z, self.x = self.w // 2, lax.rem(self.w, 2)
+        self.y, self.c = self.s // 2, lax.rem(self.s, 2)
+        self.s_sib = 2 * self.y + 1 - self.c
+        self.s_far = 2 * (1 - self.y) + self.c
+        self.s_diag = 2 * (1 - self.y) + 1 - self.c
+        self.side = (2 * self.z + 1 - self.x, self.s)
+        self.up = (lax.rem(self.w + 2, 8), self.s)
+        self.down = (lax.rem(self.w + 6, 8), self.s)
+        self.sib = (self.w, self.s_sib)
+        self.far = (self.w, self.s_far)
+
+    def greet(self, everyone=False):
+        barrier = pltpu.get_barrier_semaphore()
+        others = [(lax.rem(self.w + k, 8), self.s) for k in range(1, 8)] if everyone else []
+        if everyone:
+            others += [(self.w, lax.rem(self.s + k, 4)) for k in range(1, 4)]
+        else:
+            others = [self.side, self.up, self.down, self.sib, self.far]
+        for other in others:
+            pl.semaphore_signal(barrier, inc=1, device_id=other, device_id_type=MESH)
+        pl.semaphore_wait(barrier, len(others))
+
+
+def dma(*shape):
+    return pltpu.SemaphoreType.DMA(shape)
+
+
+def gather_pieces_start(at, own, full, sems):
+    send, recv, local = sems
+    rows = own.shape[0] // PARTS
+    pltpu.make_async_copy(own, full.at[at.s], local).start()
+    for k in range(PARTS):
+        part = pl.ds(k * rows, rows)
+        remote(own.at[part], full.at[at.s, part], send.at[1, k], recv.at[1, k], at.far).start()
+    for k in range(PARTS):
+        part = pl.ds(k * rows, rows)
+        remote(own.at[part], full.at[at.s, part], send.at[0, k], recv.at[0, k], at.sib).start()
+
+
+def gather_pieces_pass(at, own, full, sems):
+    send, recv, _ = sems
+    rows = own.shape[0] // PARTS
+    for k in range(PARTS):
+        part = pl.ds(k * rows, rows)
+        theirs = full.at[at.s_far, part]
+        remote(theirs, theirs, send.at[1, k], recv.at[1, k], at.far).wait_recv()
+        remote(theirs, theirs, send.at[2, k], recv.at[2, k], at.sib).start()
+
+
+def gather_pieces_end(at, own, full, sems):
+    send, recv, local = sems
+    rows = own.shape[0] // PARTS
+    pltpu.make_async_copy(own, full.at[at.s], local).wait()
+    for k in range(PARTS):
+        part = pl.ds(k * rows, rows)
+        sib, diag, far = full.at[at.s_sib, part], full.at[at.s_diag, part], full.at[at.s_far, part]
+        remote(own.at[part], full.at[at.s, part], send.at[0, k], recv.at[0, k], at.sib).wait_send()
+        remote(own.at[part], full.at[at.s, part], send.at[1, k], recv.at[1, k], at.far).wait_send()
+        remote(far, far, send.at[2, k], recv.at[2, k], at.sib).wait_send()
+        remote(sib, sib, send.at[0, k], recv.at[0, k], at.sib).wait_recv()
+        remote(diag, diag, send.at[2, k], recv.at[2, k], at.sib).wait_recv()
+
+
+def gather_shards(at, main, com, main_all, com_all, sems, between):
+    send, recv, csend, crecv, psend, precv, local = sems
+    half = com.shape[0] // 2
+    mine = pl.ds(pl.multiple_of(at.c * half, half), half)
+    pltpu.make_async_copy(main, main_all.at[at.w], local.at[0]).start()
+    pltpu.make_async_copy(com, com_all.at[at.w], local.at[1]).start()
+
+    def hop(zp, way, device):
+        w = 2 * zp + at.x
+        return (
+            remote(main_all.at[w], main_all.at[w], send.at[way, zp], recv.at[w], device),
+            remote(com_all.at[w, mine], com_all.at[w, mine], csend.at[way, zp], crecv.at[w], device),
+        )
+
+    def first(way, device):
+        return (
+            remote(main, main_all.at[at.w], send.at[way, at.z], recv.at[at.w], device),
+            remote(com.at[mine], com_all.at[at.w, mine], csend.at[way, at.z], crecv.at[at.w], device),
+        )
+
+    def begin(copies):
+        for copy in copies:
+            copy.start()
+
+    begin(first(0, at.side))
+
+    @pl.when(at.z < 3)
+    def _():
+        begin(first(1, at.up))
+
+    @pl.when(at.z > 0)
+    def _():
+        begin(first(2, at.down))
+
+    def arrived(w):
+        remote(main_all.at[w], main_all.at[w], send.at[0, 0], recv.at[w], at.side).wait_recv()
+        held = com_all.at[w, mine]
+        remote(held, held, csend.at[0, 0], crecv.at[w], at.side).wait_recv()
+        remote(held, held, psend.at[w], precv.at[w], at.sib).start()
+
+    for d in (1, 2, 3):
+        if d == 3:
+            between()
+
+        @pl.when(at.z - d >= 0)
+        def _():
+            zp = at.z - d
+            arrived(2 * zp + at.x)
+
+            @pl.when(at.z < 3)
+            def _():
+                begin(hop(zp, 1, at.up))
+
+            begin(hop(zp, 0, at.side))
+
+        @pl.when(at.z + d <= 3)
+        def _():
+            zp = at.z + d
+            arrived(2 * zp + at.x)
+
+            @pl.when(at.z > 0)
+            def _():
+                begin(hop(zp, 2, at.down))
+
+            begin(hop(zp, 0, at.side))
+
+    for zp in range(4):
+        arrived(2 * zp + 1 - at.x)
+    pltpu.make_async_copy(main, main_all.at[at.w], local.at[0]).wait()
+    pltpu.make_async_copy(com, com_all.at[at.w], local.at[1]).wait()
+    other = pl.ds(pl.multiple_of((1 - at.c) * half, half), half)
+    for zp in range(4):
+        for copy in hop(zp, 0, at.side):
+            copy.wait_send()
+
+        @pl.when((at.z < 3) & (zp <= at.z))
+        def _():
+            for copy in hop(zp, 1, at.up):
+                copy.wait_send()
+
+        @pl.when((at.z > 0) & (zp >= at.z))
+        def _():
+            for copy in hop(zp, 2, at.down):
+                copy.wait_send()
+
+    for k in range(1, 8):
+        w = lax.rem(at.w + k, 8)
+        sent, got = com_all.at[w, mine], com_all.at[w, other]
+        remote(sent, sent, psend.at[w], precv.at[w], at.sib).wait_send()
+        remote(got, got, psend.at[w], precv.at[w], at.sib).wait_recv()
+
+
+def gather_kernel(hid, main, com, hid_all, main_all, com_all, *sems):
+    at = Place()
+    at.greet()
+    gather_pieces_start(at, hid, hid_all, sems[0:3])
+    pass_on = lambda: gather_pieces_pass(at, hid, hid_all, sems[0:3])
+    gather_shards(at, main, com, main_all, com_all, sems[3:10], pass_on)
+    gather_pieces_end(at, hid, hid_all, sems[0:3])
+
+
+def gather_first(hid, main, com):
+    shape = lambda n, v: jax.ShapeDtypeStruct((n,) + v.shape, v.dtype)
+    return pl.pallas_call(
+        gather_kernel,
+        in_specs=[pl.BlockSpec(memory_space=ANY)] * 3,
+        out_specs=[pl.BlockSpec(memory_space=ANY)] * 3,
+        out_shape=[shape(4, hid), shape(8, main), shape(8, com)],
+        scratch_shapes=[dma(3, PARTS), dma(3, PARTS), dma()]
+        + [dma(3, 4), dma(8), dma(3, 4), dma(8), dma(8), dma(8), dma(2)],
+        compiler_params=pltpu.CompilerParams(collective_id=1, has_side_effects=True),
+        name="gather_first",
+    )(hid, main, com)
+
+
+SLICES = 8
+
+
+def each_slice(body):
+    def run(k, _):
+        body(k)
+        return 0
+
+    lax.fori_loop(0, SLICES, run, 0)
+
+
+def forward_traffic(cot, rows):
+    class Traffic:
+        inputs = (cot, rows)
+        outputs = (
+            jax.ShapeDtypeStruct((4,) + cot.shape, cot.dtype),
+            jax.ShapeDtypeStruct((2,) + rows.shape, rows.dtype),
+        )
+        scratch = (dma(3, SLICES), dma(3, SLICES), dma(), dma(3, SLICES), dma(2, SLICES), dma())
+        collective_id = 2
+
+        def __init__(self, own, row_own, full, row_full, send, recv, local, rsend, rrecv, rlocal):
+            self.at = at = Place()
+            self.own, self.full, self.row_own, self.row_full = own, full, row_own, row_full
+            self.rrecv = rrecv
+            cut, rcut = own.shape[0] // SLICES, row_own.shape[0] // SLICES
+            part = lambda k: pl.ds(pl.multiple_of(k * cut, cut), cut)
+            rpart = lambda k: pl.ds(pl.multiple_of(k * rcut, rcut), rcut)
+            piece = lambda s, k: full.at[s, part(k)]
+            self.keep = pltpu.make_async_copy(own, full.at[at.s], local)
+            self.rkeep = pltpu.make_async_copy(row_own, row_full.at[at.x], rlocal)
+            self.to_sib = lambda k: remote(own.at[part(k)], piece(at.s, k), send.at[0, k], recv.at[0, k], at.sib)
+            self.to_far = lambda k: remote(own.at[part(k)], piece(at.s, k), send.at[1, k], recv.at[1, k], at.far)
+            self.pass_on = lambda k: remote(piece(at.s_far, k), piece(at.s_far, k), send.at[2, k], recv.at[2, k], at.sib)
+            here = lambda k, n, device: remote(
+                row_full.at[at.x, rpart(k)], row_full.at[at.x, rpart(k)], rsend.at[n, k], rrecv.at[at.x, k], device
+            )
+            self.rows = (lambda k: here(k, 0, at.side), lambda k: here(k, 1, at.up), lambda k: here(k, 2, at.down))
+            got = lambda s, n, k: remote(piece(s, k), piece(s, k), send.at[n, k], recv.at[n, k], at.sib)
+            self.from_sib = lambda k: got(at.s_sib, 0, k)
+            self.from_far = lambda k: got(at.s_far, 1, k)
+            self.from_diag = lambda k: got(at.s_diag, 2, k)
+            other = lambda k: row_full.at[1 - at.x, rpart(k)]
+            self.from_side = lambda k: remote(other(k), other(k), rsend.at[0, k], rrecv.at[1 - at.x, k], at.side)
+
+        def step(self, i, last):
+            at = self.at
+            upward, downward = (at.z >= at.s) & (at.z < 3), (at.z <= at.s) & (at.z > 0)
+            side, up, down = self.rows
+
+            @pl.when(i == 0)
+            def _():
+                at.greet()
+                self.keep.start()
+                each_slice(lambda k: self.to_sib(k).start())
+
+                @pl.when(at.z == at.s)
+                def _():
+                    self.rkeep.start()
+                    self.rkeep.wait()
+
+            k = i - 1
+
+            @pl.when((k >= 0) & (k < SLICES))
+            def _():
+                self.to_far(k).start()
+
+            @pl.when((k >= SLICES) & (k < 2 * SLICES))
+            def _():
+                self.from_far(k - SLICES).wait_recv()
+                self.pass_on(k - SLICES).start()
+
+            far_away = jnp.where(at.z > at.s, at.z - at.s, at.s - at.z)
+            r = i - 1 - 2 * far_away
+
+            @pl.when((r >= 0) & (r < SLICES))
+            def _():
+                @pl.when(at.z != at.s)
+                def _():
+                    side(r).wait_recv()
+
+                side(r).start()
+
+                @pl.when(upward)
+                def _():
+                    up(r).start()
+
+                @pl.when(downward)
+                def _():
+                    down(r).start()
+
+            @pl.when(i == last)
+            def _():
+                self.keep.wait()
+
+                def finish(k):
+                    self.to_sib(k).wait_send()
+                    self.to_far(k).wait_send()
+                    self.pass_on(k).wait_send()
+                    self.from_sib(k).wait_recv()
+                    self.from_diag(k).wait_recv()
+                    side(k).wait_send()
+                    self.from_side(k).wait_recv()
+
+                    @pl.when(upward)
+                    def _():
+                        up(k).wait_send()
+
+                    @pl.when(downward)
+                    def _():
+                        down(k).wait_send()
+
+                each_slice(finish)
+
+    return Traffic
+
+
+def add_into(dst, src, rows):
+    def body(i, _):
+        part = pl.ds(pl.multiple_of(i * 16, 16), 16)
+        dst[part, :] = (dst[part, :].astype(f32) + src[part, :].astype(f32)).astype(bf16)
+        return 0
+
+    lax.fori_loop(0, rows // 16, body, 0)
+
+
+def backward_traffic(layer, rows):
+    piece, cols = layer.shape[1:]
+    rrows = rows.shape[1]
+
+    class Traffic:
+        inputs = (layer, rows)
+        outputs = (jax.ShapeDtypeStruct((piece, cols), f32), jax.ShapeDtypeStruct((rrows, cols), bf16))
+        scratch = (
+            *[pltpu.VMEM((piece, cols), bf16)] * 5,
+            pltpu.VMEM((piece, cols), f32),
+            *[pltpu.VMEM((rrows, cols), bf16)] * 4,
+            dma(3, SLICES),
+            dma(3, SLICES),
+            dma(3),
+            dma(3, SLICES),
+            dma(3, SLICES),
+            dma(2),
+        )
+        collective_id = 3
+
+        def __init__(
+            self, layer, rows, out, rows_out,
+            own_v, far_v, sib_v, pass_v, got_v, sum_v, acc, side_v, low_v, high_v,
+            send, recv, local, rsend, rrecv, rlocal,
+        ):
+            self.at = at = Place()
+            cut, rcut = piece // SLICES, rrows // SLICES
+            part = lambda k: pl.ds(pl.multiple_of(k * cut, cut), cut)
+            rpart = lambda k: pl.ds(pl.multiple_of(k * rcut, rcut), rcut)
+            self.own, self.sib, self.passed, self.got, self.sum = own_v, sib_v, pass_v, got_v, sum_v
+            self.part, self.rpart, self.cut, self.rcut = part, rpart, cut, rcut
+            self.far_v, self.acc, self.side_v, self.low_v, self.high_v = far_v, acc, side_v, low_v, high_v
+            self.load_far = pltpu.make_async_copy(layer.at[at.s_far], far_v, local.at[0])
+            self.load_own = pltpu.make_async_copy(layer.at[at.s], own_v, local.at[1])
+            self.store = pltpu.make_async_copy(sum_v, out, local.at[2])
+            self.to_pass = lambda k: remote(
+                layer.at[at.s_diag, part(k)], pass_v.at[part(k)], send.at[0, k], recv.at[0, k], at.sib
+            )
+            self.to_sib = lambda k: remote(
+                layer.at[at.s_sib, part(k)], sib_v.at[part(k)], send.at[1, k], recv.at[1, k], at.sib
+            )
+            self.to_far = lambda k: remote(
+                far_v.at[part(k)], got_v.at[part(k)], send.at[2, k], recv.at[2, k], at.far
+            )
+            self.load_acc = pltpu.make_async_copy(rows.at[at.x], acc, rlocal.at[0])
+            self.store_acc = pltpu.make_async_copy(acc, rows_out, rlocal.at[1])
+            self.to_side = lambda k: remote(
+                rows.at[1 - at.x, rpart(k)], side_v.at[rpart(k)], rsend.at[0, k], rrecv.at[0, k], at.side
+            )
+            self.to_up = lambda k: remote(
+                acc.at[rpart(k)], low_v.at[rpart(k)], rsend.at[1, k], rrecv.at[1, k], at.up
+            )
+            self.to_down = lambda k: remote(
+                acc.at[rpart(k)], high_v.at[rpart(k)], rsend.at[2, k], rrecv.at[2, k], at.down
+            )
+
+        def step(self, i, last):
+            at = self.at
+
+            @pl.when(i == 0)
+            def _():
+                at.greet()
+                self.load_far.start()
+                self.load_own.start()
+                self.load_acc.start()
+                each_slice(lambda k: self.to_pass(k).start())
+                each_slice(lambda k: self.to_sib(k).start())
+
+            @pl.when(i < SLICES)
+            def _():
+                self.to_side(i).start()
+
+            @pl.when(i == 1)
+            def _():
+                self.load_far.wait()
+                self.load_own.wait()
+                self.load_acc.wait()
+
+            k = i - 1
+
+            @pl.when((k >= 0) & (k < SLICES))
+            def _():
+                self.to_pass(k).wait_recv()
+                add_into(self.far_v.at[self.part(k)], self.passed.at[self.part(k)], self.cut)
+                self.to_far(k).start()
+
+            m = i - SLICES
+
+            @pl.when((m >= 0) & (m < SLICES))
+            def _():
+                self.to_sib(m).wait_recv()
+                self.to_far(m).wait_recv()
+                p = self.part(m)
+                self.sum[p, :] = (
+                    self.own[p, :].astype(f32) + self.sib[p, :].astype(f32) + self.got[p, :].astype(f32)
+                )
+
+            ends = jnp.where(at.z > 3 - at.z, at.z, 3 - at.z)
+            chain = jnp.where(at.z < at.s, at.z, jnp.where(at.z > at.s, 3 - at.z, ends))
+            r = i - 2 - 2 * chain
+
+            @pl.when((r >= 0) & (r < SLICES))
+            def _():
+                acc = self.acc.at[self.rpart(r)]
+                self.to_side(r).wait_recv()
+                add_into(acc, self.side_v.at[self.rpart(r)], self.rcut)
+
+                @pl.when((at.z <= at.s) & (at.z > 0))
+                def _():
+                    self.to_up(r).wait_recv()
+                    add_into(acc, self.low_v.at[self.rpart(r)], self.rcut)
+
+                @pl.when((at.z >= at.s) & (at.z < 3))
+                def _():
+                    self.to_down(r).wait_recv()
+                    add_into(acc, self.high_v.at[self.rpart(r)], self.rcut)
+
+                @pl.when(at.z < at.s)
+                def _():
+                    self.to_up(r).start()
+
+                @pl.when(at.z > at.s)
+                def _():
+                    self.to_down(r).start()
+
+            @pl.when(i == last)
+            def _():
+                self.store.start()
+                self.store_acc.start()
+
+                def finish(k):
+                    self.to_pass(k).wait_send()
+                    self.to_sib(k).wait_send()
+                    self.to_far(k).wait_send()
+                    self.to_side(k).wait_send()
+
+                    @pl.when(at.z < at.s)
+                    def _():
+                        self.to_up(k).wait_send()
+
+                    @pl.when(at.z > at.s)
+                    def _():
+                        self.to_down(k).wait_send()
+
+                each_slice(finish)
+                self.store.wait()
+                self.store_acc.wait()
+
+    return Traffic
+
+
+def reduce_pieces_start(at, partial, bufs, sems):
+    own_v, far_v, from_sib, pass_sib, from_far = bufs
+    send, recv, local = sems
+    rows = partial.shape[1] // PARTS
+    pltpu.make_async_copy(partial.at[at.s_far], far_v, local.at[0]).start()
+    pltpu.make_async_copy(partial.at[at.s], own_v, local.at[1]).start()
+    for k in range(PARTS):
+        part = pl.ds(k * rows, rows)
+        remote(partial.at[at.s_diag, part], pass_sib.at[part], send.at[0, k], recv.at[0, k], at.sib).start()
+    for k in range(PARTS):
+        part = pl.ds(k * rows, rows)
+        remote(partial.at[at.s_sib, part], from_sib.at[part], send.at[1, k], recv.at[1, k], at.sib).start()
+
+
+def reduce_pieces_pass(at, partial, bufs, sems):
+    own_v, far_v, from_sib, pass_sib, from_far = bufs
+    send, recv, local = sems
+    rows = partial.shape[1] // PARTS
+    pltpu.make_async_copy(partial.at[at.s_far], far_v, local.at[0]).wait()
+    for k in range(PARTS):
+        part = pl.ds(k * rows, rows)
+        got = pass_sib.at[part]
+        remote(got, got, send.at[0, k], recv.at[0, k], at.sib).wait_recv()
+        add_into(far_v.at[part], got, rows)
+        remote(far_v.at[part], from_far.at[part], send.at[2, k], recv.at[2, k], at.far).start()
+
+
+def reduce_pieces_end(at, partial, bufs, sems, out):
+    own_v, far_v, from_sib, pass_sib, from_far = bufs
+    send, recv, local = sems
+    rows = partial.shape[1] // PARTS
+    pltpu.make_async_copy(partial.at[at.s], own_v, local.at[1]).wait()
+    for k in range(PARTS):
+        part = pl.ds(k * rows, rows)
+        sib, far = from_sib.at[part], from_far.at[part]
+        remote(sib, sib, send.at[1, k], recv.at[1, k], at.sib).wait_recv()
+        remote(far, far, send.at[2, k], recv.at[2, k], at.far).wait_recv()
+
+        def body(i, _):
+            r = pl.ds(pl.multiple_of(k * rows + i * 16, 16), 16)
+            out[r, :] = own_v[r, :].astype(f32) + from_sib[r, :].astype(f32) + from_far[r, :].astype(f32)
+            return 0
+
+        lax.fori_loop(0, rows // 16, body, 0)
+        remote(partial.at[at.s_diag, part], pass_sib.at[part], send.at[0, k], recv.at[0, k], at.sib).wait_send()
+        remote(partial.at[at.s_sib, part], from_sib.at[part], send.at[1, k], recv.at[1, k], at.sib).wait_send()
+        remote(far_v.at[part], from_far.at[part], send.at[2, k], recv.at[2, k], at.far).wait_send()
+
+
+def far_first(at, i):
+    inner = (at.z == 1) | (at.z == 2)
+    if i >= 2:
+        i = jnp.where(inner, 5 - i, i)
+    return jnp.where(at.z < 2, 3 - i, i)
+
+
+class ReduceShards:
+    def __init__(self, at, partial, cuts, acc, from_side, from_down, from_up, sems):
+        self.at, self.partial, self.cuts, self.acc = at, partial, cuts, acc
+        self.from_side, self.from_down, self.from_up = from_side, from_down, from_up
+        self.send, self.recv_side, self.recv_down, self.recv_up = sems
+        self.rows = acc.shape[1] // cuts
+
+    def unit(self, j):
+        zp, cut = far_first(self.at, j // self.cuts), j % self.cuts
+        return zp, zp * self.cuts + cut, pl.ds(cut * self.rows, self.rows)
+
+    def side_copy(self, j):
+        at = self.at
+        zp, n, part = self.unit(j)
+        return remote(
+            self.partial.at[2 * zp + 1 - at.x, part], self.from_side.at[zp, part],
+            self.send.at[0, n], self.recv_side.at[n], at.side,
+        )
+
+    def up_copy(self, j):
+        zp, n, part = self.unit(j)
+        return remote(
+            self.acc.at[zp, part], self.from_down.at[zp, part], self.send.at[1, n], self.recv_down.at[n], self.at.up
+        )
+
+    def down_copy(self, j):
+        zp, n, part = self.unit(j)
+        return remote(
+            self.acc.at[zp, part], self.from_up.at[zp, part], self.send.at[2, n], self.recv_up.at[n], self.at.down
+        )
+
+    def start(self):
+        self.side_copy(0).start()
+        self.side_copy(1).start()
+
+    def step(self, j):
+        at = self.at
+        zp, _, part = self.unit(j)
+        self.side_copy(j).wait()
+        if j + 2 < 4 * self.cuts:
+            self.side_copy(j + 2).start()
+        acc = self.acc.at[zp, part]
+        add_into(acc, self.from_side.at[zp, part], self.rows)
+
+        @pl.when((at.z > 0) & (zp >= at.z))
+        def _():
+            self.up_copy(j).wait_recv()
+            add_into(acc, self.from_down.at[zp, part], self.rows)
+
+        @pl.when((at.z < 3) & (zp <= at.z))
+        def _():
+            self.down_copy(j).wait_recv()
+            add_into(acc, self.from_up.at[zp, part], self.rows)
+
+        @pl.when(zp > at.z)
+        def _():
+            self.up_copy(j).start()
+
+        @pl.when(zp < at.z)
+        def _():
+            self.down_copy(j).start()
+
+    def end(self):
+        at = self.at
+        for j in range(4 * self.cuts):
+            zp = self.unit(j)[0]
+
+            @pl.when(zp > at.z)
+            def _():
+                self.up_copy(j).wait_send()
+
+            @pl.when(zp < at.z)
+            def _():
+                self.down_copy(j).wait_send()
+
+
+def spread_start(at, rows, out, sems):
+    send, recv, local = sems
+
+    @pl.when(at.s == at.z)
+    def _():
+        copy = pltpu.make_async_copy(rows, out, local)
+        copy.start()
+        remote(rows, out, send.at[1], recv, at.far).start()
+        remote(rows, out, send.at[0], recv, at.sib).start()
+        copy.wait()
+
+
+def spread_pass(at, rows, out, sems):
+    send, recv, local = sems
+
+    @pl.when(at.s_far == at.z)
+    def _():
+        remote(out, out, send.at[1], recv, at.far).wait_recv()
+        remote(out, out, send.at[0], recv, at.sib).start()
+
+
+def spread_end(at, rows, out, sems):
+    send, recv, local = sems
+
+    @pl.when(at.s == at.z)
+    def _():
+        remote(rows, out, send.at[1], recv, at.far).wait_send()
+        remote(rows, out, send.at[0], recv, at.sib).wait_send()
+
+    @pl.when(at.s_far == at.z)
+    def _():
+        remote(out, out, send.at[0], recv, at.sib).wait_send()
+
+    @pl.when((at.s_sib == at.z) | (at.s_diag == at.z))
+    def _():
+        remote(out, out, send.at[0], recv, at.sib).wait_recv()
+
+
+def small_start(at, small, got, sems):
+    send, recv = sems
+    for k in range(1, 8):
+        peer = (lax.rem(at.w + k, 8), at.s)
+        remote(small, got.at[k], send.at[k], recv.at[k], peer).start()
+
+
+def small_pass(at, small, got, total, full, sems, more):
+    send, recv = sems
+    send2, recv2, local = more
+    value = small[...]
+    for k in range(1, 8):
+        remote(small, got.at[k], send.at[k], recv.at[k], at.side).wait_recv()
+        value = value + got[k]
+    total[...] = value
+    pltpu.make_async_copy(total, full.at[at.s], local).start()
+    for k, s in enumerate((at.s_sib, at.s_far, at.s_diag)):
+        remote(total, full.at[at.s], send2.at[k], recv2.at[k], (at.w, s)).start()
+
+
+def small_end(at, small, got, total, full, sems, more):
+    send, recv = sems
+    send2, recv2, local = more
+    pltpu.make_async_copy(total, full.at[at.s], local).wait()
+    for k in range(1, 8):
+        remote(small, got.at[k], send.at[k], recv.at[k], at.side).wait_send()
+    for k, s in enumerate((at.s_sib, at.s_far, at.s_diag)):
+        remote(total, full.at[at.s], send2.at[k], recv2.at[k], (at.w, s)).wait_send()
+        remote(total, full.at[s], send2.at[k], recv2.at[k], (at.w, s)).wait_recv()
+
+
+def reduce_kernel(back, main, com, rows, small,
+                  back_sum, main_out, com_out, rows_out, small_out,
+                  b0, b1, b2, b3, b4,
+                  macc, mside, mlow, mhigh, mown, cown, csib, cacc, cside, clow, chigh, cfar, csum,
+                  sgot, stotal, *sems):
+    at = Place()
+    sems = list(sems)
+    take = lambda n: [sems.pop(0) for _ in range(n)]
+    bsem, msem, csem, cx, rsem, ssem, smore, asem, mlocal = (
+        take(3), take(4), take(4), take(5), take(3), take(2), take(3), take(3), take(1)[0]
+    )
+    bbuf = (b0, b1, b2, b3, b4)
+    half = com.shape[1] // 2
+    mine = pl.ds(pl.multiple_of(at.c * half, half), half)
+    other = pl.ds(pl.multiple_of((1 - at.c) * half, half), half)
+    big = ReduceShards(at, main, 2, macc, mside, mlow, mhigh, msem)
+    few = ReduceShards(at, cown, 1, cacc, cside, clow, chigh, csem)
+    at.greet(everyone=True)
+
+    csib_copy = remote(com.at[:, other], csib, cx[0], cx[1], at.sib)
+    csib_copy.start()
+    own_copy = pltpu.make_async_copy(com.at[:, mine], cown, mlocal.at[4])
+    own_copy.start()
+    big.start()
+    reduce_pieces_start(at, back, bbuf, bsem)
+    for zp in range(4):
+        pltpu.make_async_copy(main.at[2 * zp + at.x], macc.at[zp], mlocal.at[zp]).start()
+    small_start(at, small, sgot, ssem)
+    own_copy.wait()
+    csib_copy.wait_recv()
+    for w in range(8):
+        add_into(cown.at[w], csib.at[w], half)
+    few.start()
+    for zp in range(4):
+        cacc[zp] = cown[2 * zp + at.x]
+    reduce_pieces_pass(at, back, bbuf, bsem)
+    spread_start(at, rows, rows_out, rsem)
+    for zp in range(4):
+        pltpu.make_async_copy(main.at[2 * zp + at.x], macc.at[zp], mlocal.at[zp]).wait()
+    for j in range(8):
+        big.step(j)
+        if j % 2 == 0:
+            few.step(j // 2)
+        if j == 2:
+            small_pass(at, small, sgot, stotal, small_out, ssem, smore)
+    mown[...] = macc[at.z]
+    gather_pieces_start(at, mown, main_out, asem)
+    csum[...] = cacc[at.z].astype(f32)
+    far_copy = remote(csum, cfar, cx[2].at[0], cx[3].at[0], at.far)
+    far_copy.start()
+    reduce_pieces_end(at, back, bbuf, bsem, back_sum)
+    spread_pass(at, rows, rows_out, rsem)
+    far_copy.wait()
+    csum[...] = csum[...] + cfar[...]
+    com_copy = remote(csum, com_out.at[mine], cx[2].at[1], cx[3].at[1], at.sib)
+    com_copy.start()
+    keep_copy = pltpu.make_async_copy(csum, com_out.at[mine], cx[4])
+    keep_copy.start()
+    gather_pieces_pass(at, mown, main_out, asem)
+    big.end()
+    few.end()
+    csib_copy.wait_send()
+    gather_pieces_end(at, mown, main_out, asem)
+    keep_copy.wait()
+    com_copy.wait_send()
+    got = com_out.at[other]
+    remote(csum, got, cx[2].at[1], cx[3].at[1], at.sib).wait_recv()
+    small_end(at, small, sgot, stotal, small_out, ssem, smore)
+    spread_end(at, rows, rows_out, rsem)
+
+
+def reduce_last(back, main, com, rows, small):
+    piece, cols = back.shape[1:]
+    mrows, mcols = main.shape[1:]
+    half, ccols = com.shape[1] // 2, com.shape[2]
+    vm = pltpu.VMEM
+    shards4 = lambda cuts: [dma(3, 4 * cuts), dma(4 * cuts), dma(4 * cuts), dma(4 * cuts)]
+    return pl.pallas_call(
+        reduce_kernel,
+        in_specs=[pl.BlockSpec(memory_space=ANY)] * 4 + [pl.BlockSpec(memory_space=pltpu.VMEM)],
+        out_specs=[pl.BlockSpec(memory_space=pltpu.VMEM)] + [pl.BlockSpec(memory_space=ANY)] * 4,
+        out_shape=[
+            jax.ShapeDtypeStruct((piece, cols), f32),
+            jax.ShapeDtypeStruct((4, mrows, mcols), bf16),
+            jax.ShapeDtypeStruct((2 * half, ccols), f32),
+            jax.ShapeDtypeStruct(rows.shape, bf16),
+            jax.ShapeDtypeStruct((4,) + small.shape, f32),
+        ],
+        scratch_shapes=[vm((piece, cols), bf16)] * 5
+        + [vm((4, mrows, mcols), bf16)] * 4
+        + [vm((mrows, mcols), bf16)]
+        + [vm((8, half, ccols), bf16)] * 2
+        + [vm((4, half, ccols), bf16)] * 4
+        + [vm((half, ccols), f32)] * 2
+        + [vm((8,) + small.shape, f32), vm(small.shape, f32)]
+        + [dma(3, PARTS), dma(3, PARTS), dma(2)]
+        + shards4(2)
+        + shards4(1)
+        + [dma(), dma(), dma(2), dma(2), dma()]
+        + [dma(2), dma(), dma()]
+        + [dma(8), dma(8)]
+        + [dma(3), dma(3), dma()]
+        + [dma(3, PARTS), dma(3, PARTS), dma()]
+        + [dma(5)],
+        compiler_params=pltpu.CompilerParams(
+            collective_id=4, has_side_effects=True, vmem_limit_bytes=56 * 2**20
+        ),
+        name="reduce_last",
+    )(back, main, com, rows, small)
+
+
 def over_rows(left, right):
     return lax.dot_general(
         left, right, (((0,), (0,)), ((), ())), preferred_element_type=jnp.float32
     )
 
 
-def own_columns(weight, group, groups):
-    heads = H // groups
-    wide = heads * P_SIZE
-    dt = lax.dynamic_slice_in_dim(weight, 2 * E + 2 * N + group * heads, heads, 1)
-    return jnp.concatenate(
-        [
-            lax.dynamic_slice_in_dim(weight, group * wide, wide, 1),
-            lax.dynamic_slice_in_dim(weight, E + group * wide, wide, 1),
-            weight[:, 2 * E : 2 * E + 2 * N],
-            jnp.pad(dt, ((0, 0), (0, 128 - heads))),
-        ],
-        axis=1,
-    )
+def gather_plain(hid, main, com):
+    hid_all = lax.all_gather(hid, "seq", axis=0)
+    main_all = lax.all_gather(main, "wshard", axis=0)
+    return hid_all, main_all, lax.all_gather(com, "wshard", axis=0)
+
+
+def gather_more_plain(cot, rows, wide):
+    cot_all = lax.all_gather(cot, "seq", axis=0)
+    cols = lax.all_to_all(rows, "wshard", split_axis=1, concat_axis=0, tiled=True)
+    own = lax.dynamic_slice_in_dim(cols, lax.axis_index("seq") * wide, wide, 0)
+    return cot_all, lax.all_gather(own, "wshard", axis=1, tiled=True)
+
+
+def reduce_scattered(v, axis):
+    return lax.psum_scatter(v, axis, scatter_dimension=0, tiled=False)
+
+
+def reduce_first_plain(layer, rows):
+    layer_sum = reduce_scattered(layer, "seq").astype(f32)
+    rows = rows.reshape(-1, rows.shape[-1])
+    part = lax.psum_scatter(rows, "wshard", scatter_dimension=1, tiled=True)
+    part = lax.all_gather(part, "seq", axis=0, tiled=True)
+    return layer_sum, lax.all_to_all(part, "wshard", split_axis=0, concat_axis=1, tiled=True)
+
+
+def reduce_plain(back, main, com, rows, small):
+    back_sum = reduce_scattered(back, "seq").astype(f32)
+    main_out = lax.all_gather(reduce_scattered(main, "wshard"), "seq", axis=0)
+    com_all = lax.all_gather(reduce_scattered(com, "wshard"), "seq", axis=0)
+    small_out = lax.all_gather(lax.psum(small, "wshard"), "seq", axis=0)
+    return back_sum, main_out, jnp.sum(com_all.astype(f32), axis=0), rows, small_out
 
 
 def shards(
@@ -405,33 +1284,32 @@
     cotangent,
 ):
     group = lax.axis_index("seq")
-    groups = lax.axis_size("seq")
+    groups, owners = lax.axis_size("seq"), lax.axis_size("wshard")
+    direct = (groups, owners) == (4, 8)
     heads = H // groups
     wide = heads * P_SIZE
-    piece = hidden.shape[1]
     length = segments.shape[1]
     hidden_own, cot_own = hidden[0], cotangent[0]
-    hidden_all = lax.all_gather(hidden_own, "seq", axis=0, tiled=True)
     in_gain = norm_gain.astype(f32)[:, None]
     in_scaled = (in_weight.astype(f32) * in_gain).astype(bf16)
-    in_own = lax.all_gather(own_columns(in_scaled, group, groups), "wshard", axis=0, tiled=True)
+    main = jnp.concatenate(
+        [
+            lax.dynamic_slice_in_dim(in_scaled, group * wide, wide, 1),
+            lax.dynamic_slice_in_dim(in_scaled, E + group * wide, wide, 1),
+        ],
+        axis=1,
+    )
+    com = jnp.pad(in_scaled[:, 2 * E :], ((0, 0), (0, 128 - H)))
     out_gain = gate_gain.astype(f32)[:, None]
     out_scaled = (out_weight.astype(f32) * out_gain).astype(bf16)
-    out_cols = lax.all_to_all(out_scaled, "wshard", split_axis=1, concat_axis=0, tiled=True)
-    out_own = lax.all_gather(
-        lax.dynamic_slice_in_dim(out_cols, group * wide, wide, 0), "wshard", axis=1, tiled=True
-    )
-    cot_all = lax.all_gather(cot_own, "seq", axis=0, tiled=True)
-
-    hidden_wide = hidden_all.astype(f32)
-    scale = lax.rsqrt(jnp.mean(hidden_wide * hidden_wide, axis=-1, keepdims=True) + eps)
-    gate = jnp.dot(hidden_all, in_own[:, :wide], preferred_element_type=f32) * scale
-    u = (
-        jnp.dot(hidden_all, in_own[:, wide : 2 * wide + 2 * N], preferred_element_type=f32) * scale
-    ).astype(bf16)
-    dt = (
-        jnp.dot(hidden_all, in_own[:, 2 * wide + 2 * N :], preferred_element_type=f32) * scale
-    ).astype(bf16)
+    gather = gather_first if direct else gather_plain
+    hidden_all, w_main, w_com = gather(hidden_own, main, com)
+    hidden_all = hidden_all.reshape(length, D)
+    w_main, w_com = w_main.reshape(D, 2 * wide), w_com.reshape(D, -1)
+    w_bc = w_com[:, : 2 * N]
+    w_dt = jnp.pad(
+        lax.dynamic_slice_in_dim(w_com, 2 * N + group * heads, heads, 1), ((0, 0), (0, 128 - heads))
+    )
 
     seg = segments[0]
     tok = token_facts(seg)
@@ -445,103 +1323,105 @@
     head = jnp.pad(jnp.stack([own_head(step_bias), rate]), ((0, 0), (0, 128 - heads)))
     skip = jnp.repeat(own_head(skip_scale), P_SIZE)[None]
     spot = (jnp.arange(wide)[:, None] // P_SIZE == jnp.arange(128)[None]).astype(bf16)
-    mixed, save = mixer_fwd(u, dt, tok, segc, segr, taps, bias, head, skip)
+    beside, more = (forward_traffic(cot_own, out_scaled), (cot_own, out_scaled)) if direct else (NoTraffic, ())
+    u, dt, gate, scale, mixed, save, *got = mixer_fwd(
+        beside, more, hidden_all, w_main, w_bc, w_dt, tok, segc, segr, taps, bias, head, skip
+    )
+    cot_all, w_out = got if direct else gather_more_plain(cot_own, out_scaled, wide)
+    cot_all, w_out = cot_all.reshape(length, D), w_out.reshape(wide, D)
 
     mixed_wide = mixed.astype(f32)
     sg = jax.nn.sigmoid(gate)
     silu = gate * sg
     g = mixed_wide * silu
     g_low = g.astype(bf16)
-    a = lax.dot_general(cot_all, out_own, (((1,), (1,)), ((), ())), preferred_element_type=f32)
+    a = lax.dot_general(cot_all, w_out, (((1,), (1,)), ((), ())), preferred_element_type=f32)
     sums = lax.psum(jnp.stack([jnp.sum(g * g, axis=1), jnp.sum(a * g, axis=1)]), "seq")
     r = lax.rsqrt(sums[0] / E + eps)[:, None]
     pull = (r * r * r) * (sums[1] / E)[:, None]
     d_g = r * a - g * pull
-    gate_gain_part = jnp.sum(a * (g * r), axis=0)
     d_mixed = (d_g * silu).astype(bf16)
     d_gate = (d_g * mixed_wide * (sg * (1.0 + gate * (1.0 - sg))) * scale).astype(bf16)
-    partial = (jnp.dot(g_low, out_own, preferred_element_type=f32) * r).astype(bf16)
-    out_sum = lax.psum_scatter(partial, "seq", scatter_dimension=0, tiled=True)
-    layer_output = hidden_own.astype(f32) + out_sum.astype(f32)
+    layer_part = (jnp.dot(g_low, w_out, preferred_element_type=f32) * r).astype(bf16)
     cot_r = (cot_all.astype(f32) * r).astype(bf16)
     out_part = over_rows(g_low, cot_r).astype(bf16)
-    out_part = lax.psum_scatter(out_part, "wshard", scatter_dimension=1, tiled=True)
-    out_part = lax.all_gather(out_part, "seq", axis=0, tiled=True)
-    out_part = lax.all_to_all(out_part, "wshard", split_axis=0, concat_axis=1, tiled=True)
-    out_weight_grad = out_part.astype(f32) * out_gain
-
-    du, ddt, taps_sum, head_sum, skip_sum = mixer_bwd(
-        u, dt, tok, segc, segr, taps, bias, head, skip, save, d_mixed, spot
-    )
+
+    layer_part, out_part = layer_part.reshape(groups, -1, D), out_part.reshape(2, -1, D)
+    beside, more = (backward_traffic(layer_part, out_part), (layer_part, out_part)) if direct else (NoTraffic, ())
+    du, ddt, taps_sum, head_sum, skip_sum, *got = mixer_bwd(
+        beside, more, u, dt, tok, segc, segr, taps, bias, head, skip, save, d_mixed, spot
+    )
+    layer_sum, out_sum = got if direct else reduce_first_plain(layer_part, out_part)
     du = (du.astype(f32) * scale).astype(bf16)
     ddt = (ddt.astype(f32) * scale).astype(bf16)
-    d_proj = jnp.concatenate([d_gate, du, ddt], axis=1)
-    in_part = over_rows(hidden_all, d_proj).astype(bf16)
-    b_part = lax.dot_general(
-        d_proj, in_own, (((1,), (1,)), ((), ())), preferred_element_type=f32
-    ).astype(bf16)
-    b_sum = lax.psum_scatter(b_part, "seq", scatter_dimension=0, tiled=True).astype(f32)
+    d_main = jnp.concatenate([d_gate, du[:, :wide]], axis=1)
+    d_com = jnp.concatenate([du[:, wide:], ddt], axis=1)
+    main_part = over_rows(hidden_all, d_main).astype(bf16)
+    com_part = over_rows(hidden_all, d_com).astype(bf16)
+    com_part = jnp.concatenate(
+        [
+            com_part[:, : 2 * N],
+            lax.dynamic_update_slice_in_dim(
+                jnp.zeros((D, 128), bf16), com_part[:, 2 * N : 2 * N + heads], group * heads, 1
+            ),
+        ],
+        axis=1,
+    )
+    w_rest = jnp.concatenate([w_bc, w_dt], axis=1)
+    nt = lambda p, q: lax.dot_general(p, q, (((1,), (1,)), ((), ())), preferred_element_type=f32)
+    back_part = (nt(d_main, w_main) + nt(d_com, w_rest)).astype(bf16)
+
+    head_sum = jnp.sum(head_sum.reshape(2, 8, -1), axis=1)[:, :heads]
+    head_sum = head_sum * jnp.stack([jnp.ones_like(rate), rate])
+    skip_sum = jnp.sum(skip_sum, axis=0).reshape(heads, P_SIZE).sum(axis=1)
+    small = jnp.concatenate(
+        [
+            jnp.sum(taps_sum.reshape(5, 8, -1), axis=1),
+            jnp.pad(jnp.concatenate([head_sum, skip_sum[None]]), ((0, 0), (0, wide + 2 * N - heads))),
+        ]
+    )
+    reduce = reduce_last if direct else reduce_plain
+    back_sum, main_out, com_out, out_sum, small_out = reduce(
+        back_part.reshape(groups, -1, D),
+        main_part.reshape(owners, -1, 2 * wide),
+        com_part.reshape(owners, D // owners, -1),
+        out_sum,
+        small,
+    )
+
     own_wide = hidden_own.astype(f32)
+    layer_output = own_wide + layer_sum
     own_scale = lax.rsqrt(jnp.mean(own_wide * own_wide, axis=-1, keepdims=True) + eps)
     hidden_grad = (
         cot_own.astype(f32)
-        + b_sum
-        - own_wide * (own_scale * own_scale) * jnp.mean(b_sum * own_wide, axis=-1, keepdims=True)
-    )
-    norm_part = jnp.sum(b_sum * own_wide, axis=0)
-
-    in_part = lax.psum_scatter(in_part, "wshard", scatter_dimension=0, tiled=True)
-    in_all = lax.all_gather(in_part, "seq", axis=0, tiled=False).astype(f32)
-    side = lambda lo, hi: jnp.concatenate([in_all[i, :, lo:hi] for i in range(groups)], axis=1)
-    in_weight_grad = (
-        jnp.concatenate(
-            [
-                side(0, wide),
-                side(wide, 2 * wide),
-                jnp.sum(in_all[:, :, 2 * wide : 2 * wide + 2 * N], axis=0),
-                side(2 * wide + 2 * N, 2 * wide + 2 * N + heads),
-            ],
-            axis=1,
-        )
-        * in_gain
-    )
-
-    taps_sum = jnp.sum(taps_sum.reshape(5, 8, -1), axis=1)
-    head_sum = jnp.sum(head_sum.reshape(2, 8, -1), axis=1)[:, :heads]
-    head_sum = head_sum * jnp.stack([jnp.ones_like(rate), rate])
-    skip_sum = jnp.sum(skip_sum, axis=0).reshape(heads, P_SIZE).sum(axis=1)
-    place = lambda v, size, at: lax.dynamic_update_slice_in_dim(
-        jnp.zeros(v.shape[:-1] + (size,), f32), v, at, v.ndim - 1
-    )
-    chan_sums = jnp.concatenate([place(taps_sum[:, :wide], E, group * wide), taps_sum[:, wide:]], axis=1)
-    flat = jnp.concatenate(
-        [
-            chan_sums.reshape(-1),
-            place(jnp.concatenate([head_sum, skip_sum[None]]), H, group * heads).reshape(-1),
-            place(gate_gain_part, E, group * wide),
-            norm_part,
-        ]
-    )
-    flat = lax.psum(flat, ("wshard", "seq"))
-    channels = E + 2 * N
-    chan_sums = flat[: 5 * channels].reshape(5, channels)
-    at = 5 * channels
-    head_sums = flat[at : at + 3 * H].reshape(3, H)
-    at = at + 3 * H
-    shard = lax.axis_index("wshard")
-    gate_rows, norm_rows = out_weight.shape[0], in_weight.shape[0]
-    gate_gain_grad = lax.dynamic_slice_in_dim(flat[at : at + E], shard * gate_rows, gate_rows, 0) / gate_gain.astype(f32)
-    norm_gain_grad = lax.dynamic_slice_in_dim(flat[at + E :], shard * norm_rows, norm_rows, 0) / norm_gain.astype(f32)
+        + back_sum
+        - own_wide * (own_scale * own_scale) * jnp.mean(back_sum * own_wide, axis=-1, keepdims=True)
+    )
+    main_out = main_out.astype(f32)
+    in_sum = jnp.concatenate(
+        [main_out[i, :, :wide] for i in range(groups)]
+        + [main_out[i, :, wide:] for i in range(groups)]
+        + [com_out[:, : 2 * N + H]],
+        axis=1,
+    )
+    in_weight_grad = in_sum * in_gain
+    norm_gain_grad = jnp.sum(in_sum * in_weight.astype(f32), axis=1)
+    out_sum = out_sum.astype(f32)
+    out_weight_grad = out_sum * out_gain
+    gate_gain_grad = jnp.sum(out_sum * out_weight.astype(f32), axis=1)
+    side = lambda lo, hi: jnp.concatenate([small_out[i, lo:hi, :wide] for i in range(groups)], axis=1)
+    chan = jnp.concatenate([side(0, 5), jnp.sum(small_out[:, :5, wide:], axis=0)], axis=1)
+    per_head = lambda k: small_out[:, k, :heads].reshape(H)
     return (
         layer_output[None],
         hidden_grad[None],
         norm_gain_grad,
         in_weight_grad,
-        chan_sums[:4],
-        chan_sums[4],
-        head_sums[0],
-        head_sums[1],
-        head_sums[2],
+        chan[:4],
+        chan[4],
+        per_head(5),
+        per_head(6),
+        per_head(7),
         gate_gain_grad,
         out_weight_grad,
     )

time: 842 us -> 456 us (0.54)
  the two profiles are of different devices: /device:TPU:0 before, /device:TPU:15 now
where the time goes in v2:
time: 456 us; the launch traced here: 448 us
  Pallas kernels  293 us (64%)
  matrix products  70.8 us (16%)
  other arithmetic  39.1 us (9%)
  local copies, waits for them, and re-layouts  33.2 us (7%)
  blocking collectives  10.2 us (2%)
    pallas_call x1, Pallas kernels, reduce_last(): pl.pallas_call(reduce_kernel, in_specs=[pl.BlockSpec(memory_space=ANY)] *...  107 us
    pallas_call x1, Pallas kernels, gather_first(): pl.pallas_call(gather_kernel, in_specs=[pl.BlockSpec(memory_space=ANY)] *...  73.2 us
    pallas_call x1, Pallas kernels, mixer_fwd(): pl.pallas_call(functools.partial(fwd_kernel, traffic), grid=(n + 1,), in_...  57 us
    pallas_call x1, Pallas kernels, mixer_bwd(): pl.pallas_call(functools.partial(bwd_kernel, traffic), grid=(n,), in_spec...  55.4 us
    dot_general x3, matrix products, over_rows(): lax.dot_general(left, right, (((0,), (0,)), ((), ())), preferred_element_...  32.1 us
    dot_general x2, matrix products, shards(): lax.dot_general(p, q, (((1,), (1,)), ((), ())), preferred_element_type=f32)  19.2 us
    dot_general x1, matrix products, shards(): lax.dot_general(cot_all, w_out, (((1,), (1,)), ((), ())), preferred_eleme...  12.3 us
    unnamed x72, local copies, waits for them, and re-layouts  11 us

profile of v2, /device:TPU:15, one launch (start us, length us, event | category | flops | bytes accessed | tf_op | source)
XLA Modules:
  0.0 448.0 jit_solution(18128627271991556712)
XLA Ops:
  14.6 2.5 fusion.17.rest_1_
  17.1 2.2 fusion.6
  21.2 73.2 %gather_first.1 = (bf16[4,512,1536]{2,1,0:T(8,128)(2,1)}, bf16[8,192,1536]{2,1,0:T(8,128)(2,1)}, bf16[8,192,384]{2,1,0:T(8,128)(2,1)}) custom-call(bf16[512,1536]{1,0:T(8,128)(2,1)} %bitcast.110, bf16[192,1536]{1,0:T(8,128)(2,1)} %pad_maximum_fusion.7.main, bf16[192,384]{1,0:T(8,128)(2,1)} %pad.21.com), custom_call_target="tpu_custom_call" | custom-call | tf_op jit(solution)/shard_map/gather_first/pallas_call | solution.py:632
  98.2 57.0 %mixer_forward.1 = (bf16[2048,1024]{1,0:T(8,128)(2,1)}, bf16[2048,128]{1,0:T(8,128)(2,1)S(1)}, f32[2048,768]{1,0:T(8,128)}, f32[2048,1]{1,0:T(8,128)S(1)}, bf16[...) custom-call(bf16[2048,1536]{1,0:T(8,128)(2,1)} %bitcast.112, ...), custom_call_target="tpu_custom_call" | custom-call | tf_op jit(solution)/shard_map/mixer_forward/pallas_call | solution.py:176
  157.0 1.6 reduce
  158.5 12.3 %multiply_reduce_fusion.1 = (f32[2048]{0:T(1024)S(1)}, f32[2048]{0:T(1024)S(1)}, f32[2048,768]{1,0:T(8,128)}) fusion(bf16[2048,768]{1,0:T(8,128)(2,1)} %get-tuple-element.40, f32[2048,768]{1,0:T(8,128)} %get-tuple-element.41, bf16[2048,1536]{1,0:T(8,128)(2,1)} %bitcast.141, bf16[768,1536]{1,0:T(8,128)(2,1)} %bitcast.143), kind=kOutput, calls=%fused_computation.16 | convolution fusion | flops 4847562752 | bytes 24395776 | tf_op jit(solution)/shard_map/dot_general | solution.py:1338
  171.5 10.2 %psum.7 = f32[2,2048]{1,0:T(2,128)S(1)} all-reduce(f32[2,2048]{1,0:T(2,128)} %pad_maximum_fusion.10), channel_id=1, replica_groups=mesh['wshard'=8,'seq'=4] {'seq'}, use_global_device_ids=true, to_apply=%region_2.3 | all-reduce | flops 4096 | bytes 32768 | tf_op jit(solution)/shard_map/psum | solution.py:1339
  181.8 13.2 %fusion.9 = bf16[768,1536]{1,0:T(8,128)(2,1)} fusion(bf16[2048,1536]{1,0:T(8,128)(2,1)} %bitcast.142, f32[2048]{0:T(1024)S(1)} %bitcast.125, bf16[2048,768]{1,0:T(8,128)(2,1)} %get-tuple-element.40, f32[2048,768]{1,0:T(8,128)} %get-tuple-element.41), kind=kOutput, calls=%fused_computation.28 | convolution fusion | flops 4853465088 | bytes 18096128 | tf_op jit(solution)/shard_map/dot_general | solution.py:1234
  195.0 5.9 %fusion.2 = (bf16[2048,768]{1,0:T(8,128)(2,1)}, bf16[2048,768]{1,0:T(8,128)(2,1)}) fusion(bf16[2048,768]{1,0:T(8,128)(2,1)S(1)} %copy-done.18, f32[2048,768]{1,0:T(8,128)S(1)} %copy-done.12, f32[2048]{0:T(1024)S(1)} %reduce, f32[2048]{0:T(1024)S(1)} %fusion.31, f32[2048,768]{1,0:T(8,128)S(1)} %copy-done.13, f32[2048]{0:T(1024)S(1)} %bitcast.127), kind=kLoop, calls=%fused_computation.9 | loop fusion | flops 29884416 | bytes 22044672 | tf_op jit(solution)/shard_map/convert_element_type | solution.py:1344
  200.9 7.1 %multiply_convert_fusion.1 = bf16[2048,1536]{1,0:T(8,128)(2,1)} fusion(bf16[768,1536]{1,0:T(8,128)(2,1)S(1)} %bitcast.144, f32[2048]{0:T(1024)S(1)} %bitcast.128, bf16[2048,768]{1,0:T(8,128)(2,1)S(1)} %copy-done.18, f32[2048,768]{1,0:T(8,128)S(1)} %copy-done.12), kind=kOutput, calls=%fused_computation.2 | convolution fusion | flops 4849139712 | bytes 18096128 | tf_op jit(solution)/shard_map/dot_general | solution.py:1345
  208.0 55.4 %mixer_backward.1 = (bf16[2048,1024]{1,0:T(8,128)(2,1)}, bf16[2048,128]{1,0:T(8,128)(2,1)S(1)}, f32[40,1024]{1,0:T(8,128)S(1)}, f32[16,128]{1,0:T(8,128)S(1)}, f...) custom-call(bf16[2048,1024]{1,0:T(8,128)(2,1)} %get-tuple-element.37.u_ref.halo_ref, ...), custom_call_target="tpu_custom_call" | custom-call | tf_op jit(solution)/shard_map/mixer_backward/pallas_call | solution.py:377
  267.7 1.4 multiply_convert_fusion.7
  269.1 3.1 multiply_convert_fusion.2
  272.8 6.8 %convolution_convert_fusion.1 = bf16[1536,384]{0,1:T(8,128)(2,1)S(1)} fusion(bf16[2048,1536]{1,0:T(8,128)(2,1)} %bitcast.113, bf16[2048,128]{1,0:T(8,128)(2,1)S(1)} %multiply_convert_fusion.7, bf16[2048,256]{1,0:T(8,128)(2,1)S(1)} %slice.182), kind=kOutput, calls=%fused_computation.39 | convolution fusion | flops 2419654656 | bytes 9043968 | tf_op jit(solution)/shard_map/dot_general | solution.py:1234
  279.6 12.1 %convolution_convert_fusion = bf16[1536,1536]{1,0:T(8,128)(2,1)} fusion(bf16[2048,1536]{1,0:T(8,128)(2,1)S(1)} %bitcast.116, bf16[2048,768]{1,0:T(8,128)(2,1)S(1)} %slice.181, bf16[2048,768]{1,0:T(8,128)(2,1)S(1)} %copy-done.17), kind=kOutput, calls=%fused_computation.6 | convolution fusion | flops 9678618624 | bytes 17301504 | tf_op jit(solution)/shard_map/dot_general | solution.py:1234
  293.5 1.5 dynamic_update_slice.3
  296.3 1.4 copy.62
  297.8 13.7 %fusion.8 = f32[2048,1536]{1,0:T(8,128)S(1)} fusion(bf16[1536,1536]{1,0:T(8,128)(2,1)} %bitcast.121, bf16[2048,768]{1,0:T(8,128)(2,1)} %copy-done.15, bf16[2048,768]{1,0:T(8,128)(2,1)} %get-tuple-element.64), kind=kOutput, calls=%fused_computation.27 | convolution fusion | flops 9676259328 | bytes 23592960 | tf_op jit(solution)/shard_map/dot_general | solution.py:1371
  311.5 5.5 %add_convert_fusion = bf16[2048,1536]{1,0:T(8,128)(2,1)} fusion(f32[2048,1536]{1,0:T(8,128)S(1)} %fusion.8, bf16[1536,128]{1,0:T(8,128)(2,1)S(1)} %pad.22.wdt_ref, bf16[1536,256]{1,0:T(8,128)(2,1)S(1)} %slice.176.bc_ref, bf16[2048,128]{1,0:T(8,128)(2,1)S(1)} %copy-done.21, bf16[2048,256]{1,0:T(8,128)(2,1)S(1)} %slice.182), kind=kOutput, calls=%fused_computation | convolution fusion | flops 2427715584 | bytes 21626880 | tf_op jit(solution)/shard_map/dot_general | solution.py:1371
  317.0 107.4 %reduce_last.1 = (f32[512,1536]{1,0:T(8,128)}, bf16[4,192,1536]{2,1,0:T(8,128)(2,1)}, f32[192,384]{1,0:T(8,128)}, bf16[384,1536]{1,0:T(8,128)(2,1)}, f32[4,8,1024]{2,1,0:T(8,128)}) custom-call(bf16[4,512,1536]{2,1,0:T(8,128)(2,1)} %bitcast.109, bf16[8,192,1536]{2,1,0:T(8,128)(2,1)} %bitcast.119, bf16[8,192,384]{2,1,0:T(8,128)(2,1)} %bitcast.118, ...), custom_call_target="tpu_custom_call" | custom-call | tf_op jit(solution)/shard_map/reduce_last/pallas_call | solution.py:1199
  424.4 2.7 fusion.11
  427.7 3.5 fusion.14
  439.6 2.4 convert_multiply_fusion.7
  443.9 3.7 broadcast_multiply_fusion
  (142 shorter events, 40.4 us)
Async XLA Ops:
  2.8 14.3 %copy-start.24 = (f32[192]{0:T(256)}, f32[192]{0:T(256)S(1)}, u32[]{:S(2)}) copy-start(f32[192]{0:T(256)S(1)} %convert_element_type.93) | copy-start | bytes 2308
  19.3 77.5 %copy-start.1 = (s32[1,2048]{1,0:T(1,128)S(1)}, s32[1,2048]{1,0:T(1,128)}, u32[]{:S(2)}) copy-start(s32[1,2048]{1,0:T(1,128)} %param.13) | copy-start | bytes 24580
  96.9 1.3 copy-start
  181.8 13.2 %copy-start.12 = (f32[2048,768]{1,0:T(8,128)S(1)}, f32[2048,768]{1,0:T(8,128)}, u32[]{:S(2)}) copy-start(f32[2048,768]{1,0:T(8,128)} %get-tuple-element.41) | copy-start | bytes 18874372
  181.8 13.2 %copy-start.13 = (f32[2048,768]{1,0:T(8,128)S(1)}, f32[2048,768]{1,0:T(8,128)}, u32[]{:S(2)}) copy-start(f32[2048,768]{1,0:T(8,128)} %get-tuple-element.90) | copy-start | bytes 18874372
  181.8 13.2 %copy-start.18 = (bf16[2048,768]{1,0:T(8,128)(2,1)S(1)}, bf16[2048,768]{1,0:T(8,128)(2,1)}, u32[]{:S(2)}) copy-start(bf16[2048,768]{1,0:T(8,128)(2,1)} %get-tuple-element.40) | copy-start | bytes 9437188
  195.0 5.9 %copy-start.26 = (bf16[2,384,1536]{2,1,0:T(8,128)(2,1)S(1)}, bf16[2,384,1536]{2,1,0:T(8,128)(2,1)}, u32[]{:S(2)}) copy-start(bf16[2,384,1536]{2,1,0:T(8,128)(2,1)} %get-tuple-element.43) | copy-start | bytes 7077892
  200.9 7.1 %copy-start.5 = (bf16[2048,128]{1,0:T(8,128)(2,1)S(1)}, bf16[2048,128]{1,0:T(8,128)(2,1)}, u32[]{:S(2)}) copy-start(bf16[2048,128]{1,0:T(8,128)(2,1)} %copy-done.4) | copy-start | bytes 1572868
  263.4 1.0 copy-start.2
  269.1 3.6 copy-start.20
  272.4 7.2 %slice-start = ((s8[6291456]{0:T(1024)(128)(4,1)}), s8[4194304]{0:T(1024)(128)(4,1)S(1)}, s32[]{:S(2)}) async-start(s8[6291456]{0:T(1024)(128)(4,1)} %bitcast.114), calls=%async_computation | async-start | bytes 8388608
  272.8 6.8 %copy-start.15 = (bf16[2048,768]{1,0:T(8,128)(2,1)}, bf16[2048,768]{1,0:T(8,128)(2,1)S(1)}, u32[]{:S(2)}) copy-start(bf16[2048,768]{1,0:T(8,128)(2,1)S(1)} %slice.181) | copy-start | bytes 9437188
  272.8 6.8 %slice-start.1 = ((s8[6291456]{0:T(1024)(128)(4,1)}), s8[2097152]{0:T(1024)(128)(4,1)S(1)}, s32[]{:S(2)}) async-start(s8[6291456]{0:T(1024)(128)(4,1)} %bitcast.114), calls=%async_computation.1 | async-start | bytes 4194304
  272.8 6.8 %copy-start.17 = (bf16[2048,768]{1,0:T(8,128)(2,1)S(1)}, bf16[2048,768]{1,0:T(8,128)(2,1)}, u32[]{:S(2)}) copy-start(bf16[2048,768]{1,0:T(8,128)(2,1)} %get-tuple-element.64) | copy-start | bytes 9437188
  297.7 13.7 %copy-start.21 = (bf16[2048,128]{1,0:T(8,128)(2,1)S(1)}, bf16[2048,128]{1,0:T(8,128)(2,1)}, u32[]{:S(2)}) copy-start(bf16[2048,128]{1,0:T(8,128)(2,1)} %copy-done.20) | copy-start | bytes 1572868
  317.0 107.4 %copy-start.8 = (bf16[1,512,1536]{2,1,0:T(8,128)(2,1)S(1)}, bf16[1,512,1536]{2,1,0:T(8,128)(2,1)}, u32[]{:S(2)}) copy-start(bf16[1,512,1536]{2,1,0:T(8,128)(2,1)} %param.12) | copy-start | bytes 4718596
  317.0 110.2 %copy-start.16 = (f32[512,1536]{1,0:T(8,128)S(1)}, f32[512,1536]{1,0:T(8,128)}, u32[]{:S(2)}) copy-start(f32[512,1536]{1,0:T(8,128)} %get-tuple-element.44) | copy-start | bytes 9437188
  424.4 2.8 copy-start.9
  424.4 3.3 copy-start.11
  427.7 11.3 %copy-start.19 = (bf16[4,192,1536]{2,1,0:T(8,128)(2,1)S(1)}, bf16[4,192,1536]{2,1,0:T(8,128)(2,1)}, u32[]{:S(2)}) copy-start(bf16[4,192,1536]{2,1,0:T(8,128)(2,1)} %get-tuple-element.53) | copy-start | bytes 7077892
  431.2 8.4 %copy-start.14 = (bf16[384,1536]{1,0:T(8,128)(2,1)S(1)}, bf16[384,1536]{1,0:T(8,128)(2,1)}, u32[]{:S(2)}) copy-start(bf16[384,1536]{1,0:T(8,128)(2,1)} %param.22) | copy-start | bytes 3538948
  433.8 5.7 %copy-start.22 = (bf16[384,1536]{1,0:T(8,128)(2,1)S(1)}, bf16[384,1536]{1,0:T(8,128)(2,1)}, u32[]{:S(2)}) copy-start(bf16[384,1536]{1,0:T(8,128)(2,1)} %get-tuple-element.56) | copy-start | bytes 3538948
  442.0 1.8 copy-start.10
  442.0 1.8 copy-start.25
  (5 other events, 4.2 us)

commit v3 on v2

v3 whole, which is shorter than its diff:
```python
import functools

import jax
import jax.numpy as jnp
from jax import lax
from jax.experimental import pallas as pl
from jax.experimental.pallas import tpu as pltpu
from jax.sharding import PartitionSpec as P

D = 1536
H = 48
P_SIZE = 64
N = 128
E = 3072

eps = 1e-05
f32, bf16 = jnp.float32, jnp.bfloat16
Q = 128
NEG = -1e30


def dot(a, b):
    return jnp.dot(a, b, preferred_element_type=f32)


def dot_nt(a, b):
    return lax.dot_general(a, b, (((1,), (1,)), ((), ())), preferred_element_type=f32)


def dot3(tri, v):
    hi = v.astype(bf16)
    rest = v - hi.astype(f32)
    mid = rest.astype(bf16)
    low = (rest - mid.astype(f32)).astype(bf16)
    return dot(tri, hi) + dot(tri, mid) + dot(tri, low)


def sigmoid(v):
    return 1.0 / (1.0 + jnp.exp(-v))


def spread_col(v, col):
    return jnp.broadcast_to(v[:, col : col + 1], (Q, 128))


def softplus(v):
    return jnp.maximum(v, 0.0) + jnp.log1p(jnp.exp(-jnp.abs(v)))


def conv_pre(useen, flags, wk, bias, lanes, chans):
    pre = bias[:, chans] + wk[3:4, chans] * useen[8 : 8 + Q, lanes]
    for j in (1, 2, 3):
        pre = pre + wk[3 - j : 4 - j, chans] * (useen[8 - j : 8 - j + Q, lanes] * flags[j])
    return pre


class Facts:
    def __init__(self, chunk, seg_ref, par_ref, xw):
        self.group = lax.axis_index("seq")
        self.heads = xw // P_SIZE
        self.xw = xw
        near = seg_ref[pl.ds(pl.multiple_of(chunk * Q, 8), Q + 16), :]
        now = near[8 : 8 + Q]
        same = lambda other: jnp.broadcast_to(jnp.where(other == now, 1.0, 0.0), (Q, 128))
        self.before = [None] + [same(near[8 - j : 8 - j + Q]) for j in (1, 2, 3)]
        self.after = lambda j: same(near[8 + j : 8 + j + Q])
        self.carried = same(near[7:8])
        self.samelast = same(near[7 + Q : 8 + Q])
        self.now = now
        self.turn = self.heads * self.group
        lane = lax.broadcasted_iota(jnp.int32, (8, 128), 1)
        par = self.own(par_ref[...])
        self.bias = par[0:1]
        self.rate = jnp.where(lane < self.heads, -jnp.exp(par), 0.0)[1:2]

    def own(self, v):
        lane = lax.broadcasted_iota(jnp.int32, v.shape, 1)
        return jnp.where(lane < self.heads, pltpu.roll(v, lax.rem(128 - self.turn, 128), 1), 0.0)

    def back(self, v):
        return pltpu.roll(v, self.turn, 1)

    def chans(self, p):
        if p < self.xw // 128:
            return pl.ds(pl.multiple_of(self.group * self.xw + 128 * p, 128), 128)
        at = E + 128 * (p - self.xw // 128)
        return slice(at, at + 128)


class NoTraffic:
    inputs, outputs, scratch, collective_id = (), (), (), None

    def __init__(self, *refs):
        pass

    def step(self, i, last):
        pass


def fwd_kernel(traffic, hid_ref, main_ref, com_ref, seg_ref, segr_ref, wk_ref, bias_ref, par_ref, skip_ref, *rest):
    n_in, n_out = len(traffic.inputs), len(traffic.outputs)
    extra_in, rest = rest[:n_in], rest[n_in:]
    u_ref, dt_ref, gate_ref, scale_ref, mixed_ref, save_ref = rest[:6]
    extra_out, rest = rest[6 : 6 + n_out], rest[6 + n_out :]
    state, useen, act, next_u, next_dt = rest[:5]
    step_no = pl.program_id(0)
    traffic(*extra_in, *extra_out, *rest[5:]).step(step_no, pl.num_programs(0) - 1)
    xw = mixed_ref.shape[1]
    width = xw + 256
    pairs = xw // 128
    facts = Facts(jnp.maximum(step_no - 1, 0), seg_ref, par_ref, xw)

    @pl.when(step_no == 0)
    def _():
        next_u[...] = jnp.zeros_like(next_u)
        next_dt[...] = jnp.zeros_like(next_dt)

    @pl.when(step_no <= 1)
    def _():
        state[...] = jnp.zeros_like(state)
        useen[0:8, :] = jnp.zeros((8, width), f32)

    useen[8 : 8 + Q, :] = next_u[...]
    dt_now = next_dt[...]

    low = hid_ref[...]
    total = jnp.zeros((Q, 128), f32)
    for k in range(low.shape[1] // 128):
        part = low[:, 128 * k : 128 * k + 128].astype(f32)
        total = total + part * part
    scale = lax.rsqrt(jnp.sum(total, axis=1, keepdims=True) / low.shape[1] + eps)
    scale_ref[...] = scale
    for k in range(xw // 256):
        gate_ref[:, 256 * k : 256 * k + 256] = dot(low, main_ref[:, 256 * k : 256 * k + 256]) * scale
    for k in range(xw // 256):
        got = (dot(low, main_ref[:, xw + 256 * k : xw + 256 * k + 256]) * scale).astype(bf16)
        u_ref[:, 256 * k : 256 * k + 256] = got
        next_u[:, 256 * k : 256 * k + 256] = got.astype(f32)
    got = (dot(low, com_ref[:, 0:256]) * scale).astype(bf16)
    u_ref[:, xw : xw + 256] = got
    next_u[:, xw : xw + 256] = got.astype(f32)
    got = facts.own((dot(low, com_ref[:, 256:384]) * scale).astype(bf16).astype(f32))
    dt_ref[...] = got.astype(bf16)
    next_dt[...] = got

    carried, samelast = facts.carried, facts.samelast
    for p in range(width // 128):
        lanes = slice(128 * p, 128 * p + 128)
        pre = conv_pre(useen, facts.before, wk_ref, bias_ref, lanes, facts.chans(p))
        act[:, lanes] = pre * sigmoid(pre)
    tail = useen[Q : Q + 8, :]
    useen[0:8, :] = tail

    step = softplus(dt_now + facts.bias)
    row = lax.broadcasted_iota(jnp.int32, (Q, Q), 0)
    col = lax.broadcasted_iota(jnp.int32, (Q, Q), 1)
    tri = jnp.where(row >= col, 1.0, 0.0).astype(bf16)
    decay = dot3(tri, step * facts.rate)
    decay_t = decay.T
    madd = jnp.where((row >= col) & (facts.now == segr_ref[0]), 0.0, NEG)
    b_now = act[:, xw : xw + 128]
    c_low = act[:, xw + 128 : xw + 256].astype(bf16)
    gram = dot_nt(c_low, b_now.astype(bf16))
    b_t = b_now.T.astype(bf16)
    left = lax.broadcasted_iota(jnp.int32, (Q, 128), 1) < 64
    for p in range(pairs):
        lanes = slice(128 * p, 128 * p + 128)
        d0, d1 = spread_col(decay, 2 * p), spread_col(decay, 2 * p + 1)
        dp = jnp.where(left, d0, d1)
        sp = jnp.where(left, spread_col(step, 2 * p), spread_col(step, 2 * p + 1))
        xs = act[:, lanes]
        xp = xs * sp
        m0 = gram * jnp.exp(d0 - decay_t[2 * p : 2 * p + 1, :] + madd)
        m1 = gram * jnp.exp(d1 - decay_t[2 * p + 1 : 2 * p + 2, :] + madd)
        both = jnp.concatenate([m0.astype(bf16), m1.astype(bf16)], axis=1)
        stacked = jnp.concatenate(
            [jnp.where(left, xp, 0.0).astype(bf16), jnp.where(left, 0.0, xp).astype(bf16)], axis=0
        )
        st = state[:, lanes]
        st_low = st.astype(bf16)
        save_ref[0, :, lanes] = st_low
        y = dot(both, stacked) + dot(c_low, st_low) * (jnp.exp(dp) * carried)
        mixed_ref[:, lanes] = (y + skip_ref[:, facts.chans(p)] * xs).astype(bf16)
        last = dp[Q - 1 : Q, :]
        to_end = (xp * (jnp.exp(last - dp) * samelast)).astype(bf16)
        state[:, lanes] = st * (jnp.exp(last) * carried[Q - 1 : Q, :]) + dot(b_t, to_end)


def mixer_fwd(traffic, extra, hid, main, com, seg, segr, wk, bias, par, skip):
    length, depth = hid.shape
    xw = main.shape[1] // 2
    width = xw + 256
    n = length // Q
    whole = lambda shape: pl.BlockSpec(shape, lambda i: (0,) * len(shape), pipeline_mode=pl.Buffered(1))
    ahead = lambda i: (jnp.minimum(i, n - 1), 0)
    now = lambda i: (jnp.maximum(i - 1, 0), 0)
    now3 = lambda i: (jnp.maximum(i - 1, 0), 0, 0)
    return pl.pallas_call(
        functools.partial(fwd_kernel, traffic),
        grid=(n + 1,),
        in_specs=[
            pl.BlockSpec((Q, depth), ahead),
            whole(main.shape),
            whole(com.shape),
            whole(seg.shape),
            pl.BlockSpec((1, 1, Q), now3),
            whole(wk.shape),
            whole(bias.shape),
            whole(par.shape),
            whole(skip.shape),
        ]
        + [pl.BlockSpec(memory_space=pl.ANY)] * len(extra),
        out_specs=[
            pl.BlockSpec((Q, width), ahead),
            pl.BlockSpec((Q, 128), ahead),
            pl.BlockSpec((Q, xw), ahead),
            pl.BlockSpec((Q, 1), ahead),
            pl.BlockSpec((Q, xw), now),
            pl.BlockSpec((1, 128, xw), now3),
        ]
        + [pl.BlockSpec(memory_space=pl.ANY)] * len(traffic.outputs),
        out_shape=[
            jax.ShapeDtypeStruct((length, width), bf16),
            jax.ShapeDtypeStruct((length, 128), bf16),
            jax.ShapeDtypeStruct((length, xw), f32),
            jax.ShapeDtypeStruct((length, 1), f32),
            jax.ShapeDtypeStruct((length, xw), bf16),
            jax.ShapeDtypeStruct((n, 128, xw), bf16),
            *traffic.outputs,
        ],
        scratch_shapes=[
            pltpu.VMEM((128, xw), f32),
            pltpu.VMEM((Q + 8, width), f32),
            pltpu.VMEM((Q, width), f32),
            pltpu.VMEM((Q, width), f32),
            pltpu.VMEM((Q, 128), f32),
            *traffic.scratch,
        ],
        compiler_params=pltpu.CompilerParams(
            vmem_limit_bytes=48 * 2**20,
            collective_id=traffic.collective_id,
            has_side_effects=traffic.collective_id is not None,
        ),
        name="mixer_forward",
    )(hid, main, com, seg, segr, wk, bias, par, skip, *extra)


def bwd_kernel(traffic, u_ref, halo_ref, dt_ref, scale_ref, seg_ref, segr_ref, wk_ref, bias_ref, par_ref, skip_ref,
               save_ref, dy_ref, *rest):
    n_in, n_out = len(traffic.inputs), len(traffic.outputs)
    extra_in, rest = rest[:n_in], rest[n_in:]
    du_ref, ddt_ref, small_ref = rest[:3]
    extra_out, rest = rest[3 : 3 + n_out], rest[3 + n_out :]
    dstate, useen, act, slope, dpre, keep_y, keep_x, prod_a, prod_b, rows_a, held = rest[:11]
    wgrad_ref, hgrad_ref, sgrad_ref, spot_ref = rest[11:15]
    step_no = pl.program_id(0)
    last_step = pl.num_programs(0) - 1
    traffic(*extra_in, *extra_out, *rest[15:]).step(step_no, last_step)
    width = u_ref.shape[1]
    xw = width - 256
    pairs = xw // 128

    @pl.when(step_no == 0)
    def _():
        dstate[...] = jnp.zeros_like(dstate)
        dpre[Q : Q + 8, :] = jnp.zeros((8, width), f32)
        wgrad_ref[...] = jnp.zeros_like(wgrad_ref)
        hgrad_ref[...] = jnp.zeros_like(hgrad_ref)
        sgrad_ref[...] = jnp.zeros_like(sgrad_ref)
        rows_a[...] = jnp.zeros_like(rows_a)
        head_of = lax.broadcasted_iota(jnp.int32, (xw, 128), 0) // P_SIZE
        mark = head_of == lax.broadcasted_iota(jnp.int32, (xw, 128), 1)
        spot_ref[...] = jnp.where(mark, 1.0, 0.0).astype(bf16)

    useen[0:8, :] = halo_ref[...].astype(f32)[8:16, :]
    useen[8 : 8 + Q, :] = u_ref[...].astype(f32)
    facts = Facts(last_step - step_no, seg_ref, par_ref, xw)
    flags, carried, samelast = facts.before, facts.carried, facts.samelast
    for p in range(width // 128):
        lanes = slice(128 * p, 128 * p + 128)
        pre = conv_pre(useen, flags, wk_ref, bias_ref, lanes, facts.chans(p))
        sg = sigmoid(pre)
        act[:, lanes] = pre * sg
        slope[:, lanes] = sg * (1.0 + pre * (1.0 - sg))

    raw = dt_ref[...].astype(f32) + facts.bias
    step = softplus(raw)
    rate = facts.rate
    row = lax.broadcasted_iota(jnp.int32, (Q, Q), 0)
    col = lax.broadcasted_iota(jnp.int32, (Q, Q), 1)
    tri = jnp.where(row >= col, 1.0, 0.0).astype(bf16)
    upper = jnp.where(row <= col, 1.0, 0.0).astype(bf16)
    below = jnp.where(row > col, 1.0, 0.0).astype(bf16)
    decay = dot3(tri, step * rate)
    decay_t = decay.T
    madd = jnp.where((row <= col) & (facts.now == segr_ref[0]), 0.0, NEG)
    b_now, c_now = act[:, xw : xw + 128], act[:, xw + 128 : xw + 256]
    b_low, c_low = b_now.astype(bf16), c_now.astype(bf16)
    c_t = c_now.T.astype(bf16)
    gram = dot_nt(b_low, c_low)
    left = lax.broadcasted_iota(jnp.int32, (Q, 128), 1) < 64
    lane = lax.broadcasted_iota(jnp.int32, (Q, 128), 1)
    dgram = jnp.zeros((Q, Q), f32)
    cols_b = jnp.zeros((Q, 128), f32)
    for p in range(pairs):
        lanes = slice(128 * p, 128 * p + 128)
        d0, d1 = spread_col(decay, 2 * p), spread_col(decay, 2 * p + 1)
        dp = jnp.where(left, d0, d1)
        sp = jnp.where(left, spread_col(step, 2 * p), spread_col(step, 2 * p + 1))
        xs = act[:, lanes]
        xp = xs * sp
        dy_low = dy_ref[:, lanes]
        dy = dy_low.astype(f32)
        stacked = jnp.concatenate(
            [jnp.where(left, dy, 0.0).astype(bf16), jnp.where(left, 0.0, dy).astype(bf16)], axis=0
        )
        pair = dot_nt(xp.astype(bf16), stacked)
        mts = []
        for k, dk in ((0, d0), (1, d1)):
            h = 2 * p + k
            e = jnp.exp(decay_t[h : h + 1, :] - dk + madd)
            f = e * pair[:, 128 * k : 128 * k + 128]
            dgram = dgram + f
            w = gram * f
            mts.append((gram * e).astype(bf16))
            rows_a[h : h + 1, :] = jnp.sum(w, axis=0, keepdims=True)
            cols_b = jnp.where(lane == h, jnp.sum(w, axis=1, keepdims=True), cols_b)
        within = dot(jnp.concatenate(mts, axis=1), stacked)
        grow = jnp.exp(dp) * carried
        dy_in = dy * grow
        dy_in_low = dy_in.astype(bf16)
        keep_y[:, lanes] = dy_in_low
        st = save_ref[0, :, lanes]
        prod_a[:, lanes] = (dy_in * dot(c_low, st)).astype(bf16)
        last = dp[Q - 1 : Q, :]
        fade = jnp.exp(last - dp) * samelast
        ds = dstate[:, lanes]
        ds_low = ds.astype(bf16)
        xe = xp * fade
        keep_x[:, lanes] = xe.astype(bf16)
        later = dot(b_low, ds_low)
        prod_b[:, lanes] = (xe * later).astype(bf16)
        retain = jnp.exp(last) * carried[Q - 1 : Q, :]
        held[0:1, lanes] = jnp.sum(ds * st.astype(f32), axis=0, keepdims=True) * retain
        dxs = sp * (within + later * fade) + skip_ref[:, facts.chans(p)] * dy
        skp = xs * dy
        sgrad_ref[:, lanes] += jnp.sum(skp.reshape(Q // 8, 8, 128), axis=0)
        dpre[0:Q, lanes] = dxs * slope[:, lanes]
        dstate[:, lanes] = ds * retain + dot(c_t, dy_in_low)
        if p == 0:
            db_in, dc_in = dot_nt(keep_x[:, lanes], ds_low), dot_nt(dy_in_low, st)
        else:
            db_in, dc_in = db_in + dot_nt(keep_x[:, lanes], ds_low), dc_in + dot_nt(dy_in_low, st)

    dg_low = dgram.astype(bf16)
    db = dot(dg_low, c_low) + db_in
    dc = dot(dgram.T.astype(bf16), b_low) + dc_in
    dpre[0:Q, xw : xw + 128] = db * slope[:, xw : xw + 128]
    dpre[0:Q, xw + 128 : xw + 256] = dc * slope[:, xw + 128 : xw + 256]

    spot = spot_ref[...]
    a_in = dot(prod_a[...], spot)
    b_in = dot(prod_b[...], spot)
    hv = jnp.broadcast_to(held[0:1, :], (8, xw))
    h_hi = hv.astype(bf16)
    h_lo = (hv - h_hi.astype(f32)).astype(bf16)
    through = (dot(h_hi, spot) + dot(h_lo, spot))[0:1, :]
    a_own = rows_a[...].T
    cross = dot3(upper, a_own - cols_b + a_in) + dot3(below, b_in) + through
    total = cols_b + b_in
    sg = sigmoid(raw)
    ratio = jnp.where(step > 1e-30, sg / jnp.maximum(step, 1e-30), 1.0)
    draw = total * ratio + rate * cross * sg
    scale = jnp.broadcast_to(scale_ref[...], (Q, 128))
    ddt_ref[...] = facts.back(draw * scale).astype(bf16)
    hgrad_ref[0:8, :] += jnp.sum(draw.reshape(Q // 8, 8, 128), axis=0)
    hgrad_ref[8:16, :] += jnp.sum((step * cross).reshape(Q // 8, 8, 128), axis=0)

    ahead = [None] + [facts.after(j) for j in (1, 2, 3)]
    for p in range(width // 128):
        lanes = slice(128 * p, 128 * p + 128)
        own = dpre[0:Q, lanes]
        chans = facts.chans(p)
        du = wk_ref[3:4, chans] * own
        wgrad_ref[24:32, lanes] += jnp.sum((own * useen[8 : 8 + Q, lanes]).reshape(Q // 8, 8, 128), axis=0)
        wgrad_ref[32:40, lanes] += jnp.sum(own.reshape(Q // 8, 8, 128), axis=0)
        for j in (1, 2, 3):
            du = du + wk_ref[3 - j : 4 - j, chans] * (dpre[j : j + Q, lanes] * ahead[j])
            moved = own * (useen[8 - j : 8 - j + Q, lanes] * flags[j])
            k = 3 - j
            wgrad_ref[8 * k : 8 * k + 8, lanes] += jnp.sum(moved.reshape(Q // 8, 8, 128), axis=0)
        du_ref[:, lanes] = (du * scale).astype(bf16)
    first = dpre[0:8, :]
    dpre[Q : Q + 8, :] = first

    @pl.when(step_no == last_step)
    def _():
        small_ref[...] = jnp.zeros_like(small_ref)
        for k in range(5):
            small_ref[k : k + 1, :] = jnp.sum(wgrad_ref[8 * k : 8 * k + 8, :], axis=0, keepdims=True)
        small_ref[5:6, 0:128] = jnp.sum(hgrad_ref[0:8, :], axis=0, keepdims=True)
        small_ref[6:7, 0:128] = rate * jnp.sum(hgrad_ref[8:16, :], axis=0, keepdims=True)
        skips = sgrad_ref[...]
        hi = skips.astype(bf16)
        mid = (skips - hi.astype(f32)).astype(bf16)
        by_head = dot(hi, spot_ref[...]) + dot(mid, spot_ref[...])
        small_ref[7:8, 0:128] = jnp.sum(by_head, axis=0, keepdims=True)


def mixer_bwd(traffic, extra, u, dt, scale, seg, segr, wk, bias, par, skip, save, dy):
    length, width = u.shape
    xw = width - 256
    n = length // Q
    whole = lambda shape: pl.BlockSpec(shape, lambda i: (0,) * len(shape))
    back = lambda i: (n - 1 - i, 0)
    return pl.pallas_call(
        functools.partial(bwd_kernel, traffic),
        grid=(n,),
        in_specs=[
            pl.BlockSpec((Q, width), back),
            pl.BlockSpec((16, width), lambda i: (jnp.maximum((n - 1 - i) * (Q // 16) - 1, 0), 0)),
            pl.BlockSpec((Q, 128), back),
            pl.BlockSpec((Q, 1), back),
            whole(seg.shape),
            pl.BlockSpec((1, 1, Q), lambda i: (n - 1 - i, 0, 0)),
            whole(wk.shape),
            whole(bias.shape),
            whole(par.shape),
            whole(skip.shape),
            pl.BlockSpec((1, 128, xw), lambda i: (n - 1 - i, 0, 0)),
            pl.BlockSpec((Q, xw), back),
        ]
        + [pl.BlockSpec(memory_space=pl.ANY)] * len(extra),
        out_specs=[
            pl.BlockSpec((Q, width), back),
            pl.BlockSpec((Q, 128), back),
            whole((8, width)),
        ]
        + [pl.BlockSpec(memory_space=pl.ANY)] * len(traffic.outputs),
        out_shape=[
            jax.ShapeDtypeStruct((length, width), bf16),
            jax.ShapeDtypeStruct((length, 128), bf16),
            jax.ShapeDtypeStruct((8, width), f32),
            *traffic.outputs,
        ],
        scratch_shapes=[
            pltpu.VMEM((128, xw), f32),
            pltpu.VMEM((Q + 8, width), f32),
            pltpu.VMEM((Q, width), f32),
            pltpu.VMEM((Q, width), f32),
            pltpu.VMEM((Q + 8, width), f32),
            pltpu.VMEM((Q, xw), bf16),
            pltpu.VMEM((Q, xw), bf16),
            pltpu.VMEM((Q, xw), bf16),
            pltpu.VMEM((Q, xw), bf16),
            pltpu.VMEM((128, 128), f32),
            pltpu.VMEM((8, xw), f32),
            pltpu.VMEM((40, width), f32),
            pltpu.VMEM((16, 128), f32),
            pltpu.VMEM((8, xw), f32),
            pltpu.VMEM((xw, 128), bf16),
            *traffic.scratch,
        ],
        compiler_params=pltpu.CompilerParams(
            vmem_limit_bytes=48 * 2**20,
            collective_id=traffic.collective_id,
            has_side_effects=traffic.collective_id is not None,
        ),
        name="mixer_backward",
    )(u, u, dt, scale, seg, segr, wk, bias, par, skip, save, dy, *extra)


MESH = pl.DeviceIdType.MESH
ANY = pl.ANY
PARTS = 4


def remote(src, dst, send_sem, recv_sem, device):
    return pltpu.make_async_remote_copy(
        src_ref=src, dst_ref=dst, send_sem=send_sem, recv_sem=recv_sem, device_id=device, device_id_type=MESH
    )


class Place:
    def __init__(self):
        self.w, self.s = lax.axis_index("wshard"), lax.axis_index("seq")
        self.z, self.x = self.w // 2, lax.rem(self.w, 2)
        self.y, self.c = self.s // 2, lax.rem(self.s, 2)
        self.s_sib = 2 * self.y + 1 - self.c
        self.s_far = 2 * (1 - self.y) + self.c
        self.s_diag = 2 * (1 - self.y) + 1 - self.c
        self.side = (2 * self.z + 1 - self.x, self.s)
        self.up = (lax.rem(self.w + 2, 8), self.s)
        self.down = (lax.rem(self.w + 6, 8), self.s)
        self.sib = (self.w, self.s_sib)
        self.far = (self.w, self.s_far)

    def greet(self, everyone=False):
        barrier = pltpu.get_barrier_semaphore()
        others = [(lax.rem(self.w + k, 8), self.s) for k in range(1, 8)] if everyone else []
        if everyone:
            others += [(self.w, lax.rem(self.s + k, 4)) for k in range(1, 4)]
        else:
            others = [self.side, self.up, self.down, self.sib, self.far]
        for other in others:
            pl.semaphore_signal(barrier, inc=1, device_id=other, device_id_type=MESH)
        pl.semaphore_wait(barrier, len(others))


def dma(*shape):
    return pltpu.SemaphoreType.DMA(shape)


def gather_pieces_start(at, own, slot, sems):
    send, recv, local = sems
    rows = own.shape[0] // PARTS
    pltpu.make_async_copy(own, slot(at.s), local).start()
    for k in range(PARTS):
        part = pl.ds(k * rows, rows)
        remote(own.at[part], slot(at.s).at[part], send.at[1, k], recv.at[1, k], at.far).start()
    for k in range(PARTS):
        part = pl.ds(k * rows, rows)
        remote(own.at[part], slot(at.s).at[part], send.at[0, k], recv.at[0, k], at.sib).start()


def gather_pieces_pass(at, own, slot, sems):
    send, recv, _ = sems
    rows = own.shape[0] // PARTS
    for k in range(PARTS):
        part = pl.ds(k * rows, rows)
        theirs = slot(at.s_far).at[part]
        remote(theirs, theirs, send.at[1, k], recv.at[1, k], at.far).wait_recv()
        remote(theirs, theirs, send.at[2, k], recv.at[2, k], at.sib).start()


def gather_pieces_end(at, own, slot, sems):
    send, recv, local = sems
    rows = own.shape[0] // PARTS
    pltpu.make_async_copy(own, slot(at.s), local).wait()
    for k in range(PARTS):
        part = pl.ds(k * rows, rows)
        sib, diag, far = slot(at.s_sib).at[part], slot(at.s_diag).at[part], slot(at.s_far).at[part]
        remote(own.at[part], slot(at.s).at[part], send.at[0, k], recv.at[0, k], at.sib).wait_send()
        remote(own.at[part], slot(at.s).at[part], send.at[1, k], recv.at[1, k], at.far).wait_send()
        remote(far, far, send.at[2, k], recv.at[2, k], at.sib).wait_send()
        remote(sib, sib, send.at[0, k], recv.at[0, k], at.sib).wait_recv()
        remote(diag, diag, send.at[2, k], recv.at[2, k], at.sib).wait_recv()


CUTS = 2


def gather_shards(at, main, com, main_all, com_all, sems, between):
    send, recv, csend, crecv, psend, precv, local = sems
    half, cut = com.shape[0] // 2, main.shape[0] // CUTS
    mine = pl.ds(pl.multiple_of(at.c * half, half), half)
    keep = pltpu.make_async_copy(main, main_all.at[at.w], local.at[0])
    com_keep = pltpu.make_async_copy(com, com_all.at[at.w], local.at[1])
    keep.start()
    com_keep.start()

    def hop(zp, q, way, device, own=False):
        w, n, part = 2 * zp + at.x, zp * CUTS + q, pl.ds(q * cut, cut)
        slot, com_slot = main_all.at[w, part], com_all.at[w, mine]
        copies = [remote(main.at[part] if own else slot, slot, send.at[way, n], recv.at[w * CUTS + q], device)]
        if q == 0:
            copies.append(remote(com.at[mine] if own else com_slot, com_slot, csend.at[way, zp], crecv.at[w], device))
        return copies

    def begin(copies):
        for copy in copies:
            copy.start()

    def sent(copies):
        for copy in copies:
            copy.wait_send()

    def all_ways(act, q):
        act(hop(at.z, q, 0, at.side, True))

        @pl.when(at.z < 3)
        def _():
            act(hop(at.z, q, 1, at.up, True))

        @pl.when(at.z > 0)
        def _():
            act(hop(at.z, q, 2, at.down, True))

    def arrived(w, q):
        slot = main_all.at[w, pl.ds(q * cut, cut)]
        remote(slot, slot, send.at[0, 0], recv.at[w * CUTS + q], at.side).wait_recv()
        if q == 0:
            held = com_all.at[w, mine]
            remote(held, held, csend.at[0, 0], crecv.at[w], at.side).wait_recv()
            remote(held, held, psend.at[w], precv.at[w], at.sib).start()

    for q in range(CUTS):
        if q > 0:
            all_ways(sent, q - 1)
        all_ways(begin, q)
    for d in (1, 2, 3):
        if d == 3:
            between()
        for q in range(CUTS):

            @pl.when(at.z - d >= 0)
            def _():
                zp = at.z - d
                arrived(2 * zp + at.x, q)

                @pl.when(at.z < 3)
                def _():
                    begin(hop(zp, q, 1, at.up))

                begin(hop(zp, q, 0, at.side))

            @pl.when(at.z + d <= 3)
            def _():
                zp = at.z + d
                arrived(2 * zp + at.x, q)

                @pl.when(at.z > 0)
                def _():
                    begin(hop(zp, q, 2, at.down))

                begin(hop(zp, q, 0, at.side))

    for zp in range(4):
        for q in range(CUTS):
            arrived(2 * zp + 1 - at.x, q)
    keep.wait()
    com_keep.wait()
    all_ways(sent, CUTS - 1)
    for zp in range(4):
        for q in range(CUTS):

            @pl.when(at.z != zp)
            def _():
                sent(hop(zp, q, 0, at.side))

            @pl.when((at.z < 3) & (zp < at.z))
            def _():
                sent(hop(zp, q, 1, at.up))

            @pl.when((at.z > 0) & (zp > at.z))
            def _():
                sent(hop(zp, q, 2, at.down))

    other = pl.ds(pl.multiple_of((1 - at.c) * half, half), half)
    for k in range(1, 8):
        w = lax.rem(at.w + k, 8)
        gone, got = com_all.at[w, mine], com_all.at[w, other]
        remote(gone, gone, psend.at[w], precv.at[w], at.sib).wait_send()
        remote(got, got, psend.at[w], precv.at[w], at.sib).wait_recv()


def gather_kernel(hid, main, com, hid_all, main_all, com_all, *sems):
    at = Place()
    at.greet()
    slot = lambda s: hid_all.at[s]
    gather_pieces_start(at, hid, slot, sems[0:3])
    pass_on = lambda: gather_pieces_pass(at, hid, slot, sems[0:3])
    gather_shards(at, main, com, main_all, com_all, sems[3:10], pass_on)
    gather_pieces_end(at, hid, slot, sems[0:3])


def gather_first(hid, main, com):
    shape = lambda n, v: jax.ShapeDtypeStruct((n,) + v.shape, v.dtype)
    return pl.pallas_call(
        gather_kernel,
        in_specs=[pl.BlockSpec(memory_space=ANY)] * 3,
        out_specs=[pl.BlockSpec(memory_space=ANY)] * 3,
        out_shape=[shape(4, hid), shape(8, main), shape(8, com)],
        scratch_shapes=[dma(3, PARTS), dma(3, PARTS), dma()]
        + [dma(3, 4 * CUTS), dma(8 * CUTS), dma(3, 4), dma(8), dma(8), dma(8), dma(2)],
        compiler_params=pltpu.CompilerParams(collective_id=1, has_side_effects=True),
        name="gather_first",
    )(hid, main, com)


SLICES = 8


def each_slice(body):
    def run(k, _):
        body(k)
        return 0

    lax.fori_loop(0, SLICES, run, 0)


def forward_traffic(cot, rows):
    class Traffic:
        inputs = (cot, rows)
        outputs = (
            jax.ShapeDtypeStruct((4,) + cot.shape, cot.dtype),
            jax.ShapeDtypeStruct((2,) + rows.shape, rows.dtype),
        )
        scratch = (dma(3, SLICES), dma(3, SLICES), dma(), dma(3, SLICES), dma(2, SLICES), dma())
        collective_id = 2

        def __init__(self, own, row_own, full, row_full, send, recv, local, rsend, rrecv, rlocal):
            self.at = at = Place()
            self.own, self.full, self.row_own, self.row_full = own, full, row_own, row_full
            self.rrecv = rrecv
            cut, rcut = own.shape[0] // SLICES, row_own.shape[0] // SLICES
            part = lambda k: pl.ds(pl.multiple_of(k * cut, cut), cut)
            rpart = lambda k: pl.ds(pl.multiple_of(k * rcut, rcut), rcut)
            piece = lambda s, k: full.at[s, part(k)]
            self.keep = pltpu.make_async_copy(own, full.at[at.s], local)
            self.rkeep = pltpu.make_async_copy(row_own, row_full.at[at.x], rlocal)
            self.to_sib = lambda k: remote(own.at[part(k)], piece(at.s, k), send.at[0, k], recv.at[0, k], at.sib)
            self.to_far = lambda k: remote(own.at[part(k)], piece(at.s, k), send.at[1, k], recv.at[1, k], at.far)
            self.pass_on = lambda k: remote(piece(at.s_far, k), piece(at.s_far, k), send.at[2, k], recv.at[2, k], at.sib)
            here = lambda k, n, device: remote(
                row_full.at[at.x, rpart(k)], row_full.at[at.x, rpart(k)], rsend.at[n, k], rrecv.at[at.x, k], device
            )
            self.rows = (lambda k: here(k, 0, at.side), lambda k: here(k, 1, at.up), lambda k: here(k, 2, at.down))
            got = lambda s, n, k: remote(piece(s, k), piece(s, k), send.at[n, k], recv.at[n, k], at.sib)
            self.from_sib = lambda k: got(at.s_sib, 0, k)
            self.from_far = lambda k: got(at.s_far, 1, k)
            self.from_diag = lambda k: got(at.s_diag, 2, k)
            other = lambda k: row_full.at[1 - at.x, rpart(k)]
            self.from_side = lambda k: remote(other(k), other(k), rsend.at[0, k], rrecv.at[1 - at.x, k], at.side)

        def step(self, i, last):
            at = self.at
            upward, downward = (at.z >= at.s) & (at.z < 3), (at.z <= at.s) & (at.z > 0)
            side, up, down = self.rows

            @pl.when(i == 0)
            def _():
                at.greet()
                self.keep.start()
                each_slice(lambda k: self.to_sib(k).start())

                @pl.when(at.z == at.s)
                def _():
                    self.rkeep.start()
                    self.rkeep.wait()

            k = i - 1

            @pl.when((k >= 0) & (k < SLICES))
            def _():
                self.to_far(k).start()

            @pl.when((k >= SLICES) & (k < 2 * SLICES))
            def _():
                self.from_far(k - SLICES).wait_recv()
                self.pass_on(k - SLICES).start()

            far_away = jnp.where(at.z > at.s, at.z - at.s, at.s - at.z)
            r = i - 1 - 2 * far_away

            @pl.when((r >= 0) & (r < SLICES))
            def _():
                @pl.when(at.z != at.s)
                def _():
                    side(r).wait_recv()

                side(r).start()

                @pl.when(upward)
                def _():
                    up(r).start()

                @pl.when(downward)
                def _():
                    down(r).start()

            @pl.when(i == last)
            def _():
                self.keep.wait()

                def finish(k):
                    self.to_sib(k).wait_send()
                    self.to_far(k).wait_send()
                    self.pass_on(k).wait_send()
                    self.from_sib(k).wait_recv()
                    self.from_diag(k).wait_recv()
                    side(k).wait_send()
                    self.from_side(k).wait_recv()

                    @pl.when(upward)
                    def _():
                        up(k).wait_send()

                    @pl.when(downward)
                    def _():
                        down(k).wait_send()

                each_slice(finish)

    return Traffic


def add_into(dst, src, rows):
    def body(i, _):
        part = pl.ds(pl.multiple_of(i * 16, 16), 16)
        dst[part, :] = (dst[part, :].astype(f32) + src[part, :].astype(f32)).astype(bf16)
        return 0

    lax.fori_loop(0, rows // 16, body, 0)


def far_first(at, i):
    inner = (at.z == 1) | (at.z == 2)
    i = jnp.where(inner & (i >= 2), 5 - i, i)
    return jnp.where(at.z < 2, 3 - i, i)


class ReduceShards:
    def __init__(self, at, partial, cuts, acc, from_side, from_down, from_up, sems):
        self.at, self.partial, self.cuts, self.acc = at, partial, cuts, acc
        self.from_side, self.from_down, self.from_up = from_side, from_down, from_up
        self.send, self.recv_side, self.recv_down, self.recv_up = sems
        self.rows = acc.shape[1] // cuts

    def unit(self, j):
        if isinstance(j, int):
            shard, cut = j // self.cuts, j % self.cuts
        else:
            shard, cut = lax.div(j, self.cuts), lax.rem(j, self.cuts)
        zp = far_first(self.at, shard)
        return zp, zp * self.cuts + cut, pl.ds(pl.multiple_of(cut * self.rows, self.rows), self.rows)

    def side_copy(self, j):
        at = self.at
        zp, n, part = self.unit(j)
        return remote(
            self.partial(zp).at[part], self.from_side.at[zp, part],
            self.send.at[0, n], self.recv_side.at[n], at.side,
        )

    def up_copy(self, j):
        zp, n, part = self.unit(j)
        return remote(
            self.acc.at[zp, part], self.from_down.at[zp, part], self.send.at[1, n], self.recv_down.at[n], self.at.up
        )

    def down_copy(self, j):
        zp, n, part = self.unit(j)
        return remote(
            self.acc.at[zp, part], self.from_up.at[zp, part], self.send.at[2, n], self.recv_up.at[n], self.at.down
        )

    def start(self):
        self.side_copy(0).start()
        self.side_copy(1).start()

    def step(self, j):
        at = self.at
        zp, _, part = self.unit(j)
        self.side_copy(j).wait()
        acc = self.acc.at[zp, part]
        add_into(acc, self.from_side.at[zp, part], self.rows)

        @pl.when((at.z > 0) & (zp >= at.z))
        def _():
            self.up_copy(j).wait_recv()
            add_into(acc, self.from_down.at[zp, part], self.rows)

        @pl.when((at.z < 3) & (zp <= at.z))
        def _():
            self.down_copy(j).wait_recv()
            add_into(acc, self.from_up.at[zp, part], self.rows)

        @pl.when(zp > at.z)
        def _():
            self.up_copy(j).start()

        @pl.when(zp < at.z)
        def _():
            self.down_copy(j).start()

    def end(self):
        at = self.at
        for j in range(4 * self.cuts):
            zp = self.unit(j)[0]

            @pl.when(zp > at.z)
            def _():
                self.up_copy(j).wait_send()

            @pl.when(zp < at.z)
            def _():
                self.down_copy(j).wait_send()


def backward_traffic(layer, rows, gate):
    piece, cols = layer.shape[1:]
    rrows = rows.shape[1]
    grows, gcols = gate.shape[1:]

    class Traffic:
        inputs = (layer, rows, gate)
        outputs = (
            jax.ShapeDtypeStruct((piece, cols), f32),
            jax.ShapeDtypeStruct((rrows, cols), bf16),
            jax.ShapeDtypeStruct((grows, gcols), bf16),
        )
        scratch = (
            *[pltpu.VMEM((piece, cols), bf16)] * 5,
            pltpu.VMEM((piece, cols), f32),
            *[pltpu.VMEM((rrows, cols), bf16)] * 4,
            dma(3, SLICES),
            dma(3, SLICES),
            dma(3),
            dma(3, SLICES),
            dma(3, SLICES),
            dma(2),
            dma(2, SLICES),
            dma(2, SLICES),
            *[pltpu.VMEM((4, grows, gcols), bf16)] * 4,
            dma(3, 8),
            dma(8),
            dma(8),
            dma(8),
            dma(5),
        )
        collective_id = 3

        def __init__(
            self, layer, rows, gate, out, rows_out, gate_out,
            own_v, far_v, sib_v, pass_v, got_v, sum_v, acc, side_v, low_v, high_v,
            send, recv, local, rsend, rrecv, rlocal, fsend, frecv,
            gacc, gside, glow, ghigh, gsend, grecv_side, grecv_low, grecv_high, glocal,
        ):
            self.at = at = Place()
            cut, rcut = piece // SLICES, rrows // SLICES
            part = lambda k: pl.ds(pl.multiple_of(k * cut, cut), cut)
            rpart = lambda k: pl.ds(pl.multiple_of(k * rcut, rcut), rcut)
            self.own, self.sib, self.passed, self.got, self.sum = own_v, sib_v, pass_v, got_v, sum_v
            self.part, self.rpart, self.cut, self.rcut = part, rpart, cut, rcut
            self.far_v, self.acc, self.side_v, self.low_v, self.high_v = far_v, acc, side_v, low_v, high_v
            self.load_far = pltpu.make_async_copy(layer.at[at.s_far], far_v, local.at[0])
            self.load_own = pltpu.make_async_copy(layer.at[at.s], own_v, local.at[1])
            self.store = pltpu.make_async_copy(sum_v, out, local.at[2])
            self.to_pass = lambda k: remote(
                layer.at[at.s_diag, part(k)], pass_v.at[part(k)], send.at[0, k], recv.at[0, k], at.sib
            )
            self.to_sib = lambda k: remote(
                layer.at[at.s_sib, part(k)], sib_v.at[part(k)], send.at[1, k], recv.at[1, k], at.sib
            )
            self.to_far = lambda k: remote(
                far_v.at[part(k)], got_v.at[part(k)], send.at[2, k], recv.at[2, k], at.far
            )
            self.load_acc = pltpu.make_async_copy(rows.at[at.x], acc, rlocal.at[0])
            self.store_acc = pltpu.make_async_copy(acc, rows_out, rlocal.at[1])
            spread = lambda k, n, device: remote(
                acc.at[rpart(k)], rows_out.at[rpart(k)], fsend.at[n, k], frecv.at[n, k], device
            )
            self.spread_far = lambda k: spread(k, 0, at.far)
            self.spread_sib = lambda k: spread(k, 1, at.sib)
            self.spread_on = lambda k: remote(
                rows_out.at[rpart(k)], rows_out.at[rpart(k)], fsend.at[1, k], frecv.at[1, k], at.sib
            )
            self.gates = ReduceShards(
                at, lambda zp: gate.at[2 * zp + 1 - at.x], 2, gacc, gside, glow, ghigh,
                (gsend, grecv_side, grecv_low, grecv_high),
            )
            self.load_gate = [
                pltpu.make_async_copy(gate.at[2 * zp + at.x], gacc.at[zp], glocal.at[zp]) for zp in range(4)
            ]
            self.store_gate = pltpu.make_async_copy(gacc.at[at.z], gate_out, glocal.at[4])
            self.to_side = lambda k: remote(
                rows.at[1 - at.x, rpart(k)], side_v.at[rpart(k)], rsend.at[0, k], rrecv.at[0, k], at.side
            )
            self.to_up = lambda k: remote(
                acc.at[rpart(k)], low_v.at[rpart(k)], rsend.at[1, k], rrecv.at[1, k], at.up
            )
            self.to_down = lambda k: remote(
                acc.at[rpart(k)], high_v.at[rpart(k)], rsend.at[2, k], rrecv.at[2, k], at.down
            )

        def step(self, i, last):
            at = self.at

            @pl.when(i == 0)
            def _():
                at.greet()
                self.load_far.start()
                self.load_own.start()
                self.load_acc.start()
                for copy in self.load_gate:
                    copy.start()
                each_slice(lambda k: self.to_pass(k).start())
                each_slice(lambda k: self.to_sib(k).start())

            @pl.when(i < SLICES)
            def _():
                self.to_side(i).start()

            @pl.when(i == 1)
            def _():
                self.load_far.wait()
                self.load_own.wait()
                self.load_acc.wait()
                for copy in self.load_gate:
                    copy.wait()

            k = i - 1

            @pl.when((k >= 0) & (k < SLICES))
            def _():
                self.to_pass(k).wait_recv()
                add_into(self.far_v.at[self.part(k)], self.passed.at[self.part(k)], self.cut)
                self.to_far(k).start()

            m = i - SLICES

            @pl.when((m >= 0) & (m < SLICES))
            def _():
                self.to_sib(m).wait_recv()
                self.to_far(m).wait_recv()
                p = self.part(m)
                self.sum[p, :] = (
                    self.own[p, :].astype(f32) + self.sib[p, :].astype(f32) + self.got[p, :].astype(f32)
                )

            ends = jnp.where(at.z > 3 - at.z, at.z, 3 - at.z)
            chain = jnp.where(at.z < at.s, at.z, jnp.where(at.z > at.s, 3 - at.z, ends))
            r = i - 2 - 2 * chain

            @pl.when((r >= 0) & (r < SLICES))
            def _():
                acc = self.acc.at[self.rpart(r)]
                self.to_side(r).wait_recv()
                add_into(acc, self.side_v.at[self.rpart(r)], self.rcut)

                @pl.when((at.z <= at.s) & (at.z > 0))
                def _():
                    self.to_up(r).wait_recv()
                    add_into(acc, self.low_v.at[self.rpart(r)], self.rcut)

                @pl.when((at.z >= at.s) & (at.z < 3))
                def _():
                    self.to_down(r).wait_recv()
                    add_into(acc, self.high_v.at[self.rpart(r)], self.rcut)

                @pl.when(at.z < at.s)
                def _():
                    self.to_up(r).start()

                @pl.when(at.z > at.s)
                def _():
                    self.to_down(r).start()

                @pl.when(at.z == at.s)
                def _():
                    self.spread_far(r).start()
                    self.spread_sib(r).start()

            g = i - 6

            @pl.when((g >= 0) & (g < 8))
            def _():
                self.gates.side_copy(g).start()

            inner = jnp.where((at.z == 1) | (at.z == 2), 1, 0)
            g = i - 8 - inner

            @pl.when((g >= 0) & (g < 8))
            def _():
                self.gates.step(g)

            @pl.when(i == last)
            def _():
                @pl.when(inner == 1)
                def _():
                    self.gates.step(jnp.int32(7))

                self.store.start()
                self.store_gate.start()

                @pl.when(at.s == at.z)
                def _():
                    self.store_acc.start()

                def forward(k):
                    @pl.when(at.s_far == at.z)
                    def _():
                        self.spread_far(k).wait_recv()
                        self.spread_on(k).start()

                each_slice(forward)

                def finish(k):
                    @pl.when(at.s == at.z)
                    def _():
                        self.spread_far(k).wait_send()
                        self.spread_sib(k).wait_send()

                    @pl.when(at.s_far == at.z)
                    def _():
                        self.spread_on(k).wait_send()

                    @pl.when((at.s_sib == at.z) | (at.s_diag == at.z))
                    def _():
                        self.spread_on(k).wait_recv()

                    self.to_pass(k).wait_send()
                    self.to_sib(k).wait_send()
                    self.to_far(k).wait_send()
                    self.to_side(k).wait_send()

                    @pl.when(at.z < at.s)
                    def _():
                        self.to_up(k).wait_send()

                    @pl.when(at.z > at.s)
                    def _():
                        self.to_down(k).wait_send()

                each_slice(finish)
                self.gates.end()
                self.store.wait()
                self.store_gate.wait()

                @pl.when(at.s == at.z)
                def _():
                    self.store_acc.wait()

    return Traffic


def small_start(at, small, got, sems):
    send, recv = sems
    for k in range(1, 8):
        peer = (lax.rem(at.w + k, 8), at.s)
        remote(small, got.at[k], send.at[k], recv.at[k], peer).start()


def small_pass(at, small, got, total, full, sems, more):
    send, recv = sems
    send2, recv2, local = more
    value = small[...]
    for k in range(1, 8):
        remote(small, got.at[k], send.at[k], recv.at[k], at.side).wait_recv()
        value = value + got[k]
    total[...] = value
    pltpu.make_async_copy(total, full.at[at.s], local).start()
    for k, s in enumerate((at.s_sib, at.s_far, at.s_diag)):
        remote(total, full.at[at.s], send2.at[k], recv2.at[k], (at.w, s)).start()


def small_end(at, small, got, total, full, sems, more):
    send, recv = sems
    send2, recv2, local = more
    pltpu.make_async_copy(total, full.at[at.s], local).wait()
    for k in range(1, 8):
        remote(small, got.at[k], send.at[k], recv.at[k], at.side).wait_send()
    for k, s in enumerate((at.s_sib, at.s_far, at.s_diag)):
        remote(total, full.at[at.s], send2.at[k], recv2.at[k], (at.w, s)).wait_send()
        remote(total, full.at[s], send2.at[k], recv2.at[k], (at.w, s)).wait_recv()


def last_kernel(hid, d_gate, d_u, d_dt, w_main, w_com, gate_sum, small,
                back_sum, in_sum, sums_out,
                hid_v, dg_v, du_v, dt_v, wm_v, wc_v,
                b_diag, b_sib, b_far, b_own, from_sib, pass_sib, from_far,
                part_v, mside, mlow, mhigh, macc, mown, csib, cown, cacc, cside, clow, chigh, cfar, csum,
                sgot, stotal, sfull, *sems):
    at = Place()
    sems = list(sems)
    take = lambda n: [sems.pop(0) for _ in range(n)]
    load, bsem, msem, csem, cx, ssem, smore, asem, gsem = (
        take(6), take(2), take(4), take(4), take(7), take(2), take(3), take(3), take(3)
    )
    piece = hid_v.shape[0] // 4
    shard = hid_v.shape[1] // 8
    wide = dg_v.shape[1]
    half = shard // 2
    mine = pl.ds(pl.multiple_of(at.c * half, half), half)
    other = pl.ds(pl.multiple_of((1 - at.c) * half, half), half)
    at.greet(everyone=True)

    order = (at.s_diag, at.s_far, at.s_sib, at.s)
    rows_of = lambda s: pl.ds(pl.multiple_of(s * piece, piece), piece)
    weights = [
        pltpu.make_async_copy(w_main, wm_v, load[0].at[0]),
        pltpu.make_async_copy(w_com, wc_v, load[0].at[1]),
    ]
    loads = []
    for k, s in enumerate(order):
        r = rows_of(s)
        loads.append(
            [
                pltpu.make_async_copy(d_gate.at[r], dg_v.at[r], load[1].at[k]),
                pltpu.make_async_copy(d_u.at[r], du_v.at[r], load[2].at[k]),
                pltpu.make_async_copy(d_dt.at[r], dt_v.at[r], load[3].at[k]),
            ]
        )
    hid_load = pltpu.make_async_copy(hid, hid_v, load[4])
    for copy in loads[0] + weights + loads[1] + loads[2] + loads[3] + [hid_load]:
        copy.start()
    gate_slot = lambda s: in_sum.at[:, pl.ds(pl.multiple_of(s * wide, 128), wide)]
    x_slot = lambda s: in_sum.at[:, pl.ds(pl.multiple_of(E + s * wide, 128), wide)]
    gather_pieces_start(at, gate_sum, gate_slot, gsem)
    small_start(at, small, sgot, ssem)

    send, recv = bsem
    rows = piece // PARTS
    parts = [pl.ds(k * rows, rows) for k in range(PARTS)]
    to_pass = [remote(b_diag.at[p], pass_sib.at[p], send.at[0, k], recv.at[0, k], at.sib) for k, p in enumerate(parts)]
    to_sib = [remote(b_sib.at[p], from_sib.at[p], send.at[1, k], recv.at[1, k], at.sib) for k, p in enumerate(parts)]
    to_far = [remote(b_far.at[p], from_far.at[p], send.at[2, k], recv.at[2, k], at.far) for k, p in enumerate(parts)]

    def back_piece(s, out):
        base = s * piece

        def body(t, _):
            tile = pl.ds(pl.multiple_of(base + t * 256, 256), 256)
            place = pl.ds(pl.multiple_of(t * 256, 256), 256)
            for n in range(hid_v.shape[1] // 256):
                col = slice(256 * n, 256 * n + 256)
                total = dot_nt(dg_v[tile, :], wm_v[col, 0:wide])
                total = total + dot_nt(du_v[tile, 0:wide], wm_v[col, wide : 2 * wide])
                total = total + dot_nt(du_v[tile, wide : wide + 256], wc_v[col, 0:256])
                total = total + dot_nt(dt_v[tile, :], wc_v[col, 256:384])
                out[place, col] = total.astype(bf16)
            return 0

        lax.fori_loop(0, piece // 256, body, 0)

    big = ReduceShards(at, lambda zp: part_v.at[zp, 1 - at.x, :, pl.ds(0, wide)], 1, macc, mside, mlow, mhigh, msem)
    few = ReduceShards(at, lambda zp: cown.at[zp, 1 - at.x], 1, cacc, cside, clow, chigh, csem)
    com_cols = pl.ds(wide, 384)
    com_to_sib = lambda zp: remote(
        part_v.at[zp, :, other, com_cols], csib.at[zp], cx[0].at[zp], cx[1].at[zp], at.sib
    )

    def shard_pair(i):
        zp = far_first(at, i)
        lanes = pl.ds(pl.multiple_of(zp * 2 * shard, 128), 2 * shard)
        left = hid_v[:, lanes]
        tn = lambda right: lax.dot_general(left, right, (((0,), (0,)), ((), ())), preferred_element_type=f32)
        for n in range((wide + 256) // 256):
            col = slice(256 * n, 256 * n + 256)
            got = tn(du_v[:, col]).astype(bf16)
            part_v[zp, 0, :, col] = got[0:shard]
            part_v[zp, 1, :, col] = got[shard : 2 * shard]
        col = slice(wide + 256, wide + 384)
        got = tn(dt_v[...]).astype(bf16)
        part_v[zp, 0, :, col] = got[0:shard]
        part_v[zp, 1, :, col] = got[shard : 2 * shard]
        macc[zp] = part_v[zp, at.x, :, 0:wide]
        big.side_copy(i).start()
        com_to_sib(zp).start()

    def com_pair(i):
        zp = far_first(at, i)
        com_to_sib(zp).wait_recv()
        for x in range(2):
            cown[zp, x] = part_v[zp, x, mine, com_cols]
            add_into(cown.at[zp, x], csib.at[zp, x], half)
        cacc[zp] = cown[zp, at.x]
        few.side_copy(i).start()

    for copy in loads[0] + weights:
        copy.wait()
    back_piece(at.s_diag, b_diag)
    for copy in to_pass:
        copy.start()
    for copy in loads[1] + loads[2] + loads[3] + [hid_load]:
        copy.wait()
    shard_pair(0)
    back_piece(at.s_far, b_far)
    for k, p in enumerate(parts):
        to_pass[k].wait_recv()
        add_into(b_far.at[p], pass_sib.at[p], rows)
        to_far[k].start()
    com_pair(0)
    shard_pair(1)
    shard_pair(2)
    com_pair(1)
    big.step(0)
    few.step(0)
    gather_pieces_pass(at, gate_sum, gate_slot, gsem)
    shard_pair(3)
    com_pair(2)
    back_piece(at.s_sib, b_sib)
    for copy in to_sib:
        copy.start()
    com_pair(3)
    big.step(1)
    few.step(1)
    back_piece(at.s, b_own)
    big.step(2)
    few.step(2)
    small_pass(at, small, sgot, stotal, sfull, ssem, smore)
    big.step(3)
    few.step(3)
    mown[...] = macc[at.z]
    gather_pieces_start(at, mown, x_slot, asem)
    csum[...] = cacc[at.z]
    far_copy = remote(csum, cfar, cx[2], cx[3], at.far)
    far_copy.start()
    for k, p in enumerate(parts):
        to_sib[k].wait_recv()
        to_far[k].wait_recv()

        def body(i, _):
            r = pl.ds(pl.multiple_of(k * rows + i * 16, 16), 16)
            back_sum[r, :] = b_own[r, :].astype(f32) + from_sib[r, :].astype(f32) + from_far[r, :].astype(f32)
            return 0

        lax.fori_loop(0, rows // 16, body, 0)
    far_copy.wait()
    add_into(csum, cfar, half)
    com_out = in_sum.at[mine, pl.ds(2 * E, 384)]
    com_copy = remote(csum, com_out, cx[4], cx[5], at.sib)
    com_copy.start()
    keep_copy = pltpu.make_async_copy(csum, com_out, cx[6])
    keep_copy.start()
    gather_pieces_pass(at, mown, x_slot, asem)
    small_end(at, small, sgot, stotal, sfull, ssem, smore)
    sums_out[...] = jnp.zeros_like(sums_out)
    bc, heads = jnp.zeros((8, 256), f32), jnp.zeros((8, 128), f32)
    for s in range(4):
        sums_out[:, wide * s : wide * s + wide] = sfull[s, :, 0:wide]
        bc = bc + sfull[s, :, wide : wide + 256]
        shift = (wide // P_SIZE) * s
        own = sfull[s, :, 0:128]
        heads = heads + (pltpu.roll(own, shift, 1) if shift else own)
    sums_out[:, E : E + 256] = bc
    sums_out[:, E + 256 : E + 384] = heads
    for copy in to_pass + to_sib + to_far:
        copy.wait_send()
    for zp in range(4):
        com_to_sib(zp).wait_send()
    big.end()
    few.end()
    gather_pieces_end(at, gate_sum, gate_slot, gsem)
    gather_pieces_end(at, mown, x_slot, asem)
    keep_copy.wait()
    com_copy.wait_send()
    got = in_sum.at[other, pl.ds(2 * E, 384)]
    remote(csum, got, cx[4], cx[5], at.sib).wait_recv()


def finish_last(hid, d_gate, d_u, d_dt, w_main, w_com, gate_sum, small):
    length, depth = hid.shape
    piece, shard, half = length // 4, depth // 8, depth // 16
    wide = d_gate.shape[1]
    vm = pltpu.VMEM
    shards4 = [dma(3, 4), dma(4), dma(4), dma(4)]
    return pl.pallas_call(
        last_kernel,
        in_specs=[pl.BlockSpec(memory_space=ANY)] * 7 + [pl.BlockSpec(memory_space=pltpu.VMEM)],
        out_specs=[
            pl.BlockSpec(memory_space=pltpu.VMEM),
            pl.BlockSpec(memory_space=ANY),
            pl.BlockSpec(memory_space=pltpu.VMEM),
        ],
        out_shape=[
            jax.ShapeDtypeStruct((piece, depth), f32),
            jax.ShapeDtypeStruct((shard, 2 * E + 384), bf16),
            jax.ShapeDtypeStruct((8, E + 384), f32),
        ],
        scratch_shapes=[vm(v.shape, bf16) for v in (hid, d_gate, d_u, d_dt, w_main, w_com)]
        + [vm((piece, depth), bf16)] * 7
        + [vm((4, 2, shard, wide + 384), bf16)]
        + [vm((4, shard, wide), bf16)] * 4
        + [vm((shard, wide), bf16)]
        + [vm((4, 2, half, 384), bf16)] * 2
        + [vm((4, half, 384), bf16)] * 4
        + [vm((half, 384), bf16)] * 2
        + [vm((8,) + small.shape, f32), vm(small.shape, f32), vm((4,) + small.shape, f32)]
        + [dma(2), dma(4), dma(4), dma(4), dma(), dma()]
        + [dma(3, PARTS), dma(3, PARTS)]
        + shards4
        + shards4
        + [dma(4), dma(4), dma(), dma(), dma(), dma(), dma()]
        + [dma(8), dma(8)]
        + [dma(3), dma(3), dma()]
        + [dma(3, PARTS), dma(3, PARTS), dma()]
        + [dma(3, PARTS), dma(3, PARTS), dma()],
        compiler_params=pltpu.CompilerParams(
            collective_id=4, has_side_effects=True, vmem_limit_bytes=60 * 2**20
        ),
        name="finish_last",
    )(hid, d_gate, d_u, d_dt, w_main, w_com, gate_sum, small)


def over_rows(left, right):
    return lax.dot_general(
        left, right, (((0,), (0,)), ((), ())), preferred_element_type=jnp.float32
    )


def gather_plain(hid, main, com):
    hid_all = lax.all_gather(hid, "seq", axis=0)
    main_all = lax.all_gather(main, "wshard", axis=0)
    return hid_all, main_all, lax.all_gather(com, "wshard", axis=0)


def gather_more_plain(cot, rows, wide):
    cot_all = lax.all_gather(cot, "seq", axis=0)
    cols = lax.all_to_all(rows, "wshard", split_axis=1, concat_axis=0, tiled=True)
    own = lax.dynamic_slice_in_dim(cols, lax.axis_index("seq") * wide, wide, 0)
    return cot_all, lax.all_gather(own, "wshard", axis=1, tiled=True)


def reduce_scattered(v, axis):
    return lax.psum_scatter(v, axis, scatter_dimension=0, tiled=False)


def reduce_first_plain(layer, rows, gate):
    layer_sum = reduce_scattered(layer, "seq").astype(f32)
    rows = rows.reshape(-1, rows.shape[-1])
    part = lax.psum_scatter(rows, "wshard", scatter_dimension=1, tiled=True)
    part = lax.all_gather(part, "seq", axis=0, tiled=True)
    part = lax.all_to_all(part, "wshard", split_axis=0, concat_axis=1, tiled=True)
    return layer_sum, part, reduce_scattered(gate, "wshard")


def finish_plain(hid, d_gate, d_u, d_dt, w_main, w_com, gate_sum, small):
    groups, owners = lax.axis_size("seq"), lax.axis_size("wshard")
    wide = d_gate.shape[1]
    rest = jnp.concatenate([d_u, d_dt], axis=1)
    nt = lambda p, q: lax.dot_general(p, q, (((1,), (1,)), ((), ())), preferred_element_type=f32)
    back = nt(d_gate, w_main[:, :wide]) + nt(rest, jnp.concatenate([w_main[:, wide:], w_com], axis=1))
    back_sum = reduce_scattered(back.astype(bf16).reshape(groups, -1, D), "seq").astype(f32)
    part = reduce_scattered(over_rows(hid, rest).astype(bf16).reshape(owners, -1, rest.shape[1]), "wshard")
    part = lax.all_gather(jnp.concatenate([gate_sum, part], axis=1), "seq", axis=0)
    in_sum = jnp.concatenate(
        [part[i, :, :wide] for i in range(groups)]
        + [part[i, :, wide : 2 * wide] for i in range(groups)]
        + [jnp.sum(part[:, :, 2 * wide :].astype(f32), axis=0).astype(bf16)],
        axis=1,
    )
    full = lax.all_gather(lax.psum(small, "wshard"), "seq", axis=0)
    turned = [jnp.roll(full[i, :, :128], i * (wide // P_SIZE), axis=1) for i in range(groups)]
    sums = jnp.concatenate(
        [full[i, :, :wide] for i in range(groups)] + [jnp.sum(full[:, :, wide:], axis=0), sum(turned)], axis=1
    )
    return back_sum, in_sum, sums


def shards(
    hidden,
    segments,
    norm_gain,
    in_weight,
    conv_weight,
    conv_bias,
    step_bias,
    decay_log,
    skip_scale,
    gate_gain,
    out_weight,
    cotangent,
):
    group = lax.axis_index("seq")
    groups, owners = lax.axis_size("seq"), lax.axis_size("wshard")
    direct = (groups, owners) == (4, 8)
    heads = H // groups
    wide = heads * P_SIZE
    length = segments.shape[1]
    hidden_own, cot_own = hidden[0], cotangent[0]
    in_gain = norm_gain.astype(f32)[:, None]
    in_scaled = (in_weight.astype(f32) * in_gain).astype(bf16)
    main = jnp.concatenate(
        [
            lax.dynamic_slice_in_dim(in_scaled, group * wide, wide, 1),
            lax.dynamic_slice_in_dim(in_scaled, E + group * wide, wide, 1),
        ],
        axis=1,
    )
    com = jnp.pad(in_scaled[:, 2 * E :], ((0, 0), (0, 128 - H)))
    out_gain = gate_gain.astype(f32)[:, None]
    out_scaled = (out_weight.astype(f32) * out_gain).astype(bf16)
    gather = gather_first if direct else gather_plain
    hidden_all, w_main, w_com = gather(hidden_own, main, com)
    hidden_all = hidden_all.reshape(length, D)
    w_main, w_com = w_main.reshape(D, 2 * wide), w_com.reshape(D, -1)

    seg = segments[0]
    seg_col = jnp.pad(seg, (8, 8), constant_values=-1)[:, None]
    segr = seg.reshape(length // Q, 1, Q)
    par = jnp.pad(jnp.stack([step_bias, decay_log]), ((0, 6), (0, 128 - H)))
    skip = jnp.repeat(skip_scale, P_SIZE)[None]
    facts = (seg_col, segr, conv_weight, conv_bias[None], par, skip)
    beside, more = (forward_traffic(cot_own, out_scaled), (cot_own, out_scaled)) if direct else (NoTraffic, ())
    u, dt, gate, scale, mixed, save, *got = mixer_fwd(beside, more, hidden_all, w_main, w_com, *facts)
    cot_all, w_out = got if direct else gather_more_plain(cot_own, out_scaled, wide)
    cot_all, w_out = cot_all.reshape(length, D), w_out.reshape(wide, D)

    mixed_wide = mixed.astype(f32)
    sg = jax.nn.sigmoid(gate)
    silu = gate * sg
    g = mixed_wide * silu
    g_low = g.astype(bf16)
    a = lax.dot_general(cot_all, w_out, (((1,), (1,)), ((), ())), preferred_element_type=f32)
    sums = lax.psum(jnp.stack([jnp.sum(g * g, axis=1), jnp.sum(a * g, axis=1)]), "seq")
    r = lax.rsqrt(sums[0] / E + eps)[:, None]
    pull = (r * r * r) * (sums[1] / E)[:, None]
    d_g = r * a - g * pull
    d_mixed = (d_g * silu).astype(bf16)
    d_gate = (d_g * mixed_wide * (sg * (1.0 + gate * (1.0 - sg))) * scale).astype(bf16)
    layer_part = (jnp.dot(g_low, w_out, preferred_element_type=f32) * r).astype(bf16)
    cot_r = (cot_all.astype(f32) * r).astype(bf16)
    out_part = over_rows(g_low, cot_r).astype(bf16)

    gate_part = over_rows(hidden_all, d_gate).astype(bf16)

    layer_part, out_part = layer_part.reshape(groups, -1, D), out_part.reshape(2, -1, D)
    gate_part = gate_part.reshape(owners, -1, wide)
    more = (layer_part, out_part, gate_part) if direct else ()
    beside = backward_traffic(*more) if direct else NoTraffic
    du, ddt, small, *got = mixer_bwd(beside, more, u, dt, scale, *facts, save, d_mixed)
    layer_sum, out_sum, gate_sum = got if direct else reduce_first_plain(*(layer_part, out_part, gate_part))
    finish = finish_last if direct else finish_plain
    back_sum, in_sum, sums = finish(hidden_all, d_gate, du, ddt, w_main, w_com, gate_sum, small)

    own_wide = hidden_own.astype(f32)
    layer_output = own_wide + layer_sum
    own_scale = lax.rsqrt(jnp.mean(own_wide * own_wide, axis=-1, keepdims=True) + eps)
    hidden_grad = (
        cot_own.astype(f32)
        + back_sum
        - own_wide * (own_scale * own_scale) * jnp.mean(back_sum * own_wide, axis=-1, keepdims=True)
    )
    in_sum = in_sum[:, : 2 * E + 2 * N + H].astype(f32)
    in_weight_grad = in_sum * in_gain
    norm_gain_grad = jnp.sum(in_sum * in_weight.astype(f32), axis=1)
    out_sum = out_sum.astype(f32)
    out_weight_grad = out_sum * out_gain
    gate_gain_grad = jnp.sum(out_sum * out_weight.astype(f32), axis=1)
    chan, per_head = sums[:, : E + 2 * N], sums[:, E + 2 * N : E + 2 * N + H]
    return (
        layer_output[None],
        hidden_grad[None],
        norm_gain_grad,
        in_weight_grad,
        chan[:4],
        chan[4],
        per_head[5],
        per_head[6],
        per_head[7],
        gate_gain_grad,
        out_weight_grad,
    )


def solution(mesh):
    in_specs = (
        P("wshard", "seq", None),
        P("wshard", None),
        P("wshard"),
        P("wshard", None),
        P(),
        P(),
        P(),
        P(),
        P(),
        P("wshard"),
        P("wshard", None),
        P("wshard", "seq", None),
    )
    out_specs = (
        P("wshard", "seq", None),
        P("wshard", "seq", None),
        P("wshard"),
        P("wshard", None),
        P(),
        P(),
        P(),
        P(),
        P(),
        P("wshard"),
        P("wshard", None),
    )
    return jax.shard_map(shards, mesh=mesh, in_specs=in_specs, out_specs=out_specs, check_vma=False)
```

time: 456 us -> 370 us (0.81)
  the two profiles are of different devices: /device:TPU:15 before, /device:TPU:0 now
where the time goes in v3:
time: 370 us; the launch traced here: 364 us
  Pallas kernels  274 us (74%)
  matrix products  42 us (11%)
  other arithmetic  25.6 us (7%)
  blocking collectives  10.6 us (3%)
  local copies, waits for them, and re-layouts  10.5 us (3%)
    pallas_call x1, Pallas kernels, gather_first(): pl.pallas_call(gather_kernel, in_specs=[pl.BlockSpec(memory_space=ANY)] *...  77.1 us
    pallas_call x1, Pallas kernels, mixer_bwd(): pl.pallas_call(functools.partial(bwd_kernel, traffic), grid=(n,), in_spec...  71.8 us
    pallas_call x1, Pallas kernels, finish_last(): pl.pallas_call(last_kernel, in_specs=[pl.BlockSpec(memory_space=ANY)] * 7...  68.3 us
    pallas_call x1, Pallas kernels, mixer_fwd(): pl.pallas_call(functools.partial(fwd_kernel, traffic), grid=(n + 1,), in_...  56.7 us
    dot_general x2, matrix products, over_rows(): lax.dot_general(left, right, (((0,), (0,)), ((), ())), preferred_element_...  19.7 us
    dot_general x1, matrix products, shards(): lax.dot_general(cot_all, w_out, (((1,), (1,)), ((), ())), preferred_eleme...  12.3 us
    psum x1, blocking collectives, shards(): lax.psum(jnp.stack([jnp.sum(g * g, axis=1), jnp.sum(a * g, axis=1)]), 'seq')  10.6 us
    dot_general x1, matrix products, shards(): jnp.dot(g_low, w_out, preferred_element_type=f32) * r  10 us

profile of v3, /device:TPU:0, one launch (start us, length us, event | category | flops | bytes accessed | tf_op | source)
XLA Modules:
  0.0 364.1 jit_solution(18101431292035173404)
XLA Ops:
  2.7 0.8 pad.13
  3.4 0.7 broadcast_in_dim.22.bias_ref
  4.2 0.7 broadcast_in_dim.23
  5.3 1.7 fusion.16.rest_1_
  7.9 0.9 pad_maximum_fusion.main
  9.4 77.1 %gather_first.1 = (bf16[4,512,1536]{2,1,0:T(8,128)(2,1)}, bf16[8,192,1536]{2,1,0:T(8,128)(2,1)}, bf16[8,192,384]{2,1,0:T(8,128)(2,1)}) custom-call(bf16[512,1536]{1,0:T(8,128)(2,1)} %bitcast.50, bf16[192,1536]{1,0:T(8,128)(2,1)} %pad_maximum_fusion.main, bf16[192,384]{1,0:T(8,128)(2,1)} %pad.12.com), custom_call_target="tpu_custom_call" | custom-call | tf_op jit(solution)/shard_map/gather_first/pallas_call | solution.py:669
  86.6 1.3 copy-done
  87.9 56.7 %mixer_forward.1 = (bf16[2048,1024]{1,0:T(8,128)(2,1)}, bf16[2048,128]{1,0:T(8,128)(2,1)S(1)}, f32[2048,768]{1,0:T(8,128)}, f32[2048,1]{1,0:T(8,128)S(1)}, bf16[...) custom-call(bf16[2048,1536]{1,0:T(8,128)(2,1)} %bitcast.43, ...), custom_call_target="tpu_custom_call" | custom-call | tf_op jit(solution)/shard_map/mixer_forward/pallas_call | solution.py:198
  144.6 0.8 copy-done.1
  145.7 12.3 %multiply_reduce_fusion.1 = (f32[2048]{0:T(1024)S(1)}, f32[2048]{0:T(1024)S(1)}, f32[2048,768]{1,0:T(8,128)}) fusion(bf16[2048,768]{1,0:T(8,128)(2,1)} %get-tuple-element.38, f32[2048,768]{1,0:T(8,128)} %get-tuple-element.39, bf16[2048,1536]{1,0:T(8,128)(2,1)} %bitcast.64, bf16[768,1536]{1,0:T(8,128)(2,1)} %bitcast.66), kind=kOutput, calls=%fused_computation.12 | convolution fusion | flops 4847562752 | bytes 24395776 | tf_op jit(solution)/shard_map/dot_general | solution.py:1496
  158.1 10.6 %psum.7 = f32[2,2048]{1,0:T(2,128)S(1)} all-reduce(f32[2,2048]{1,0:T(2,128)S(1)} %pad_maximum_fusion.1), channel_id=1, replica_groups=mesh['wshard'=8,'seq'=4] {'seq'}, use_global_device_ids=true, to_apply=%region_2.3 | all-reduce | flops 4096 | bytes 32768 | tf_op jit(solution)/shard_map/psum | solution.py:1497
  168.8 13.2 %fusion.8 = bf16[768,1536]{1,0:T(8,128)(2,1)} fusion(bf16[2048,1536]{1,0:T(8,128)(2,1)} %bitcast.65, f32[2048]{0:T(1024)S(1)} %bitcast.55, bf16[2048,768]{1,0:T(8,128)(2,1)} %get-tuple-element.38, f32[2048,768]{1,0:T(8,128)} %get-tuple-element.39), kind=kOutput, calls=%fused_computation.24 | convolution fusion | flops 4853465088 | bytes 18096128 | tf_op jit(solution)/shard_map/dot_general | solution.py:1388
  182.0 5.6 %fusion.2 = (bf16[2048,768]{1,0:T(8,128)(2,1)S(1)}, bf16[2048,768]{1,0:T(8,128)(2,1)}) fusion(bf16[2048,768]{1,0:T(8,128)(2,1)S(1)} %copy-done.17, f32[2048,768]{1,0:T(8,128)S(1)} %copy-done.13, f32[2048]{0:T(1024)S(1)} %reduce, f32[2048]{0:T(1024)S(1)} %fusion.18, f32[2048,768]{1,0:T(8,128)S(1)} %copy-done.14, f32[2048]{0:T(1024)S(1)} %bitcast.57), kind=kLoop, calls=%fused_computation.6 | loop fusion | flops 29884416 | bytes 22044672 | tf_op jit(solution)/shard_map/convert_element_type | solution.py:1502
  187.6 10.0 %multiply_convert_fusion.1 = bf16[2048,1536]{1,0:T(8,128)(2,1)} fusion(bf16[768,1536]{1,0:T(8,128)(2,1)} %bitcast.67, f32[2048]{0:T(1024)S(1)} %bitcast.58, bf16[2048,768]{1,0:T(8,128)(2,1)S(1)} %copy-done.17, f32[2048,768]{1,0:T(8,128)S(1)} %copy-done.13), kind=kOutput, calls=%fused_computation.1 | convolution fusion | flops 4849139712 | bytes 18096128 | tf_op jit(solution)/shard_map/dot_general | solution.py:1503
  197.6 6.5 %convolution_convert_fusion = bf16[1536,768]{1,0:T(8,128)(2,1)} fusion(bf16[2048,1536]{1,0:T(8,128)(2,1)S(1)} %bitcast.47, bf16[2048,768]{1,0:T(8,128)(2,1)S(1)} %get-tuple-element.55.d_gate), kind=kOutput, calls=%fused_computation.25 | convolution fusion | flops 4833017856 | bytes 11796480 | tf_op jit(solution)/shard_map/dot_general | solution.py:1388
  204.1 71.8 %mixer_backward.1 = (bf16[2048,1024]{1,0:T(8,128)(2,1)}, bf16[2048,128]{1,0:T(8,128)(2,1)S(1)}, f32[8,1024]{1,0:T(8,128)S(1)}, f32[512,1536]{1,0:T(8,128)}, bf16...) custom-call(bf16[2048,1024]{1,0:T(8,128)(2,1)} %get-tuple-element.34.u_ref.halo_ref, ...), custom_call_target="tpu_custom_call" | custom-call | tf_op jit(solution)/shard_map/mixer_backward/pallas_call | solution.py:416
  275.9 0.8 copy-done.3
  276.6 0.7 copy-done.4
  278.0 68.3 %finish_last.1 = (f32[512,1536]{1,0:T(8,128)}, bf16[192,6528]{1,0:T(8,128)(2,1)}, f32[8,3456]{1,0:T(8,128)}) custom-call(bf16[2048,1536]{1,0:T(8,128)(2,1)} %bitcast.44, bf16[2048,768]{1,0:T(8,128)(2,1)} %copy-done.9, bf16[2048,1024]{1,0:T(8,128)(2,1)} %get-tuple-element.43.d_u, bf16[2048,128]{1,0:T(8,128)(2,1)} %copy-done.3, bf16[1536,1536]{1,0:T(8,128)(2,1)} %bitcast.49, ...), custom_call_target="tpu_custom_call" | custom-call | tf_op jit(solution)/shard_map/finish_last/pallas_call | solution.py:1349
  346.3 1.4 slice_bitcast_fusion
  347.7 2.6 fusion.10
  350.3 5.6 %fusion.13 = (f32[1,512,1536]{2,1,0:T(8,128)}, f32[1,512,1536]{2,1,0:T(8,128)}) fusion(f32[512,1536]{1,0:T(8,128)S(1)} %copy-done.10, f32[512]{0:T(512)S(1)} %get-tuple-element.72, f32[512]{0:T(512)S(1)} %get-tuple-element.71, bf16[1,512,1536]{2,1,0:T(8,128)(2,1)S(1)} %copy-done.15, bf16[1,512,1536]{2,1,0:T(8,128)(2,1)S(1)} %copy-done.8, ...), kind=kLoop, calls=%fused_computation.30 | loop fusion | flops 5505024 | bytes 15732736 | tf_op jit(solution)/shard_map/broadcast_in_dim | solution.py:1535
  357.2 2.4 convert_multiply_fusion.8
  359.6 4.0 %convert_multiply_fusion.2 = (f32[192,6448]{1,0:T(8,128)}, f32[192]{0:T(256)}) fusion(f32[192]{0:T(256)S(1)} %convert_element_type.65, bf16[192,6528]{1,0:T(8,128)(2,1)S(1)} %copy-done.18, bf16[192,6448]{1,0:T(8,128)(2,1)S(1)} %copy-done.12), kind=kLoop, calls=%fused_computation.15 | loop fusion | flops 6189888 | bytes 9905664 | tf_op jit(solution)/shard_map/mul | solution.py:1527
  (57 shorter events, 6.3 us)
Async XLA Ops:
  5.0 2.1 copy-start.11
  7.1 79.5 %copy-start.5 = (f32[4,3328]{1,0:T(4,128)S(1)}, f32[4,3328]{1,0:T(4,128)}, u32[]{:S(2)}) copy-start(f32[4,3328]{1,0:T(4,128)} %wk_ref.3) | copy-start | bytes 159748
  7.1 79.5 %copy-start.6 = (s32[1,2048]{1,0:T(1,128)S(1)}, s32[1,2048]{1,0:T(1,128)}, u32[]{:S(2)}) copy-start(s32[1,2048]{1,0:T(1,128)} %param.13) | copy-start | bytes 24580
  86.6 1.3 copy-start
  144.6 0.8 copy-start.1
  168.7 13.2 %copy-start.13 = (f32[2048,768]{1,0:T(8,128)S(1)}, f32[2048,768]{1,0:T(8,128)}, u32[]{:S(2)}) copy-start(f32[2048,768]{1,0:T(8,128)} %get-tuple-element.39) | copy-start | bytes 18874372
  168.7 13.2 %copy-start.14 = (f32[2048,768]{1,0:T(8,128)S(1)}, f32[2048,768]{1,0:T(8,128)}, u32[]{:S(2)}) copy-start(f32[2048,768]{1,0:T(8,128)} %get-tuple-element.70) | copy-start | bytes 18874372
  168.7 13.2 %copy-start.17 = (bf16[2048,768]{1,0:T(8,128)(2,1)S(1)}, bf16[2048,768]{1,0:T(8,128)(2,1)}, u32[]{:S(2)}) copy-start(bf16[2048,768]{1,0:T(8,128)(2,1)} %get-tuple-element.38) | copy-start | bytes 9437188
  181.9 15.6 %slice-start = ((s8[6291456]{0:T(1024)(128)(4,1)}), s8[4194304]{0:T(1024)(128)(4,1)S(1)}, s32[]{:S(2)}) async-start(s8[6291456]{0:T(1024)(128)(4,1)} %bitcast.45), calls=%async_computation | async-start | bytes 8388608
  187.5 10.0 %copy-start.9 = (bf16[2048,768]{1,0:T(8,128)(2,1)}, bf16[2048,768]{1,0:T(8,128)(2,1)S(1)}, u32[]{:S(2)}) copy-start(bf16[2048,768]{1,0:T(8,128)(2,1)S(1)} %get-tuple-element.55.d_gate) | copy-start | bytes 9437188
  187.6 10.0 %slice-start.1 = ((s8[6291456]{0:T(1024)(128)(4,1)}), s8[2097152]{0:T(1024)(128)(4,1)S(1)}, s32[]{:S(2)}) async-start(s8[6291456]{0:T(1024)(128)(4,1)} %bitcast.45), calls=%async_computation.1 | async-start | bytes 4194304
  197.6 6.5 %copy-start.2 = (bf16[2048,128]{1,0:T(8,128)(2,1)S(1)}, bf16[2048,128]{1,0:T(8,128)(2,1)}, u32[]{:S(2)}) copy-start(bf16[2048,128]{1,0:T(8,128)(2,1)} %copy-done.1) | copy-start | bytes 1572868
  275.8 0.8 copy-start.3
  276.6 0.7 copy-start.4
  277.4 0.6 copy-start.7
  278.0 69.7 %copy-start.8 = (bf16[1,512,1536]{2,1,0:T(8,128)(2,1)S(1)}, bf16[1,512,1536]{2,1,0:T(8,128)(2,1)}, u32[]{:S(2)}) copy-start(bf16[1,512,1536]{2,1,0:T(8,128)(2,1)} %param.12) | copy-start | bytes 4718596
  346.3 4.0 %copy-start.10 = (f32[512,1536]{1,0:T(8,128)S(1)}, f32[512,1536]{1,0:T(8,128)}, u32[]{:S(2)}) copy-start(f32[512,1536]{1,0:T(8,128)} %get-tuple-element.47) | copy-start | bytes 9437188
  346.3 4.0 %copy-start.15 = (bf16[1,512,1536]{2,1,0:T(8,128)(2,1)S(1)}, bf16[1,512,1536]{2,1,0:T(8,128)(2,1)}, u32[]{:S(2)}) copy-start(bf16[1,512,1536]{2,1,0:T(8,128)(2,1)} %param.23) | copy-start | bytes 4718596
  350.3 5.6 %copy-start.19 = (f32[8,3456]{1,0:T(8,128)S(1)}, f32[8,3456]{1,0:T(8,128)}, u32[]{:S(2)}) copy-start(f32[8,3456]{1,0:T(8,128)} %get-tuple-element.49) | copy-start | bytes 331780
  350.3 6.9 %copy-start.16 = (bf16[384,1536]{1,0:T(8,128)(2,1)S(1)}, bf16[384,1536]{1,0:T(8,128)(2,1)}, u32[]{:S(2)}) copy-start(bf16[384,1536]{1,0:T(8,128)(2,1)} %param.22) | copy-start | bytes 3538948
  350.3 9.3 %copy-start.18 = (bf16[192,6528]{1,0:T(8,128)(2,1)S(1)}, bf16[192,6528]{1,0:T(8,128)(2,1)}, u32[]{:S(2)}) copy-start(bf16[192,6528]{1,0:T(8,128)(2,1)} %get-tuple-element.48) | copy-start | bytes 7520260
  355.9 3.7 %copy-start.12 = (bf16[192,6448]{1,0:T(8,128)(2,1)S(1)}, bf16[192,6448]{1,0:T(8,128)(2,1)}, u32[]{:S(2)}) copy-start(bf16[192,6448]{1,0:T(8,128)(2,1)} %param.15) | copy-start | bytes 7428100

commit v4 on v3

--- a/solution.py
+++ b/solution.py
@@ -511,16 +511,20 @@
     return pltpu.SemaphoreType.DMA(shape)
 
 
-def gather_pieces_start(at, own, slot, sems):
-    send, recv, local = sems
+def gather_pieces_start(at, own, slot, sems, stage=None):
+    send, recv, local = sems[:3]
     rows = own.shape[0] // PARTS
-    pltpu.make_async_copy(own, slot(at.s), local).start()
     for k in range(PARTS):
         part = pl.ds(k * rows, rows)
         remote(own.at[part], slot(at.s).at[part], send.at[1, k], recv.at[1, k], at.far).start()
     for k in range(PARTS):
         part = pl.ds(k * rows, rows)
         remote(own.at[part], slot(at.s).at[part], send.at[0, k], recv.at[0, k], at.sib).start()
+    if stage is not None:
+        copy = pltpu.make_async_copy(own, stage, local)
+        copy.start()
+        copy.wait()
+    pltpu.make_async_copy(own if stage is None else stage, slot(at.s), local).start()
 
 
 def gather_pieces_pass(at, own, slot, sems):
@@ -550,14 +554,14 @@
 CUTS = 2
 
 
-def gather_shards(at, main, com, main_all, com_all, sems, between):
+def gather_shards(at, main, com, main_all, com_all, stage, sems, between):
     send, recv, csend, crecv, psend, precv, local = sems
     half, cut = com.shape[0] // 2, main.shape[0] // CUTS
     mine = pl.ds(pl.multiple_of(at.c * half, half), half)
-    keep = pltpu.make_async_copy(main, main_all.at[at.w], local.at[0])
-    com_keep = pltpu.make_async_copy(com, com_all.at[at.w], local.at[1])
-    keep.start()
-    com_keep.start()
+    load = pltpu.make_async_copy(main, stage[0], local.at[0])
+    com_load = pltpu.make_async_copy(com, stage[1], local.at[1])
+    keep = pltpu.make_async_copy(stage[0], main_all.at[at.w], local.at[0])
+    com_keep = pltpu.make_async_copy(stage[1], com_all.at[at.w], local.at[1])
 
     def hop(zp, q, way, device, own=False):
         w, n, part = 2 * zp + at.x, zp * CUTS + q, pl.ds(q * cut, cut)
@@ -598,6 +602,13 @@
         if q > 0:
             all_ways(sent, q - 1)
         all_ways(begin, q)
+        if q == 0:
+            load.start()
+            com_load.start()
+            load.wait()
+            com_load.wait()
+            keep.start()
+            com_keep.start()
     for d in (1, 2, 3):
         if d == 3:
             between()
@@ -654,13 +665,13 @@
         remote(got, got, psend.at[w], precv.at[w], at.sib).wait_recv()
 
 
-def gather_kernel(hid, main, com, hid_all, main_all, com_all, *sems):
+def gather_kernel(hid, main, com, hid_all, main_all, com_all, hid_v, main_v, com_v, *sems):
     at = Place()
     at.greet()
     slot = lambda s: hid_all.at[s]
-    gather_pieces_start(at, hid, slot, sems[0:3])
+    gather_pieces_start(at, hid, slot, sems[0:3], hid_v)
     pass_on = lambda: gather_pieces_pass(at, hid, slot, sems[0:3])
-    gather_shards(at, main, com, main_all, com_all, sems[3:10], pass_on)
+    gather_shards(at, main, com, main_all, com_all, (main_v, com_v), sems[3:10], pass_on)
     gather_pieces_end(at, hid, slot, sems[0:3])
 
 
@@ -671,7 +682,8 @@
         in_specs=[pl.BlockSpec(memory_space=ANY)] * 3,
         out_specs=[pl.BlockSpec(memory_space=ANY)] * 3,
         out_shape=[shape(4, hid), shape(8, main), shape(8, com)],
-        scratch_shapes=[dma(3, PARTS), dma(3, PARTS), dma()]
+        scratch_shapes=[pltpu.VMEM(v.shape, v.dtype) for v in (hid, main, com)]
+        + [dma(3, PARTS), dma(3, PARTS), dma()]
         + [dma(3, 4 * CUTS), dma(8 * CUTS), dma(3, 4), dma(8), dma(8), dma(8), dma(2)],
         compiler_params=pltpu.CompilerParams(collective_id=1, has_side_effects=True),
         name="gather_first",
@@ -696,10 +708,19 @@
             jax.ShapeDtypeStruct((4,) + cot.shape, cot.dtype),
             jax.ShapeDtypeStruct((2,) + rows.shape, rows.dtype),
         )
-        scratch = (dma(3, SLICES), dma(3, SLICES), dma(), dma(3, SLICES), dma(2, SLICES), dma())
+        scratch = (
+            pltpu.VMEM(cot.shape, cot.dtype),
+            pltpu.VMEM(rows.shape, rows.dtype),
+            dma(3, SLICES),
+            dma(3, SLICES),
+            dma(),
+            dma(3, SLICES),
+            dma(2, SLICES),
+            dma(),
+        )
         collective_id = 2
 
-        def __init__(self, own, row_own, full, row_full, send, recv, local, rsend, rrecv, rlocal):
+        def __init__(self, own, row_own, full, row_full, stage, rstage, send, recv, local, rsend, rrecv, rlocal):
             self.at = at = Place()
             self.own, self.full, self.row_own, self.row_full = own, full, row_own, row_full
             self.rrecv = rrecv
@@ -707,8 +728,10 @@
             part = lambda k: pl.ds(pl.multiple_of(k * cut, cut), cut)
             rpart = lambda k: pl.ds(pl.multiple_of(k * rcut, rcut), rcut)
             piece = lambda s, k: full.at[s, part(k)]
-            self.keep = pltpu.make_async_copy(own, full.at[at.s], local)
-            self.rkeep = pltpu.make_async_copy(row_own, row_full.at[at.x], rlocal)
+            self.load = pltpu.make_async_copy(own, stage, local)
+            self.keep = pltpu.make_async_copy(stage, full.at[at.s], local)
+            self.rload = pltpu.make_async_copy(row_own, rstage, rlocal)
+            self.rkeep = pltpu.make_async_copy(rstage, row_full.at[at.x], rlocal)
             self.to_sib = lambda k: remote(own.at[part(k)], piece(at.s, k), send.at[0, k], recv.at[0, k], at.sib)
             self.to_far = lambda k: remote(own.at[part(k)], piece(at.s, k), send.at[1, k], recv.at[1, k], at.far)
             self.pass_on = lambda k: remote(piece(at.s_far, k), piece(at.s_far, k), send.at[2, k], recv.at[2, k], at.sib)
@@ -731,14 +754,19 @@
             @pl.when(i == 0)
             def _():
                 at.greet()
-                self.keep.start()
+                self.load.start()
                 each_slice(lambda k: self.to_sib(k).start())
 
                 @pl.when(at.z == at.s)
                 def _():
+                    self.rload.start()
+                    self.rload.wait()
                     self.rkeep.start()
                     self.rkeep.wait()
 
+                self.load.wait()
+                self.keep.start()
+
             k = i - 1
 
             @pl.when((k >= 0) & (k < SLICES))
@@ -751,9 +779,10 @@
                 self.pass_on(k - SLICES).start()
 
             far_away = jnp.where(at.z > at.s, at.z - at.s, at.s - at.z)
-            r = i - 1 - 2 * far_away
-
-            @pl.when((r >= 0) & (r < SLICES))
+            v = 3 * i - 6 * far_away + 1
+            r = jnp.where(v >= 0, lax.div(v, 4), -1)
+
+            @pl.when((r >= 0) & (r < SLICES) & (4 * r < v))
             def _():
                 @pl.when(at.z != at.s)
                 def _():
@@ -796,12 +825,14 @@
 
 
 def add_into(dst, src, rows):
+    step = next(n for n in (64, 48, 32, 16) if rows % n == 0)
+
     def body(i, _):
-        part = pl.ds(pl.multiple_of(i * 16, 16), 16)
+        part = pl.ds(pl.multiple_of(i * step, 16), step)
         dst[part, :] = (dst[part, :].astype(f32) + src[part, :].astype(f32)).astype(bf16)
         return 0
 
-    lax.fori_loop(0, rows // 16, body, 0)
+    lax.fori_loop(0, rows // step, body, 0)
 
 
 def far_first(at, i):
@@ -1021,9 +1052,10 @@
 
             ends = jnp.where(at.z > 3 - at.z, at.z, 3 - at.z)
             chain = jnp.where(at.z < at.s, at.z, jnp.where(at.z > at.s, 3 - at.z, ends))
-            r = i - 2 - 2 * chain
-
-            @pl.when((r >= 0) & (r < SLICES))
+            v = 10 * i - 17 * chain - 26 + 10
+            r = jnp.where(v >= 0, lax.div(v, 11), -1)
+
+            @pl.when((r >= 0) & (r < SLICES) & (11 * r < v))
             def _():
                 acc = self.acc.at[self.rpart(r)]
                 self.to_side(r).wait_recv()
@@ -1052,24 +1084,26 @@
                     self.spread_far(r).start()
                     self.spread_sib(r).start()
 
-            g = i - 6
-
-            @pl.when((g >= 0) & (g < 8))
+            g = i - (last - 7)
+
+            @pl.when(g >= 0)
             def _():
                 self.gates.side_copy(g).start()
 
             inner = jnp.where((at.z == 1) | (at.z == 2), 1, 0)
-            g = i - 8 - inner
-
-            @pl.when((g >= 0) & (g < 8))
+            g = i - 11 - inner
+
+            @pl.when(g >= 0)
             def _():
                 self.gates.step(g)
 
             @pl.when(i == last)
             def _():
-                @pl.when(inner == 1)
-                def _():
-                    self.gates.step(jnp.int32(7))
+                def rest(k, _):
+                    self.gates.step(k)
+                    return 0
+
+                lax.fori_loop(last - 10 - inner, 8, rest, 0)
 
                 self.store.start()
                 self.store_gate.start()
@@ -1158,10 +1192,10 @@
 
 def last_kernel(hid, d_gate, d_u, d_dt, w_main, w_com, gate_sum, small,
                 back_sum, in_sum, sums_out,
-                hid_v, dg_v, du_v, dt_v, wm_v, wc_v,
+                hid_v, dp_v, w_v,
                 b_diag, b_sib, b_far, b_own, from_sib, pass_sib, from_far,
                 part_v, mside, mlow, mhigh, macc, mown, csib, cown, cacc, cside, clow, chigh, cfar, csum,
-                sgot, stotal, sfull, *sems):
+                sgot, stotal, sfull, gate_v, *sems):
     at = Place()
     sems = list(sems)
     take = lambda n: [sems.pop(0) for _ in range(n)]
@@ -1170,7 +1204,7 @@
     )
     piece = hid_v.shape[0] // 4
     shard = hid_v.shape[1] // 8
-    wide = dg_v.shape[1]
+    wide = d_gate.shape[1]
     half = shard // 2
     mine = pl.ds(pl.multiple_of(at.c * half, half), half)
     other = pl.ds(pl.multiple_of((1 - at.c) * half, half), half)
@@ -1179,25 +1213,26 @@
     order = (at.s_diag, at.s_far, at.s_sib, at.s)
     rows_of = lambda s: pl.ds(pl.multiple_of(s * piece, piece), piece)
     weights = [
-        pltpu.make_async_copy(w_main, wm_v, load[0].at[0]),
-        pltpu.make_async_copy(w_com, wc_v, load[0].at[1]),
+        pltpu.make_async_copy(w_main, w_v.at[:, pl.ds(0, 2 * wide)], load[0].at[0]),
+        pltpu.make_async_copy(w_com, w_v.at[:, pl.ds(2 * wide, 384)], load[0].at[1]),
     ]
     loads = []
     for k, s in enumerate(order):
         r = rows_of(s)
         loads.append(
             [
-                pltpu.make_async_copy(d_gate.at[r], dg_v.at[r], load[1].at[k]),
-                pltpu.make_async_copy(d_u.at[r], du_v.at[r], load[2].at[k]),
-                pltpu.make_async_copy(d_dt.at[r], dt_v.at[r], load[3].at[k]),
+                pltpu.make_async_copy(d_gate.at[r], dp_v.at[r, pl.ds(0, wide)], load[1].at[k]),
+                pltpu.make_async_copy(d_u.at[r], dp_v.at[r, pl.ds(wide, wide + 256)], load[2].at[k]),
+                pltpu.make_async_copy(d_dt.at[r], dp_v.at[r, pl.ds(2 * wide + 256, 128)], load[3].at[k]),
             ]
         )
     hid_load = pltpu.make_async_copy(hid, hid_v, load[4])
-    for copy in loads[0] + weights + loads[1] + loads[2] + loads[3] + [hid_load]:
+    soon, later = weights + loads[0] + loads[1], [hid_load] + loads[2] + loads[3]
+    for copy in soon + later:
         copy.start()
     gate_slot = lambda s: in_sum.at[:, pl.ds(pl.multiple_of(s * wide, 128), wide)]
     x_slot = lambda s: in_sum.at[:, pl.ds(pl.multiple_of(E + s * wide, 128), wide)]
-    gather_pieces_start(at, gate_sum, gate_slot, gsem)
+    gather_pieces_start(at, gate_sum, gate_slot, gsem, gate_v)
     small_start(at, small, sgot, ssem)
 
     send, recv = bsem
@@ -1207,24 +1242,15 @@
     to_sib = [remote(b_sib.at[p], from_sib.at[p], send.at[1, k], recv.at[1, k], at.sib) for k, p in enumerate(parts)]
     to_far = [remote(b_far.at[p], from_far.at[p], send.at[2, k], recv.at[2, k], at.far) for k, p in enumerate(parts)]
 
-    def back_piece(s, out):
-        base = s * piece
-
-        def body(t, _):
-            tile = pl.ds(pl.multiple_of(base + t * 256, 256), 256)
-            place = pl.ds(pl.multiple_of(t * 256, 256), 256)
-            for n in range(hid_v.shape[1] // 256):
-                col = slice(256 * n, 256 * n + 256)
-                total = dot_nt(dg_v[tile, :], wm_v[col, 0:wide])
-                total = total + dot_nt(du_v[tile, 0:wide], wm_v[col, wide : 2 * wide])
-                total = total + dot_nt(du_v[tile, wide : wide + 256], wc_v[col, 0:256])
-                total = total + dot_nt(dt_v[tile, :], wc_v[col, 256:384])
-                out[place, col] = total.astype(bf16)
-            return 0
-
-        lax.fori_loop(0, piece // 256, body, 0)
-
-    big = ReduceShards(at, lambda zp: part_v.at[zp, 1 - at.x, :, pl.ds(0, wide)], 1, macc, mside, mlow, mhigh, msem)
+    def back_tile(s, out, t):
+        tile = pl.ds(pl.multiple_of(s * piece + t * 256, 256), 256)
+        place = pl.ds(t * 256, 256)
+
+        for n in range(hid_v.shape[1] // 256):
+            col = slice(256 * n, 256 * n + 256)
+            out[place, col] = dot_nt(dp_v[tile, :], w_v[col, :]).astype(bf16)
+
+    big = ReduceShards(at, lambda zp: part_v.at[zp, 1 - at.x, :, pl.ds(0, wide)], 2, macc, mside, mlow, mhigh, msem)
     few = ReduceShards(at, lambda zp: cown.at[zp, 1 - at.x], 1, cacc, cside, clow, chigh, csem)
     com_cols = pl.ds(wide, 384)
     com_to_sib = lambda zp: remote(
@@ -1234,19 +1260,13 @@
     def shard_pair(i):
         zp = far_first(at, i)
         lanes = pl.ds(pl.multiple_of(zp * 2 * shard, 128), 2 * shard)
-        left = hid_v[:, lanes]
-        tn = lambda right: lax.dot_general(left, right, (((0,), (0,)), ((), ())), preferred_element_type=f32)
-        for n in range((wide + 256) // 256):
-            col = slice(256 * n, 256 * n + 256)
-            got = tn(du_v[:, col]).astype(bf16)
-            part_v[zp, 0, :, col] = got[0:shard]
-            part_v[zp, 1, :, col] = got[shard : 2 * shard]
-        col = slice(wide + 256, wide + 384)
-        got = tn(dt_v[...]).astype(bf16)
-        part_v[zp, 0, :, col] = got[0:shard]
-        part_v[zp, 1, :, col] = got[shard : 2 * shard]
+        got = lax.dot_general(
+            hid_v[:, lanes], dp_v[:, wide : 2 * wide + 384], (((0,), (0,)), ((), ())), preferred_element_type=f32
+        ).astype(bf16)
+        part_v[zp, 0] = got[0:shard]
+        part_v[zp, 1] = got[shard : 2 * shard]
         macc[zp] = part_v[zp, at.x, :, 0:wide]
-        big.side_copy(i).start()
+        big.side_copy(2 * i).start()
         com_to_sib(zp).start()
 
     def com_pair(i):
@@ -1258,39 +1278,71 @@
         cacc[zp] = cown[zp, at.x]
         few.side_copy(i).start()
 
-    for copy in loads[0] + weights:
+    ends = (at.z == 0) | (at.z == 3)
+
+    def step(j, who):
+        @pl.when(who)
+        def _():
+            big.step(j)
+            if j % 2:
+                few.step(j // 2)
+
+    tiles = piece // 256
+    per = PARTS // tiles
+    def far_tile(t):
+        back_tile(at.s_far, b_far, t)
+        for k in range(t * per, t * per + per):
+            to_pass[k].wait_recv()
+            add_into(b_far.at[parts[k]], pass_sib.at[parts[k]], rows)
+            to_far[k].start()
+
+    for copy in soon:
         copy.wait()
-    back_piece(at.s_diag, b_diag)
-    for copy in to_pass:
-        copy.start()
-    for copy in loads[1] + loads[2] + loads[3] + [hid_load]:
+    for t in range(tiles):
+        back_tile(at.s_diag, b_diag, t)
+        for k in range(t * per, t * per + per):
+            to_pass[k].start()
+    far_tile(0)
+    for copy in later:
         copy.wait()
+    def sib_tile(t):
+        back_tile(at.s_sib, b_sib, t)
+        for k in range(t * per, t * per + per):
+            to_sib[k].start()
+
     shard_pair(0)
-    back_piece(at.s_far, b_far)
-    for k, p in enumerate(parts):
-        to_pass[k].wait_recv()
-        add_into(b_far.at[p], pass_sib.at[p], rows)
-        to_far[k].start()
+    far_tile(1)
+    big.side_copy(1).start()
+    shard_pair(1)
     com_pair(0)
-    shard_pair(1)
     shard_pair(2)
+    big.side_copy(3).start()
     com_pair(1)
-    big.step(0)
-    few.step(0)
+    step(0, ends)
+    step(1, ends)
+    shard_pair(3)
+    big.side_copy(5).start()
+    com_pair(2)
+    step(0, ~ends)
+    step(2, ends)
     gather_pieces_pass(at, gate_sum, gate_slot, gsem)
-    shard_pair(3)
-    com_pair(2)
-    back_piece(at.s_sib, b_sib)
-    for copy in to_sib:
-        copy.start()
+    sib_tile(0)
+    big.side_copy(7).start()
     com_pair(3)
-    big.step(1)
-    few.step(1)
-    back_piece(at.s, b_own)
-    big.step(2)
-    few.step(2)
+    step(1, ~ends)
+    step(3, ends)
+    sib_tile(1)
+    step(2, ~ends)
+    step(4, ends)
+    back_tile(at.s, b_own, 0)
+    step(3, ~ends)
+    step(4, ~ends)
+    step(5, ends)
+    back_tile(at.s, b_own, 1)
+    step(5, ~ends)
     small_pass(at, small, sgot, stotal, sfull, ssem, smore)
-    big.step(3)
+    for j in (6, 7):
+        big.step(j)
     few.step(3)
     mown[...] = macc[at.z]
     gather_pieces_start(at, mown, x_slot, asem)
@@ -1302,11 +1354,11 @@
         to_far[k].wait_recv()
 
         def body(i, _):
-            r = pl.ds(pl.multiple_of(k * rows + i * 16, 16), 16)
+            r = pl.ds(pl.multiple_of(k * rows + i * 32, 32), 32)
             back_sum[r, :] = b_own[r, :].astype(f32) + from_sib[r, :].astype(f32) + from_far[r, :].astype(f32)
             return 0
 
-        lax.fori_loop(0, rows // 16, body, 0)
+        lax.fori_loop(0, rows // 32, body, 0)
     far_copy.wait()
     add_into(csum, cfar, half)
     com_out = in_sum.at[mine, pl.ds(2 * E, 384)]
@@ -1345,7 +1397,7 @@
     piece, shard, half = length // 4, depth // 8, depth // 16
     wide = d_gate.shape[1]
     vm = pltpu.VMEM
-    shards4 = [dma(3, 4), dma(4), dma(4), dma(4)]
+    shards4 = lambda cuts: [dma(3, 4 * cuts), dma(4 * cuts), dma(4 * cuts), dma(4 * cuts)]
     return pl.pallas_call(
         last_kernel,
         in_specs=[pl.BlockSpec(memory_space=ANY)] * 7 + [pl.BlockSpec(memory_space=pltpu.VMEM)],
@@ -1359,7 +1411,7 @@
             jax.ShapeDtypeStruct((shard, 2 * E + 384), bf16),
             jax.ShapeDtypeStruct((8, E + 384), f32),
         ],
-        scratch_shapes=[vm(v.shape, bf16) for v in (hid, d_gate, d_u, d_dt, w_main, w_com)]
+        scratch_shapes=[vm(hid.shape, bf16), vm((length, 2 * wide + 384), bf16), vm((depth, 2 * wide + 384), bf16)]
         + [vm((piece, depth), bf16)] * 7
         + [vm((4, 2, shard, wide + 384), bf16)]
         + [vm((4, shard, wide), bf16)] * 4
@@ -1367,11 +1419,11 @@
         + [vm((4, 2, half, 384), bf16)] * 2
         + [vm((4, half, 384), bf16)] * 4
         + [vm((half, 384), bf16)] * 2
-        + [vm((8,) + small.shape, f32), vm(small.shape, f32), vm((4,) + small.shape, f32)]
+        + [vm((8,) + small.shape, f32), vm(small.shape, f32), vm((4,) + small.shape, f32), vm(gate_sum.shape, bf16)]
         + [dma(2), dma(4), dma(4), dma(4), dma(), dma()]
         + [dma(3, PARTS), dma(3, PARTS)]
-        + shards4
-        + shards4
+        + shards4(2)
+        + shards4(1)
         + [dma(4), dma(4), dma(), dma(), dma(), dma(), dma()]
         + [dma(8), dma(8)]
         + [dma(3), dma(3), dma()]

time: 370 us -> 350 us (0.946)
  Pallas kernels: 274 us -> 252 us
    pallas_call x1, Pallas kernels: 77.1 us -> 66.6 us  [gather_first(): pl.pallas_call(gather_kernel, in_specs=[pl.BlockSpec(memory_space=ANY)] *...]
    pallas_call x1, Pallas kernels: 56.7 us -> 50.5 us  [mixer_fwd(): pl.pallas_call(functools.partial(fwd_kernel, traffic), grid=(n + 1,), in_...]
where the time goes in v4:
time: 350 us; the launch traced here: 344 us
  Pallas kernels  252 us (72%)
  matrix products  42 us (12%)
  other arithmetic  25.6 us (7%)
  blocking collectives  12.7 us (4%)
  local copies, waits for them, and re-layouts  10.5 us (3%)
    pallas_call x1, Pallas kernels, mixer_bwd(): pl.pallas_call(functools.partial(bwd_kernel, traffic), grid=(n,), in_spec...  69 us
    pallas_call x1, Pallas kernels, gather_first(): pl.pallas_call(gather_kernel, in_specs=[pl.BlockSpec(memory_space=ANY)] *...  66.6 us
    pallas_call x1, Pallas kernels, finish_last(): pl.pallas_call(last_kernel, in_specs=[pl.BlockSpec(memory_space=ANY)] * 7...  65.9 us
    pallas_call x1, Pallas kernels, mixer_fwd(): pl.pallas_call(functools.partial(fwd_kernel, traffic), grid=(n + 1,), in_...  50.5 us
    dot_general x2, matrix products, over_rows(): lax.dot_general(left, right, (((0,), (0,)), ((), ())), preferred_element_...  19.7 us
    psum x1, blocking collectives, shards(): lax.psum(jnp.stack([jnp.sum(g * g, axis=1), jnp.sum(a * g, axis=1)]), 'seq')  12.7 us
    dot_general x1, matrix products, shards(): lax.dot_general(cot_all, w_out, (((1,), (1,)), ((), ())), preferred_eleme...  12.3 us
    dot_general x1, matrix products, shards(): jnp.dot(g_low, w_out, preferred_element_type=f32) * r  10 us

profile of v4, /device:TPU:0, one launch (start us, length us, event | category | flops | bytes accessed | tf_op | source)
XLA Modules:
  0.0 343.9 jit_solution(3524596841700475638)
XLA Ops:
  2.7 0.8 pad.13
  3.4 0.7 broadcast_in_dim.22.bias_ref
  4.2 0.7 broadcast_in_dim.23
  5.3 1.7 fusion.16.rest_1_
  7.9 0.9 pad_maximum_fusion.main
  9.4 66.6 %gather_first.1 = (bf16[4,512,1536]{2,1,0:T(8,128)(2,1)}, bf16[8,192,1536]{2,1,0:T(8,128)(2,1)}, bf16[8,192,384]{2,1,0:T(8,128)(2,1)}) custom-call(bf16[512,1536]{1,0:T(8,128)(2,1)} %bitcast.50, bf16[192,1536]{1,0:T(8,128)(2,1)} %pad_maximum_fusion.main, bf16[192,384]{1,0:T(8,128)(2,1)} %pad.12.com), custom_call_target="tpu_custom_call" | custom-call | tf_op jit(solution)/shard_map/gather_first/pallas_call | solution.py:680
  76.1 1.3 copy-done
  77.3 50.5 %mixer_forward.1 = (bf16[2048,1024]{1,0:T(8,128)(2,1)}, bf16[2048,128]{1,0:T(8,128)(2,1)S(1)}, f32[2048,768]{1,0:T(8,128)}, f32[2048,1]{1,0:T(8,128)S(1)}, bf16[...) custom-call(bf16[2048,1536]{1,0:T(8,128)(2,1)} %bitcast.43, ...), custom_call_target="tpu_custom_call" | custom-call | tf_op jit(solution)/shard_map/mixer_forward/pallas_call | solution.py:198
  127.8 0.8 copy-done.1
  128.9 12.3 %multiply_reduce_fusion.1 = (f32[2048]{0:T(1024)S(1)}, f32[2048]{0:T(1024)S(1)}, f32[2048,768]{1,0:T(8,128)}) fusion(bf16[2048,768]{1,0:T(8,128)(2,1)} %get-tuple-element.38, f32[2048,768]{1,0:T(8,128)} %get-tuple-element.39, bf16[2048,1536]{1,0:T(8,128)(2,1)} %bitcast.64, bf16[768,1536]{1,0:T(8,128)(2,1)} %bitcast.66), kind=kOutput, calls=%fused_computation.12 | convolution fusion | flops 4847562752 | bytes 24395776 | tf_op jit(solution)/shard_map/dot_general | solution.py:1548
  141.3 12.7 %psum.7 = f32[2,2048]{1,0:T(2,128)S(1)} all-reduce(f32[2,2048]{1,0:T(2,128)S(1)} %pad_maximum_fusion.1), channel_id=1, replica_groups=mesh['wshard'=8,'seq'=4] {'seq'}, use_global_device_ids=true, to_apply=%region_2.3 | all-reduce | flops 4096 | bytes 32768 | tf_op jit(solution)/shard_map/psum | solution.py:1549
  154.0 13.2 %fusion.8 = bf16[768,1536]{1,0:T(8,128)(2,1)} fusion(bf16[2048,1536]{1,0:T(8,128)(2,1)} %bitcast.65, f32[2048]{0:T(1024)S(1)} %bitcast.55, bf16[2048,768]{1,0:T(8,128)(2,1)} %get-tuple-element.38, f32[2048,768]{1,0:T(8,128)} %get-tuple-element.39), kind=kOutput, calls=%fused_computation.24 | convolution fusion | flops 4853465088 | bytes 18096128 | tf_op jit(solution)/shard_map/dot_general | solution.py:1440
  167.2 5.6 %fusion.2 = (bf16[2048,768]{1,0:T(8,128)(2,1)S(1)}, bf16[2048,768]{1,0:T(8,128)(2,1)}) fusion(bf16[2048,768]{1,0:T(8,128)(2,1)S(1)} %copy-done.17, f32[2048,768]{1,0:T(8,128)S(1)} %copy-done.13, f32[2048]{0:T(1024)S(1)} %reduce, f32[2048]{0:T(1024)S(1)} %fusion.18, f32[2048,768]{1,0:T(8,128)S(1)} %copy-done.14, f32[2048]{0:T(1024)S(1)} %bitcast.57), kind=kLoop, calls=%fused_computation.6 | loop fusion | flops 29884416 | bytes 22044672 | tf_op jit(solution)/shard_map/convert_element_type | solution.py:1554
  172.8 10.0 %multiply_convert_fusion.1 = bf16[2048,1536]{1,0:T(8,128)(2,1)} fusion(bf16[768,1536]{1,0:T(8,128)(2,1)} %bitcast.67, f32[2048]{0:T(1024)S(1)} %bitcast.58, bf16[2048,768]{1,0:T(8,128)(2,1)S(1)} %copy-done.17, f32[2048,768]{1,0:T(8,128)S(1)} %copy-done.13), kind=kOutput, calls=%fused_computation.1 | convolution fusion | flops 4849139712 | bytes 18096128 | tf_op jit(solution)/shard_map/dot_general | solution.py:1555
  182.9 6.5 %convolution_convert_fusion = bf16[1536,768]{1,0:T(8,128)(2,1)} fusion(bf16[2048,1536]{1,0:T(8,128)(2,1)S(1)} %bitcast.47, bf16[2048,768]{1,0:T(8,128)(2,1)S(1)} %get-tuple-element.55.d_gate), kind=kOutput, calls=%fused_computation.25 | convolution fusion | flops 4833017856 | bytes 11796480 | tf_op jit(solution)/shard_map/dot_general | solution.py:1440
  189.3 69.0 %mixer_backward.1 = (bf16[2048,1024]{1,0:T(8,128)(2,1)}, bf16[2048,128]{1,0:T(8,128)(2,1)S(1)}, f32[8,1024]{1,0:T(8,128)S(1)}, f32[512,1536]{1,0:T(8,128)}, bf16...) custom-call(bf16[2048,1024]{1,0:T(8,128)(2,1)} %get-tuple-element.34.u_ref.halo_ref, ...), custom_call_target="tpu_custom_call" | custom-call | tf_op jit(solution)/shard_map/mixer_backward/pallas_call | solution.py:416
  258.4 0.8 copy-done.3
  259.2 0.7 copy-done.4
  260.5 65.9 %finish_last.1 = (f32[512,1536]{1,0:T(8,128)}, bf16[192,6528]{1,0:T(8,128)(2,1)}, f32[8,3456]{1,0:T(8,128)}) custom-call(bf16[2048,1536]{1,0:T(8,128)(2,1)} %bitcast.44, bf16[2048,768]{1,0:T(8,128)(2,1)} %copy-done.9, bf16[2048,1024]{1,0:T(8,128)(2,1)} %get-tuple-element.43.d_u, bf16[2048,128]{1,0:T(8,128)(2,1)} %copy-done.3, bf16[1536,1536]{1,0:T(8,128)(2,1)} %bitcast.49, ...), custom_call_target="tpu_custom_call" | custom-call | tf_op jit(solution)/shard_map/finish_last/pallas_call | solution.py:1401
  326.4 1.4 slice_bitcast_fusion
  327.8 2.6 fusion.10
  330.4 5.6 %fusion.13 = (f32[1,512,1536]{2,1,0:T(8,128)}, f32[1,512,1536]{2,1,0:T(8,128)}) fusion(f32[512,1536]{1,0:T(8,128)S(1)} %copy-done.10, f32[512]{0:T(512)S(1)} %get-tuple-element.72, f32[512]{0:T(512)S(1)} %get-tuple-element.71, bf16[1,512,1536]{2,1,0:T(8,128)(2,1)S(1)} %copy-done.15, bf16[1,512,1536]{2,1,0:T(8,128)(2,1)S(1)} %copy-done.8, ...), kind=kLoop, calls=%fused_computation.30 | loop fusion | flops 5505024 | bytes 15732736 | tf_op jit(solution)/shard_map/broadcast_in_dim | solution.py:1587
  337.3 2.4 convert_multiply_fusion.8
  339.7 4.0 %convert_multiply_fusion.2 = (f32[192,6448]{1,0:T(8,128)}, f32[192]{0:T(256)}) fusion(f32[192]{0:T(256)S(1)} %convert_element_type.65, bf16[192,6528]{1,0:T(8,128)(2,1)S(1)} %copy-done.18, bf16[192,6448]{1,0:T(8,128)(2,1)S(1)} %copy-done.12), kind=kLoop, calls=%fused_computation.15 | loop fusion | flops 6189888 | bytes 9905664 | tf_op jit(solution)/shard_map/mul | solution.py:1579
  (57 shorter events, 6.3 us)
Async XLA Ops:
  5.0 2.1 copy-start.11
  7.1 69.0 %copy-start.5 = (f32[4,3328]{1,0:T(4,128)S(1)}, f32[4,3328]{1,0:T(4,128)}, u32[]{:S(2)}) copy-start(f32[4,3328]{1,0:T(4,128)} %wk_ref.3) | copy-start | bytes 159748
  7.1 69.0 %copy-start.6 = (s32[1,2048]{1,0:T(1,128)S(1)}, s32[1,2048]{1,0:T(1,128)}, u32[]{:S(2)}) copy-start(s32[1,2048]{1,0:T(1,128)} %param.13) | copy-start | bytes 24580
  76.1 1.3 copy-start
  127.8 0.8 copy-start.1
  154.0 13.2 %copy-start.13 = (f32[2048,768]{1,0:T(8,128)S(1)}, f32[2048,768]{1,0:T(8,128)}, u32[]{:S(2)}) copy-start(f32[2048,768]{1,0:T(8,128)} %get-tuple-element.39) | copy-start | bytes 18874372
  154.0 13.2 %copy-start.14 = (f32[2048,768]{1,0:T(8,128)S(1)}, f32[2048,768]{1,0:T(8,128)}, u32[]{:S(2)}) copy-start(f32[2048,768]{1,0:T(8,128)} %get-tuple-element.70) | copy-start | bytes 18874372
  154.0 13.2 %copy-start.17 = (bf16[2048,768]{1,0:T(8,128)(2,1)S(1)}, bf16[2048,768]{1,0:T(8,128)(2,1)}, u32[]{:S(2)}) copy-start(bf16[2048,768]{1,0:T(8,128)(2,1)} %get-tuple-element.38) | copy-start | bytes 9437188
  167.2 15.6 %slice-start = ((s8[6291456]{0:T(1024)(128)(4,1)}), s8[4194304]{0:T(1024)(128)(4,1)S(1)}, s32[]{:S(2)}) async-start(s8[6291456]{0:T(1024)(128)(4,1)} %bitcast.45), calls=%async_computation | async-start | bytes 8388608
  172.8 10.0 %copy-start.9 = (bf16[2048,768]{1,0:T(8,128)(2,1)}, bf16[2048,768]{1,0:T(8,128)(2,1)S(1)}, u32[]{:S(2)}) copy-start(bf16[2048,768]{1,0:T(8,128)(2,1)S(1)} %get-tuple-element.55.d_gate) | copy-start | bytes 9437188
  172.8 10.0 %slice-start.1 = ((s8[6291456]{0:T(1024)(128)(4,1)}), s8[2097152]{0:T(1024)(128)(4,1)S(1)}, s32[]{:S(2)}) async-start(s8[6291456]{0:T(1024)(128)(4,1)} %bitcast.45), calls=%async_computation.1 | async-start | bytes 4194304
  182.9 6.5 %copy-start.2 = (bf16[2048,128]{1,0:T(8,128)(2,1)S(1)}, bf16[2048,128]{1,0:T(8,128)(2,1)}, u32[]{:S(2)}) copy-start(bf16[2048,128]{1,0:T(8,128)(2,1)} %copy-done.1) | copy-start | bytes 1572868
  258.4 0.8 copy-start.3
  259.2 0.7 copy-start.4
  259.9 0.6 copy-start.7
  260.5 67.3 %copy-start.8 = (bf16[1,512,1536]{2,1,0:T(8,128)(2,1)S(1)}, bf16[1,512,1536]{2,1,0:T(8,128)(2,1)}, u32[]{:S(2)}) copy-start(bf16[1,512,1536]{2,1,0:T(8,128)(2,1)} %param.12) | copy-start | bytes 4718596
  326.4 4.0 %copy-start.10 = (f32[512,1536]{1,0:T(8,128)S(1)}, f32[512,1536]{1,0:T(8,128)}, u32[]{:S(2)}) copy-start(f32[512,1536]{1,0:T(8,128)} %get-tuple-element.47) | copy-start | bytes 9437188
  326.4 4.0 %copy-start.15 = (bf16[1,512,1536]{2,1,0:T(8,128)(2,1)S(1)}, bf16[1,512,1536]{2,1,0:T(8,128)(2,1)}, u32[]{:S(2)}) copy-start(bf16[1,512,1536]{2,1,0:T(8,128)(2,1)} %param.23) | copy-start | bytes 4718596
  330.4 5.6 %copy-start.19 = (f32[8,3456]{1,0:T(8,128)S(1)}, f32[8,3456]{1,0:T(8,128)}, u32[]{:S(2)}) copy-start(f32[8,3456]{1,0:T(8,128)} %get-tuple-element.49) | copy-start | bytes 331780
  330.4 6.9 %copy-start.16 = (bf16[384,1536]{1,0:T(8,128)(2,1)S(1)}, bf16[384,1536]{1,0:T(8,128)(2,1)}, u32[]{:S(2)}) copy-start(bf16[384,1536]{1,0:T(8,128)(2,1)} %param.22) | copy-start | bytes 3538948
  330.4 9.3 %copy-start.18 = (bf16[192,6528]{1,0:T(8,128)(2,1)S(1)}, bf16[192,6528]{1,0:T(8,128)(2,1)}, u32[]{:S(2)}) copy-start(bf16[192,6528]{1,0:T(8,128)(2,1)} %get-tuple-element.48) | copy-start | bytes 7520260
  336.0 3.7 %copy-start.12 = (bf16[192,6448]{1,0:T(8,128)(2,1)S(1)}, bf16[192,6448]{1,0:T(8,128)(2,1)}, u32[]{:S(2)}) copy-start(bf16[192,6448]{1,0:T(8,128)(2,1)} %param.15) | copy-start | bytes 7428100

commit v5 on v4

--- a/solution.py
+++ b/solution.py
@@ -97,10 +97,10 @@
         pass
 
 
-def fwd_kernel(traffic, hid_ref, main_ref, com_ref, seg_ref, segr_ref, wk_ref, bias_ref, par_ref, skip_ref, *rest):
+def fwd_kernel(traffic, hid_ref, gain_ref, main_ref, com_ref, seg_ref, segr_ref, wk_ref, bias_ref, par_ref, skip_ref, *rest):
     n_in, n_out = len(traffic.inputs), len(traffic.outputs)
     extra_in, rest = rest[:n_in], rest[n_in:]
-    u_ref, dt_ref, gate_ref, scale_ref, mixed_ref, save_ref = rest[:6]
+    u_ref, dt_ref, gate_ref, normed_ref, mixed_ref, save_ref = rest[:6]
     extra_out, rest = rest[6 : 6 + n_out], rest[6 + n_out :]
     state, useen, act, next_u, next_dt = rest[:5]
     step_no = pl.program_id(0)
@@ -123,23 +123,25 @@
     useen[8 : 8 + Q, :] = next_u[...]
     dt_now = next_dt[...]
 
-    low = hid_ref[...]
+    hid = hid_ref[...].astype(f32)
+    depth = hid.shape[1]
     total = jnp.zeros((Q, 128), f32)
-    for k in range(low.shape[1] // 128):
-        part = low[:, 128 * k : 128 * k + 128].astype(f32)
+    for k in range(depth // 128):
+        part = hid[:, 128 * k : 128 * k + 128]
         total = total + part * part
-    scale = lax.rsqrt(jnp.sum(total, axis=1, keepdims=True) / low.shape[1] + eps)
-    scale_ref[...] = scale
+    scale = lax.rsqrt(jnp.sum(total, axis=1, keepdims=True) / depth + eps)
+    normed_ref[...] = (hid * scale * gain_ref[...]).astype(bf16)
+    low = normed_ref[...]
     for k in range(xw // 256):
-        gate_ref[:, 256 * k : 256 * k + 256] = dot(low, main_ref[:, 256 * k : 256 * k + 256]) * scale
+        gate_ref[:, 256 * k : 256 * k + 256] = dot(low, main_ref[:, 256 * k : 256 * k + 256])
     for k in range(xw // 256):
-        got = (dot(low, main_ref[:, xw + 256 * k : xw + 256 * k + 256]) * scale).astype(bf16)
+        got = dot(low, main_ref[:, xw + 256 * k : xw + 256 * k + 256]).astype(bf16)
         u_ref[:, 256 * k : 256 * k + 256] = got
         next_u[:, 256 * k : 256 * k + 256] = got.astype(f32)
-    got = (dot(low, com_ref[:, 0:256]) * scale).astype(bf16)
+    got = dot(low, com_ref[:, 0:256]).astype(bf16)
     u_ref[:, xw : xw + 256] = got
     next_u[:, xw : xw + 256] = got.astype(f32)
-    got = facts.own((dot(low, com_ref[:, 256:384]) * scale).astype(bf16).astype(f32))
+    got = facts.own(dot(low, com_ref[:, 256:384]).astype(bf16).astype(f32))
     dt_ref[...] = got.astype(bf16)
     next_dt[...] = got
 
@@ -186,7 +188,7 @@
         state[:, lanes] = st * (jnp.exp(last) * carried[Q - 1 : Q, :]) + dot(b_t, to_end)
 
 
-def mixer_fwd(traffic, extra, hid, main, com, seg, segr, wk, bias, par, skip):
+def mixer_fwd(traffic, extra, hid, gain, main, com, seg, segr, wk, bias, par, skip):
     length, depth = hid.shape
     xw = main.shape[1] // 2
     width = xw + 256
@@ -200,6 +202,7 @@
         grid=(n + 1,),
         in_specs=[
             pl.BlockSpec((Q, depth), ahead),
+            whole(gain.shape),
             whole(main.shape),
             whole(com.shape),
             whole(seg.shape),
@@ -214,7 +217,7 @@
             pl.BlockSpec((Q, width), ahead),
             pl.BlockSpec((Q, 128), ahead),
             pl.BlockSpec((Q, xw), ahead),
-            pl.BlockSpec((Q, 1), ahead),
+            pl.BlockSpec((Q, depth), ahead),
             pl.BlockSpec((Q, xw), now),
             pl.BlockSpec((1, 128, xw), now3),
         ]
@@ -223,7 +226,7 @@
             jax.ShapeDtypeStruct((length, width), bf16),
             jax.ShapeDtypeStruct((length, 128), bf16),
             jax.ShapeDtypeStruct((length, xw), f32),
-            jax.ShapeDtypeStruct((length, 1), f32),
+            jax.ShapeDtypeStruct((length, depth), bf16),
             jax.ShapeDtypeStruct((length, xw), bf16),
             jax.ShapeDtypeStruct((n, 128, xw), bf16),
             *traffic.outputs,
@@ -242,10 +245,10 @@
             has_side_effects=traffic.collective_id is not None,
         ),
         name="mixer_forward",
-    )(hid, main, com, seg, segr, wk, bias, par, skip, *extra)
-
-
-def bwd_kernel(traffic, u_ref, halo_ref, dt_ref, scale_ref, seg_ref, segr_ref, wk_ref, bias_ref, par_ref, skip_ref,
+    )(hid, gain, main, com, seg, segr, wk, bias, par, skip, *extra)
+
+
+def bwd_kernel(traffic, u_ref, halo_ref, dt_ref, seg_ref, segr_ref, wk_ref, bias_ref, par_ref, skip_ref,
                save_ref, dy_ref, *rest):
     n_in, n_out = len(traffic.inputs), len(traffic.outputs)
     extra_in, rest = rest[:n_in], rest[n_in:]
@@ -371,8 +374,7 @@
     sg = sigmoid(raw)
     ratio = jnp.where(step > 1e-30, sg / jnp.maximum(step, 1e-30), 1.0)
     draw = total * ratio + rate * cross * sg
-    scale = jnp.broadcast_to(scale_ref[...], (Q, 128))
-    ddt_ref[...] = facts.back(draw * scale).astype(bf16)
+    ddt_ref[...] = facts.back(draw).astype(bf16)
     hgrad_ref[0:8, :] += jnp.sum(draw.reshape(Q // 8, 8, 128), axis=0)
     hgrad_ref[8:16, :] += jnp.sum((step * cross).reshape(Q // 8, 8, 128), axis=0)
 
@@ -389,7 +391,7 @@
             moved = own * (useen[8 - j : 8 - j + Q, lanes] * flags[j])
             k = 3 - j
             wgrad_ref[8 * k : 8 * k + 8, lanes] += jnp.sum(moved.reshape(Q // 8, 8, 128), axis=0)
-        du_ref[:, lanes] = (du * scale).astype(bf16)
+        du_ref[:, lanes] = du.astype(bf16)
     first = dpre[0:8, :]
     dpre[Q : Q + 8, :] = first
 
@@ -407,7 +409,7 @@
         small_ref[7:8, 0:128] = jnp.sum(by_head, axis=0, keepdims=True)
 
 
-def mixer_bwd(traffic, extra, u, dt, scale, seg, segr, wk, bias, par, skip, save, dy):
+def mixer_bwd(traffic, extra, u, dt, seg, segr, wk, bias, par, skip, save, dy):
     length, width = u.shape
     xw = width - 256
     n = length // Q
@@ -420,7 +422,6 @@
             pl.BlockSpec((Q, width), back),
             pl.BlockSpec((16, width), lambda i: (jnp.maximum((n - 1 - i) * (Q // 16) - 1, 0), 0)),
             pl.BlockSpec((Q, 128), back),
-            pl.BlockSpec((Q, 1), back),
             whole(seg.shape),
             pl.BlockSpec((1, 1, Q), lambda i: (n - 1 - i, 0, 0)),
             whole(wk.shape),
@@ -467,7 +468,7 @@
             has_side_effects=traffic.collective_id is not None,
         ),
         name="mixer_backward",
-    )(u, u, dt, scale, seg, segr, wk, bias, par, skip, save, dy, *extra)
+    )(u, u, dt, seg, segr, wk, bias, par, skip, save, dy, *extra)
 
 
 MESH = pl.DeviceIdType.MESH
@@ -495,10 +496,10 @@
         self.sib = (self.w, self.s_sib)
         self.far = (self.w, self.s_far)
 
-    def greet(self, everyone=False):
+    def greet(self, everyone=False, sequence=False):
         barrier = pltpu.get_barrier_semaphore()
         others = [(lax.rem(self.w + k, 8), self.s) for k in range(1, 8)] if everyone else []
-        if everyone:
+        if everyone or sequence:
             others += [(self.w, lax.rem(self.s + k, 4)) for k in range(1, 4)]
         else:
             others = [self.side, self.up, self.down, self.sib, self.far]
@@ -1159,6 +1160,165 @@
     return Traffic
 
 
+def mid_kernel(gate, mixed, cot, w_out, normed,
+               d_mixed, d_gate, gate_part, out_part, layer_part,
+               gate_v, mixed_v, cot_v, normed_v, w_v, a_v, low_v, dg_v, l_v, out_v, stats, got, *sems):
+    at = Place()
+    load, xsend, xrecv, store = sems
+    length, wide = mixed_v.shape
+    depth = cot_v.shape[1]
+    piece = length // 4
+    strips = wide // 128
+    tiles = piece // 256
+    part = lambda t: pl.ds(pl.multiple_of(t * 256, 256), 256)
+
+    def loads(k):
+        r = pl.ds(pl.multiple_of(k * piece, piece), piece)
+        pairs = ((cot, cot_v), (gate, gate_v), (mixed, mixed_v))
+        return [pltpu.make_async_copy(p.at[r], v.at[r], load.at[3 * k + n]) for n, (p, v) in enumerate(pairs)]
+
+    w_load = pltpu.make_async_copy(w_out, w_v, load.at[12])
+    normed_load = pltpu.make_async_copy(normed, normed_v, load.at[13])
+    w_load.start()
+    for k in range(4):
+        for copy in loads(k):
+            copy.start()
+    normed_load.start()
+    at.greet(sequence=True)
+
+    stats[...] = jnp.zeros_like(stats)
+    w_load.wait()
+
+    def first(i, _):
+        @pl.when(lax.rem(i, tiles) == 0)
+        def _():
+            for copy in loads(lax.div(i, tiles)):
+                copy.wait()
+
+        tile = part(i)
+        a_v[tile, :] = dot_nt(cot_v[tile, :], w_v[...])
+        sum_g, sum_a = jnp.zeros((256, 128), f32), jnp.zeros((256, 128), f32)
+        for n in range(strips):
+            col = slice(128 * n, 128 * n + 128)
+            gt = gate_v[tile, col]
+            g = mixed_v[tile, col].astype(f32) * (gt * sigmoid(gt))
+            sum_g = sum_g + g * g
+            sum_a = sum_a + a_v[tile, col] * g
+        stats[0:1, tile] = jnp.sum(sum_g.T, axis=0, keepdims=True)
+        stats[1:2, tile] = jnp.sum(sum_a.T, axis=0, keepdims=True)
+        return 0
+
+    lax.fori_loop(0, 4 * tiles, first, 0)
+
+    peers = (at.s_sib, at.s_far, at.s_diag)
+    swap = [remote(stats, got.at[k], xsend.at[k], xrecv.at[k], (at.w, s)) for k, s in enumerate(peers)]
+    for copy in swap:
+        copy.start()
+    for copy in swap:
+        copy.wait()
+    total = stats[...] + got[0] + got[1] + got[2]
+    r_row = lax.rsqrt(total[0:1] / E + eps)
+    stats[0:1, :] = r_row
+    stats[1:2, :] = r_row * r_row * r_row * (total[1:2] / E)
+
+    def column(k, at_row):
+        return jnp.broadcast_to(stats[k : k + 1, pl.ds(pl.multiple_of(at_row, 128), 256)], (128, 256)).T
+
+    def second(i, _):
+        tile = pl.ds(pl.multiple_of(i * 256, 256), 256)
+        r, pull = column(0, i * 256), column(1, i * 256)
+        for n in range(strips):
+            col = slice(128 * n, 128 * n + 128)
+            gt, mx = gate_v[tile, col], mixed_v[tile, col].astype(f32)
+            sg = sigmoid(gt)
+            silu = gt * sg
+            g = mx * silu
+            low_v[tile, col] = (g * r).astype(bf16)
+            d_g = r * a_v[tile, col] - g * pull
+            mixed_v[tile, col] = (d_g * silu).astype(bf16)
+            dg_v[tile, col] = (d_g * mx * (sg * (1.0 + gt * (1.0 - sg)))).astype(bf16)
+        l_v[tile, :] = dot(low_v[tile, :], w_v[...]).astype(bf16)
+        layer_copy(i).start()
+        return 0
+
+    layer_copy = lambda i: pltpu.make_async_copy(l_v.at[part(i)], layer_part.at[part(i)], store.at[9 + i])
+    lax.fori_loop(0, length // 256, second, 0)
+    keep = [pltpu.make_async_copy(mixed_v, d_mixed, store.at[0]), pltpu.make_async_copy(dg_v, d_gate, store.at[1])]
+    for copy in keep:
+        copy.start()
+    normed_load.wait()
+    tn = lambda p, q: lax.dot_general(p, q, (((0,), (0,)), ((), ())), preferred_element_type=f32)
+
+    def out_block(n):
+        room = out_v.at[part(n)]
+        return room, pltpu.make_async_copy(room, out_part.at[part(n)], store.at[2 + n])
+
+    def out_grad(n, _):
+        room, copy = out_block(n)
+        room[...] = tn(low_v[:, part(n)], cot_v[...]).astype(bf16)
+        copy.start()
+        return 0
+
+    lax.fori_loop(0, wide // 256, out_grad, 0)
+    shard = depth // 4
+    block = lambda n: pl.ds(pl.multiple_of(n * shard, shard), shard)
+    gate_block = lambda n: pltpu.make_async_copy(low_v.at[block(n)], gate_part.at[block(n)], store.at[5 + n])
+
+    def gate_grad(n, _):
+        low_v[block(n), :] = tn(normed_v[:, block(n)], dg_v[...]).astype(bf16)
+        gate_block(n).start()
+        return 0
+
+    lax.fori_loop(0, 4, gate_grad, 0)
+
+    for copy in keep:
+        copy.wait()
+    for n in range(wide // 256):
+        out_block(n)[1].wait()
+    for n in range(4):
+        gate_block(n).wait()
+    for i in range(length // 256):
+        layer_copy(i).wait()
+
+
+def middle(gate, mixed, cot, w_out, normed):
+    length, wide = mixed.shape
+    depth = cot.shape[1]
+    piece = length // 4
+    vm = pltpu.VMEM
+    low = lambda *shape: jax.ShapeDtypeStruct(shape, bf16)
+    return pl.pallas_call(
+        mid_kernel,
+        in_specs=[pl.BlockSpec(memory_space=ANY)] * 5,
+        out_specs=[pl.BlockSpec(memory_space=ANY)] * 5,
+        out_shape=[
+            low(length, wide),
+            low(length, wide),
+            low(depth, wide),
+            low(wide, depth),
+            low(length, depth),
+        ],
+        scratch_shapes=[
+            vm((length, wide), f32),
+            vm((length, wide), bf16),
+            vm((length, depth), bf16),
+            vm((length, depth), bf16),
+            vm((wide, depth), bf16),
+            vm((length, wide), f32),
+            vm((length, wide), bf16),
+            vm((length, wide), bf16),
+            vm((length, depth), bf16),
+            vm((wide, depth), bf16),
+        ]
+        + [vm((8, length), f32), vm((3, 8, length), f32)]
+        + [dma(14), dma(3), dma(3), dma(17)],
+        compiler_params=pltpu.CompilerParams(
+            collective_id=5, has_side_effects=True, vmem_limit_bytes=61 * 2**20
+        ),
+        name="middle",
+    )(gate, mixed, cot, w_out, normed)
+
+
 def small_start(at, small, got, sems):
     send, recv = sems
     for k in range(1, 8):
@@ -1491,6 +1651,27 @@
     return back_sum, in_sum, sums
 
 
+def middle_plain(gate, mixed, cot_all, w_out, normed):
+    mixed_wide = mixed.astype(f32)
+    sg = jax.nn.sigmoid(gate)
+    silu = gate * sg
+    g = mixed_wide * silu
+    g_low = g.astype(bf16)
+    a = lax.dot_general(cot_all, w_out, (((1,), (1,)), ((), ())), preferred_element_type=f32)
+    sums = lax.psum(jnp.stack([jnp.sum(g * g, axis=1), jnp.sum(a * g, axis=1)]), "seq")
+    r = lax.rsqrt(sums[0] / E + eps)[:, None]
+    pull = (r * r * r) * (sums[1] / E)[:, None]
+    d_g = r * a - g * pull
+    d_mixed = (d_g * silu).astype(bf16)
+    d_gate = (d_g * mixed_wide * (sg * (1.0 + gate * (1.0 - sg)))).astype(bf16)
+    layer_part = (jnp.dot(g_low, w_out, preferred_element_type=f32) * r).astype(bf16)
+    cot_r = (cot_all.astype(f32) * r).astype(bf16)
+    out_part = over_rows(g_low, cot_r).astype(bf16)
+
+    gate_part = over_rows(normed, d_gate).astype(bf16)
+    return d_mixed, d_gate, gate_part, out_part, layer_part
+
+
 def shards(
     hidden,
     segments,
@@ -1512,22 +1693,22 @@
     wide = heads * P_SIZE
     length = segments.shape[1]
     hidden_own, cot_own = hidden[0], cotangent[0]
-    in_gain = norm_gain.astype(f32)[:, None]
-    in_scaled = (in_weight.astype(f32) * in_gain).astype(bf16)
     main = jnp.concatenate(
         [
-            lax.dynamic_slice_in_dim(in_scaled, group * wide, wide, 1),
-            lax.dynamic_slice_in_dim(in_scaled, E + group * wide, wide, 1),
+            lax.dynamic_slice_in_dim(in_weight, group * wide, wide, 1),
+            lax.dynamic_slice_in_dim(in_weight, E + group * wide, wide, 1),
         ],
         axis=1,
     )
-    com = jnp.pad(in_scaled[:, 2 * E :], ((0, 0), (0, 128 - H)))
+    com = jnp.concatenate([in_weight[:, 2 * E :], norm_gain[:, None]], axis=1)
+    com = jnp.pad(com, ((0, 0), (0, 128 - H - 1)))
     out_gain = gate_gain.astype(f32)[:, None]
     out_scaled = (out_weight.astype(f32) * out_gain).astype(bf16)
     gather = gather_first if direct else gather_plain
     hidden_all, w_main, w_com = gather(hidden_own, main, com)
     hidden_all = hidden_all.reshape(length, D)
     w_main, w_com = w_main.reshape(D, 2 * wide), w_com.reshape(D, -1)
+    gain_row = w_com[:, 2 * N + H].astype(f32)[None]
 
     seg = segments[0]
     seg_col = jnp.pad(seg, (8, 8), constant_values=-1)[:, None]
@@ -1536,48 +1717,33 @@
     skip = jnp.repeat(skip_scale, P_SIZE)[None]
     facts = (seg_col, segr, conv_weight, conv_bias[None], par, skip)
     beside, more = (forward_traffic(cot_own, out_scaled), (cot_own, out_scaled)) if direct else (NoTraffic, ())
-    u, dt, gate, scale, mixed, save, *got = mixer_fwd(beside, more, hidden_all, w_main, w_com, *facts)
+    u, dt, gate, normed, mixed, save, *got = mixer_fwd(beside, more, hidden_all, gain_row, w_main, w_com, *facts)
     cot_all, w_out = got if direct else gather_more_plain(cot_own, out_scaled, wide)
     cot_all, w_out = cot_all.reshape(length, D), w_out.reshape(wide, D)
 
-    mixed_wide = mixed.astype(f32)
-    sg = jax.nn.sigmoid(gate)
-    silu = gate * sg
-    g = mixed_wide * silu
-    g_low = g.astype(bf16)
-    a = lax.dot_general(cot_all, w_out, (((1,), (1,)), ((), ())), preferred_element_type=f32)
-    sums = lax.psum(jnp.stack([jnp.sum(g * g, axis=1), jnp.sum(a * g, axis=1)]), "seq")
-    r = lax.rsqrt(sums[0] / E + eps)[:, None]
-    pull = (r * r * r) * (sums[1] / E)[:, None]
-    d_g = r * a - g * pull
-    d_mixed = (d_g * silu).astype(bf16)
-    d_gate = (d_g * mixed_wide * (sg * (1.0 + gate * (1.0 - sg))) * scale).astype(bf16)
-    layer_part = (jnp.dot(g_low, w_out, preferred_element_type=f32) * r).astype(bf16)
-    cot_r = (cot_all.astype(f32) * r).astype(bf16)
-    out_part = over_rows(g_low, cot_r).astype(bf16)
-
-    gate_part = over_rows(hidden_all, d_gate).astype(bf16)
-
-    layer_part, out_part = layer_part.reshape(groups, -1, D), out_part.reshape(2, -1, D)
-    gate_part = gate_part.reshape(owners, -1, wide)
-    more = (layer_part, out_part, gate_part) if direct else ()
+    mid = middle if direct else middle_plain
+    d_mixed, d_gate, gate_part, out_part, layer_part = mid(gate, mixed, cot_all, w_out, normed)
+    own_wide = hidden_own.astype(f32)
+
+    more = (layer_part.reshape(groups, -1, D), out_part.reshape(2, -1, D), gate_part.reshape(owners, -1, wide))
     beside = backward_traffic(*more) if direct else NoTraffic
-    du, ddt, small, *got = mixer_bwd(beside, more, u, dt, scale, *facts, save, d_mixed)
-    layer_sum, out_sum, gate_sum = got if direct else reduce_first_plain(*(layer_part, out_part, gate_part))
+    du, ddt, small, *got = mixer_bwd(
+        beside, more if direct else (), u, dt, *facts, save, d_mixed
+    )
+    layer_sum, out_sum, gate_sum = got if direct else reduce_first_plain(*more)
+    layer_output = own_wide + layer_sum
     finish = finish_last if direct else finish_plain
-    back_sum, in_sum, sums = finish(hidden_all, d_gate, du, ddt, w_main, w_com, gate_sum, small)
-
-    own_wide = hidden_own.astype(f32)
-    layer_output = own_wide + layer_sum
+    back_sum, in_sum, sums = finish(normed, d_gate, du, ddt, w_main, w_com, gate_sum, small)
+
     own_scale = lax.rsqrt(jnp.mean(own_wide * own_wide, axis=-1, keepdims=True) + eps)
+    b = back_sum * gain_row
     hidden_grad = (
         cot_own.astype(f32)
-        + back_sum
-        - own_wide * (own_scale * own_scale) * jnp.mean(back_sum * own_wide, axis=-1, keepdims=True)
+        + own_scale * b
+        - own_wide * (own_scale * own_scale * own_scale) * jnp.mean(b * own_wide, axis=-1, keepdims=True)
     )
-    in_sum = in_sum[:, : 2 * E + 2 * N + H].astype(f32)
-    in_weight_grad = in_sum * in_gain
-    norm_gain_grad = jnp.sum(in_sum * in_weight.astype(f32), axis=1)
+    in_weight_grad = in_sum[:, : 2 * E + 2 * N + H].astype(f32)
+    norm_gain_grad = jnp.sum(in_weight_grad * in_weight.astype(f32), axis=1) / norm_gain.astype(f32)
     out_sum = out_sum.astype(f32)
     out_weight_grad = out_sum * out_gain
     gate_gain_grad = jnp.sum(out_sum * out_weight.astype(f32), axis=1)

time: 350 us -> 335 us (0.957)
  matrix products: 42 us -> 0 us
  Pallas kernels: 252 us -> 293 us
  blocking collectives: 12.7 us -> 0 us
  local copies, waits for them, and re-layouts: 10.5 us -> 17.6 us
  other arithmetic: 25.6 us -> 19.9 us
    dot_general x4 -> x0, matrix products: 42 us -> none  [the longest x2 19.7 us: over_rows(): lax.dot_general(left, right, (((0,), (0,)), ((), ())), preferred_element_...]
    pallas_call x0 -> x1, Pallas kernels: none -> 40.4 us  [middle(): pl.pallas_call(mid_kernel, in_specs=[pl.BlockSpec(memory_space=ANY)] * 5,...]
    psum x1 -> x0, blocking collectives: 12.7 us -> none  [shards(): lax.psum(jnp.stack([jnp.sum(g * g, axis=1), jnp.sum(a * g, axis=1)]), 'seq')]
    convert_element_type x3 -> x1, other arithmetic: 6.76 us -> 1.3 us  [shards(): gain_row = w_com[:, 2 * N + H].astype(f32)[None]]
    unnamed x44 -> x42, local copies, waits for them, and re-layouts: 4.26 us -> 9.2 us
    mul x3 -> x0, other arithmetic: 3.98 us -> none  [the longest x1 3.97 us: shards(): in_weight_grad = in_sum * in_gain]
where the time goes in v5:
time: 335 us; the launch traced here: 332 us
  Pallas kernels  293 us (87%)
  other arithmetic  19.9 us (6%)
  local copies, waits for them, and re-layouts  17.6 us (5%)
    pallas_call x1, Pallas kernels, mixer_bwd(): pl.pallas_call(functools.partial(bwd_kernel, traffic), grid=(n,), in_spec...  68.1 us
    pallas_call x1, Pallas kernels, finish_last(): pl.pallas_call(last_kernel, in_specs=[pl.BlockSpec(memory_space=ANY)] * 7...  67.1 us
    pallas_call x1, Pallas kernels, gather_first(): pl.pallas_call(gather_kernel, in_specs=[pl.BlockSpec(memory_space=ANY)] *...  66.6 us
    pallas_call x1, Pallas kernels, mixer_fwd(): pl.pallas_call(functools.partial(fwd_kernel, traffic), grid=(n + 1,), in_...  51 us
    pallas_call x1, Pallas kernels, middle(): pl.pallas_call(mid_kernel, in_specs=[pl.BlockSpec(memory_space=ANY)] * 5,...  40.4 us
    unnamed x42, local copies, waits for them, and re-layouts  9.2 us

profile of v5, /device:TPU:0, one launch (start us, length us, event | category | flops | bytes accessed | tf_op | source)
XLA Modules:
  0.0 331.9 jit_solution(17709243307357827583)
XLA Ops:
  2.0 0.8 pad.13
  4.3 0.8 broadcast_in_dim.28
  5.2 0.9 slice.31
  6.9 1.3 constant_dynamic-slice_fusion.1
  8.2 0.9 pad_maximum_fusion.main
  9.4 1.3 fusion.6.rest_1_
  10.7 66.6 %gather_first.1 = (bf16[4,512,1536]{2,1,0:T(8,128)(2,1)}, bf16[8,192,1536]{2,1,0:T(8,128)(2,1)}, bf16[8,192,384]{2,1,0:T(8,128)(2,1)}) custom-call(bf16[512,1536]{1,0:T(8,128)(2,1)} %bitcast.39, bf16[192,1536]{1,0:T(8,128)(2,1)} %pad_maximum_fusion.main, bf16[192,384]{1,0:T(8,128)(2,1)} %fusion.10.com), custom_call_target="tpu_custom_call" | custom-call | tf_op jit(solution)/shard_map/gather_first/pallas_call | solution.py:681
  77.3 1.3 convert_reduce_fusion
  78.6 1.3 copy-done
  79.9 1.3 copy-done.2
  81.2 51.0 %mixer_forward.1 = (bf16[2048,1024]{1,0:T(8,128)(2,1)}, bf16[2048,128]{1,0:T(8,128)(2,1)S(1)}, f32[2048,768]{1,0:T(8,128)}, bf16[2048,1536]{1,0:T(8,128)(2,1)}, ...) custom-call(bf16[2048,1536]{1,0:T(8,128)(2,1)} %bitcast.40, ...), custom_call_target="tpu_custom_call" | custom-call | tf_op jit(solution)/shard_map/mixer_forward/pallas_call | solution.py:200
  132.2 0.8 copy-done.6
  133.0 40.4 %middle.1 = (bf16[2048,768]{1,0:T(8,128)(2,1)}, bf16[2048,768]{1,0:T(8,128)(2,1)}, bf16[1536,768]{1,0:T(8,128)(2,1)}, bf16[768,1536]{1,0:T(8,128)(2,1)}, bf16[2048,1536]{1,0:T(8,128)(2,1)}) custom-call(f32[2048,768]{1,0:T(8,128)} %get-tuple-element.42.gate, bf16[2048,768]{1,0:T(8,128)(2,1)} %get-tuple-element.43.mixed, bf16[2048,1536]{1,0:T(8,128)(2,1)} %bitcast.42, ...), custom_call_target="tpu_custom_call" | custom-call | tf_op jit(solution)/shard_map/middle/pallas_call | solution.py:1290
  173.4 1.7 copy-done.3
  175.0 1.0 copy-done.7
  176.1 68.1 %mixer_backward.1 = (bf16[2048,1024]{1,0:T(8,128)(2,1)}, bf16[2048,128]{1,0:T(8,128)(2,1)S(1)}, f32[8,1024]{1,0:T(8,128)S(1)}, f32[512,1536]{1,0:T(8,128)}, bf16...) custom-call(bf16[2048,1024]{1,0:T(8,128)(2,1)} %get-tuple-element.39.u_ref.halo_ref, ...), custom_call_target="tpu_custom_call" | custom-call | tf_op jit(solution)/shard_map/mixer_backward/pallas_call | solution.py:418
  244.2 1.0 copy-done.4
  245.2 0.8 copy-done.8
  247.4 67.1 %finish_last.1 = (f32[512,1536]{1,0:T(8,128)}, bf16[192,6528]{1,0:T(8,128)(2,1)}, f32[8,3456]{1,0:T(8,128)}) custom-call(bf16[2048,1536]{1,0:T(8,128)(2,1)} %get-tuple-element.46.normed.hid, bf16[2048,768]{1,0:T(8,128)(2,1)} %get-tuple-element.52.d_gate, bf16[2048,1024]{1,0:T(8,128)(2,1)} %get-tuple-element.53.d_u, bf16[2048,128]{1,0:T(8,128)(2,1)} %copy-done.8, ...), custom_call_target="tpu_custom_call" | custom-call | tf_op jit(solution)/shard_map/finish_last/pallas_call | solution.py:1561
  314.5 1.4 slice_bitcast_fusion
  315.9 2.6 fusion.1
  318.5 5.8 %fusion.4 = (f32[1,512,1536]{2,1,0:T(8,128)}, f32[1,512,1536]{2,1,0:T(8,128)}) fusion(f32[512,1536]{1,0:T(8,128)S(1)} %copy-done.14, f32[512]{0:T(512)S(1)} %get-tuple-element.76, f32[512]{0:T(512)S(1)} %get-tuple-element.75, f32[1536]{0:T(1024)S(1)} %convert_reduce_fusion, f32[512]{0:T(512)S(1)} %get-tuple-element.74, ...), kind=kLoop, calls=%fused_computation.9 | loop fusion | flops 7077888 | bytes 15740928 | tf_op jit(solution)/shard_map/broadcast_in_dim | solution.py:1753
  325.7 2.4 convert_multiply_fusion.3
  328.1 2.9 multiply_reduce_fusion
  (47 shorter events, 7.2 us)
Async XLA Ops:
  4.3 5.1 %copy-start.15 = (bf16[384,1536]{1,0:T(8,128)(2,1)S(1)}, bf16[384,1536]{1,0:T(8,128)(2,1)}, u32[]{:S(2)}) copy-start(bf16[384,1536]{1,0:T(8,128)(2,1)} %param.22) | copy-start | bytes 3538948
  9.1 69.6 %copy-start.1 = (bf16[1,512,1536]{2,1,0:T(8,128)(2,1)S(1)}, bf16[1,512,1536]{2,1,0:T(8,128)(2,1)}, u32[]{:S(2)}) copy-start(bf16[1,512,1536]{2,1,0:T(8,128)(2,1)} %param.23) | copy-start | bytes 4718596
  9.1 69.6 %copy-start.10 = (f32[4,3328]{1,0:T(4,128)S(1)}, f32[4,3328]{1,0:T(4,128)}, u32[]{:S(2)}) copy-start(f32[4,3328]{1,0:T(4,128)} %wk_ref.3) | copy-start | bytes 159748
  9.1 69.6 %copy-start.11 = (s32[1,2048]{1,0:T(1,128)S(1)}, s32[1,2048]{1,0:T(1,128)}, u32[]{:S(2)}) copy-start(s32[1,2048]{1,0:T(1,128)} %param.13) | copy-start | bytes 24580
  78.6 1.3 copy-start
  79.9 1.3 copy-start.2
  132.2 0.8 copy-start.6
  173.4 1.7 copy-start.3
  175.0 1.0 copy-start.7
  244.2 1.0 copy-start.4
  245.2 0.8 copy-start.8
  246.0 0.7 copy-start.9
  246.7 0.6 copy-start.12
  247.3 68.5 %copy-start.13 = (bf16[1,512,1536]{2,1,0:T(8,128)(2,1)S(1)}, bf16[1,512,1536]{2,1,0:T(8,128)(2,1)}, u32[]{:S(2)}) copy-start(bf16[1,512,1536]{2,1,0:T(8,128)(2,1)} %param.12) | copy-start | bytes 4718596
  314.5 4.0 %copy-start.14 = (f32[512,1536]{1,0:T(8,128)S(1)}, f32[512,1536]{1,0:T(8,128)}, u32[]{:S(2)}) copy-start(f32[512,1536]{1,0:T(8,128)} %get-tuple-element.57) | copy-start | bytes 9437188
  318.5 5.9 %copy-start.19 = (f32[8,3456]{1,0:T(8,128)S(1)}, f32[8,3456]{1,0:T(8,128)}, u32[]{:S(2)}) copy-start(f32[8,3456]{1,0:T(8,128)} %get-tuple-element.59) | copy-start | bytes 331780
  318.5 7.2 %copy-start.5 = (bf16[384,1536]{1,0:T(8,128)(2,1)S(1)}, bf16[384,1536]{1,0:T(8,128)(2,1)}, u32[]{:S(2)}) copy-start(bf16[384,1536]{1,0:T(8,128)(2,1)} %copy-done.4) | copy-start | bytes 3538948
  318.5 7.2 %copy-start.16 = (bf16[384,1536]{1,0:T(8,128)(2,1)S(1)}, bf16[384,1536]{1,0:T(8,128)(2,1)}, u32[]{:S(2)}) copy-start(bf16[384,1536]{1,0:T(8,128)(2,1)} %param.22) | copy-start | bytes 3538948
  318.5 9.6 %copy-start.18 = (bf16[192,6528]{1,0:T(8,128)(2,1)S(1)}, bf16[192,6528]{1,0:T(8,128)(2,1)}, u32[]{:S(2)}) copy-start(bf16[192,6528]{1,0:T(8,128)(2,1)} %get-tuple-element.58) | copy-start | bytes 7520260
  324.4 3.7 %copy-start.17 = (bf16[192,6448]{1,0:T(8,128)(2,1)S(1)}, bf16[192,6448]{1,0:T(8,128)(2,1)}, u32[]{:S(2)}) copy-start(bf16[192,6448]{1,0:T(8,128)(2,1)} %param.15) | copy-start | bytes 7428100
  328.1 2.9 copy-start.20

commit v6 on v5

--- a/solution.py
+++ b/solution.py
@@ -212,7 +212,7 @@
             whole(par.shape),
             whole(skip.shape),
         ]
-        + [pl.BlockSpec(memory_space=pl.ANY)] * len(extra),
+        + [pl.BlockSpec(memory_space=pltpu.MemorySpace.HBM)] * len(extra),
         out_specs=[
             pl.BlockSpec((Q, width), ahead),
             pl.BlockSpec((Q, 128), ahead),
@@ -221,7 +221,7 @@
             pl.BlockSpec((Q, xw), now),
             pl.BlockSpec((1, 128, xw), now3),
         ]
-        + [pl.BlockSpec(memory_space=pl.ANY)] * len(traffic.outputs),
+        + [pl.BlockSpec(memory_space=pltpu.MemorySpace.HBM)] * len(traffic.outputs),
         out_shape=[
             jax.ShapeDtypeStruct((length, width), bf16),
             jax.ShapeDtypeStruct((length, 128), bf16),
@@ -240,7 +240,7 @@
             *traffic.scratch,
         ],
         compiler_params=pltpu.CompilerParams(
-            vmem_limit_bytes=48 * 2**20,
+            vmem_limit_bytes=60 * 2**20,
             collective_id=traffic.collective_id,
             has_side_effects=traffic.collective_id is not None,
         ),
@@ -431,13 +431,13 @@
             pl.BlockSpec((1, 128, xw), lambda i: (n - 1 - i, 0, 0)),
             pl.BlockSpec((Q, xw), back),
         ]
-        + [pl.BlockSpec(memory_space=pl.ANY)] * len(extra),
+        + [pl.BlockSpec(memory_space=pltpu.MemorySpace.HBM)] * len(extra),
         out_specs=[
             pl.BlockSpec((Q, width), back),
             pl.BlockSpec((Q, 128), back),
             whole((8, width)),
         ]
-        + [pl.BlockSpec(memory_space=pl.ANY)] * len(traffic.outputs),
+        + [pl.BlockSpec(memory_space=pltpu.MemorySpace.HBM)] * len(traffic.outputs),
         out_shape=[
             jax.ShapeDtypeStruct((length, width), bf16),
             jax.ShapeDtypeStruct((length, 128), bf16),
@@ -463,7 +463,7 @@
             *traffic.scratch,
         ],
         compiler_params=pltpu.CompilerParams(
-            vmem_limit_bytes=48 * 2**20,
+            vmem_limit_bytes=60 * 2**20,
             collective_id=traffic.collective_id,
             has_side_effects=traffic.collective_id is not None,
         ),
@@ -472,7 +472,7 @@
 
 
 MESH = pl.DeviceIdType.MESH
-ANY = pl.ANY
+ANY = pltpu.MemorySpace.HBM
 PARTS = 4
 
 
@@ -552,11 +552,11 @@
         remote(diag, diag, send.at[2, k], recv.at[2, k], at.sib).wait_recv()
 
 
-CUTS = 2
+CUTS = 6
 
 
 def gather_shards(at, main, com, main_all, com_all, stage, sems, between):
-    send, recv, csend, crecv, psend, precv, local = sems
+    send, recv, csend, crecv, psend, precv, local, osend = sems
     half, cut = com.shape[0] // 2, main.shape[0] // CUTS
     mine = pl.ds(pl.multiple_of(at.c * half, half), half)
     load = pltpu.make_async_copy(main, stage[0], local.at[0])
@@ -568,9 +568,14 @@
         w, n, part = 2 * zp + at.x, zp * CUTS + q, pl.ds(q * cut, cut)
         slot, com_slot = main_all.at[w, part], com_all.at[w, mine]
         copies = [remote(main.at[part] if own else slot, slot, send.at[way, n], recv.at[w * CUTS + q], device)]
-        if q == 0:
+        if q == 1:
             copies.append(remote(com.at[mine] if own else com_slot, com_slot, csend.at[way, zp], crecv.at[w], device))
         return copies
+
+    def cross(zp, way, device):
+        w = 2 * zp + 1 - at.x
+        slot = main_all.at[w, pl.ds(0, cut)]
+        return [remote(slot, slot, osend.at[way, zp], recv.at[w * CUTS], device)]
 
     def begin(copies):
         for copy in copies:
@@ -594,14 +599,14 @@
     def arrived(w, q):
         slot = main_all.at[w, pl.ds(q * cut, cut)]
         remote(slot, slot, send.at[0, 0], recv.at[w * CUTS + q], at.side).wait_recv()
-        if q == 0:
+        if q == 1:
             held = com_all.at[w, mine]
             remote(held, held, csend.at[0, 0], crecv.at[w], at.side).wait_recv()
             remote(held, held, psend.at[w], precv.at[w], at.sib).start()
 
     for q in range(CUTS):
-        if q > 0:
-            all_ways(sent, q - 1)
+        if q > 1:
+            all_ways(sent, q - 2)
         all_ways(begin, q)
         if q == 0:
             load.start()
@@ -610,6 +615,16 @@
             com_load.wait()
             keep.start()
             com_keep.start()
+    arrived(2 * at.z + 1 - at.x, 0)
+
+    @pl.when(at.z < 3)
+    def _():
+        begin(cross(at.z, 0, at.up))
+
+    @pl.when(at.z > 0)
+    def _():
+        begin(cross(at.z, 1, at.down))
+
     for d in (1, 2, 3):
         if d == 3:
             between()
@@ -624,7 +639,8 @@
                 def _():
                     begin(hop(zp, q, 1, at.up))
 
-                begin(hop(zp, q, 0, at.side))
+                if q > 0:
+                    begin(hop(zp, q, 0, at.side))
 
             @pl.when(at.z + d <= 3)
             def _():
@@ -635,20 +651,48 @@
                 def _():
                     begin(hop(zp, q, 2, at.down))
 
-                begin(hop(zp, q, 0, at.side))
+                if q > 0:
+                    begin(hop(zp, q, 0, at.side))
+
+        @pl.when(at.z - d >= 0)
+        def _():
+            arrived(2 * (at.z - d) + 1 - at.x, 0)
+
+            @pl.when(at.z < 3)
+            def _():
+                begin(cross(at.z - d, 0, at.up))
+
+        @pl.when(at.z + d <= 3)
+        def _():
+            arrived(2 * (at.z + d) + 1 - at.x, 0)
+
+            @pl.when(at.z > 0)
+            def _():
+                begin(cross(at.z + d, 1, at.down))
 
     for zp in range(4):
-        for q in range(CUTS):
+        for q in range(1, CUTS):
             arrived(2 * zp + 1 - at.x, q)
     keep.wait()
     com_keep.wait()
+    all_ways(sent, CUTS - 2)
     all_ways(sent, CUTS - 1)
     for zp in range(4):
+
+        @pl.when((at.z < 3) & (zp <= at.z))
+        def _():
+            sent(cross(zp, 0, at.up))
+
+        @pl.when((at.z > 0) & (zp >= at.z))
+        def _():
+            sent(cross(zp, 1, at.down))
+
         for q in range(CUTS):
-
-            @pl.when(at.z != zp)
-            def _():
-                sent(hop(zp, q, 0, at.side))
+            if q > 0:
+
+                @pl.when(at.z != zp)
+                def _():
+                    sent(hop(zp, q, 0, at.side))
 
             @pl.when((at.z < 3) & (zp < at.z))
             def _():
@@ -672,7 +716,7 @@
     slot = lambda s: hid_all.at[s]
     gather_pieces_start(at, hid, slot, sems[0:3], hid_v)
     pass_on = lambda: gather_pieces_pass(at, hid, slot, sems[0:3])
-    gather_shards(at, main, com, main_all, com_all, (main_v, com_v), sems[3:10], pass_on)
+    gather_shards(at, main, com, main_all, com_all, (main_v, com_v), sems[3:11], pass_on)
     gather_pieces_end(at, hid, slot, sems[0:3])
 
 
@@ -685,7 +729,7 @@
         out_shape=[shape(4, hid), shape(8, main), shape(8, com)],
         scratch_shapes=[pltpu.VMEM(v.shape, v.dtype) for v in (hid, main, com)]
         + [dma(3, PARTS), dma(3, PARTS), dma()]
-        + [dma(3, 4 * CUTS), dma(8 * CUTS), dma(3, 4), dma(8), dma(8), dma(8), dma(2)],
+        + [dma(3, 4 * CUTS), dma(8 * CUTS), dma(3, 4), dma(8), dma(8), dma(8), dma(2), dma(2, 4)],
         compiler_params=pltpu.CompilerParams(collective_id=1, has_side_effects=True),
         name="gather_first",
     )(hid, main, com)

time: 335 us -> 328 us (0.979)
  local copies, waits for them, and re-layouts: 17.6 us -> 11.1 us
    unnamed x42 -> x18, local copies, waits for them, and re-layouts: 9.2 us -> 0.04 us
    pallas_call x1, Pallas kernels: 66.6 us -> 61.5 us  [gather_first(): pl.pallas_call(gather_kernel, in_specs=[pl.BlockSpec(memory_space=ANY)] *...]
where the time goes in v6:
time: 328 us; the launch traced here: 325 us
  Pallas kernels  292 us (89%)
  other arithmetic  20.6 us (6%)
  local copies, waits for them, and re-layouts  11.1 us (3%)
    pallas_call x1, Pallas kernels, mixer_bwd(): pl.pallas_call(functools.partial(bwd_kernel, traffic), grid=(n,), in_spec...  68.5 us
    pallas_call x1, Pallas kernels, finish_last(): pl.pallas_call(last_kernel, in_specs=[pl.BlockSpec(memory_space=ANY)] * 7...  66.8 us
    pallas_call x1, Pallas kernels, gather_first(): pl.pallas_call(gather_kernel, in_specs=[pl.BlockSpec(memory_space=ANY)] *...  61.5 us
    pallas_call x1, Pallas kernels, mixer_fwd(): pl.pallas_call(functools.partial(fwd_kernel, traffic), grid=(n + 1,), in_...  54 us
    pallas_call x1, Pallas kernels, middle(): pl.pallas_call(mid_kernel, in_specs=[pl.BlockSpec(memory_space=ANY)] * 5,...  41.3 us

profile of v6, /device:TPU:0, one launch (start us, length us, event | category | flops | bytes accessed | tf_op | source)
XLA Modules:
  0.0 324.9 jit_solution(1331630087156377022)
XLA Ops:
  0.7 0.8 convert_element_type.55
  1.4 1.3 select_maximum_fusion.par_ref
  2.7 0.8 pad.13
  3.5 1.3 broadcast_in_dim.24.bias_ref
  4.8 0.7 broadcast_in_dim.25
  5.5 0.7 broadcast_in_dim_reshape.3.skip_ref
  6.2 0.7 broadcast_in_dim.28
  7.0 0.9 slice.31
  7.9 0.8 fusion.10.com
  8.7 1.3 constant_dynamic-slice_fusion.1
  10.0 0.9 pad_maximum_fusion.main
  10.8 1.3 broadcast_in_dim.29.seg_ref
  12.1 1.3 fusion.6.rest_1_
  13.4 61.5 %gather_first.1 = (bf16[4,512,1536]{2,1,0:T(8,128)(2,1)}, bf16[8,192,1536]{2,1,0:T(8,128)(2,1)}, bf16[8,192,384]{2,1,0:T(8,128)(2,1)}) custom-call(bf16[512,1536]{1,0:T(8,128)(2,1)} %bitcast.31, bf16[192,1536]{1,0:T(8,128)(2,1)} %pad_maximum_fusion.main, bf16[192,384]{1,0:T(8,128)(2,1)} %fusion.10.com), custom_call_target="tpu_custom_call" | custom-call | tf_op jit(solution)/shard_map/gather_first/pallas_call | solution.py:725
  74.9 1.3 convert_reduce_fusion
  76.8 54.0 %mixer_forward.1 = (bf16[2048,1024]{1,0:T(8,128)(2,1)}, bf16[2048,128]{1,0:T(8,128)(2,1)}, f32[2048,768]{1,0:T(8,128)}, bf16[2048,1536]{1,0:T(8,128)(2,1)}, bf16...) custom-call(bf16[2048,1536]{1,0:T(8,128)(2,1)} %bitcast.35, ...), custom_call_target="tpu_custom_call" | custom-call | tf_op jit(solution)/shard_map/mixer_forward/pallas_call | solution.py:200
  130.9 41.3 %middle.1 = (bf16[2048,768]{1,0:T(8,128)(2,1)}, bf16[2048,768]{1,0:T(8,128)(2,1)}, bf16[1536,768]{1,0:T(8,128)(2,1)}, bf16[768,1536]{1,0:T(8,128)(2,1)}, bf16[2048,1536]{1,0:T(8,128)(2,1)}) custom-call(f32[2048,768]{1,0:T(8,128)} %get-tuple-element.42.gate, bf16[2048,768]{1,0:T(8,128)(2,1)} %get-tuple-element.43.mixed, bf16[2048,1536]{1,0:T(8,128)(2,1)} %bitcast.38, ...), custom_call_target="tpu_custom_call" | custom-call | tf_op jit(solution)/shard_map/middle/pallas_call | solution.py:1334
  172.2 68.5 %mixer_backward.1 = (bf16[2048,1024]{1,0:T(8,128)(2,1)}, bf16[2048,128]{1,0:T(8,128)(2,1)}, f32[8,1024]{1,0:T(8,128)}, f32[512,1536]{1,0:T(8,128)}, bf16[384,1536]{1,0:T(8,128)(2,1)}, /*index=5*/bf16[192,768]{1,0:T(8,128)(2,1)}) custom-call(bf16[2048,1024]{1,0:T(8,128)(2,1)} %get-tuple-element.39.u_ref.halo_ref, ...), custom_call_target="tpu_custom_call" | custom-call | tf_op jit(solution)/shard_map/mixer_backward/pallas_call | solution.py:418
  240.7 66.8 %finish_last.1 = (f32[512,1536]{1,0:T(8,128)}, bf16[192,6528]{1,0:T(8,128)(2,1)}, f32[8,3456]{1,0:T(8,128)}) custom-call(bf16[2048,1536]{1,0:T(8,128)(2,1)} %get-tuple-element.46.normed.hid, bf16[2048,768]{1,0:T(8,128)(2,1)} %get-tuple-element.52.d_gate, bf16[2048,1024]{1,0:T(8,128)(2,1)} %get-tuple-element.53.d_u, ...), custom_call_target="tpu_custom_call" | custom-call | tf_op jit(solution)/shard_map/finish_last/pallas_call | solution.py:1605
  307.5 1.4 slice_bitcast_fusion
  308.9 2.6 fusion.1
  311.6 5.8 %fusion.4 = (f32[1,512,1536]{2,1,0:T(8,128)}, f32[1,512,1536]{2,1,0:T(8,128)}) fusion(f32[512,1536]{1,0:T(8,128)S(1)} %copy-done.1, f32[512]{0:T(512)S(1)} %get-tuple-element.76, f32[512]{0:T(512)S(1)} %get-tuple-element.75, f32[1536]{0:T(1024)S(1)} %convert_reduce_fusion, f32[512]{0:T(512)S(1)} %get-tuple-element.74, bf16[1,512,1536]{2,1,0:T(8,128)(2,1)S(1)} %copy-done.2, ...), kind=kLoop, calls=%fused_computation.9 | loop fusion | flops 7077888 | bytes 15740928 | tf_op jit(solution)/shard_map/broadcast_in_dim | solution.py:1797
  318.7 2.5 convert_multiply_fusion.3
  321.1 2.9 multiply_reduce_fusion
  (23 shorter events, 2.5 us)
Async XLA Ops:
  0.6 11.5 %copy-start.3 = (bf16[384,1536]{1,0:T(8,128)(2,1)S(1)}, bf16[384,1536]{1,0:T(8,128)(2,1)}, u32[]{:S(2)}) copy-start(bf16[384,1536]{1,0:T(8,128)(2,1)} %param.22) | copy-start | bytes 3538948
  240.7 68.2 %copy-start = (bf16[1,512,1536]{2,1,0:T(8,128)(2,1)S(1)}, bf16[1,512,1536]{2,1,0:T(8,128)(2,1)}, u32[]{:S(2)}) copy-start(bf16[1,512,1536]{2,1,0:T(8,128)(2,1)} %param.12) | copy-start | bytes 4718596
  307.5 4.0 %copy-start.1 = (f32[512,1536]{1,0:T(8,128)S(1)}, f32[512,1536]{1,0:T(8,128)}, u32[]{:S(2)}) copy-start(f32[512,1536]{1,0:T(8,128)} %get-tuple-element.57) | copy-start | bytes 9437188
  307.5 4.0 %copy-start.2 = (bf16[1,512,1536]{2,1,0:T(8,128)(2,1)S(1)}, bf16[1,512,1536]{2,1,0:T(8,128)(2,1)}, u32[]{:S(2)}) copy-start(bf16[1,512,1536]{2,1,0:T(8,128)(2,1)} %param.23) | copy-start | bytes 4718596
  311.6 5.8 %copy-start.7 = (f32[8,3456]{1,0:T(8,128)S(1)}, f32[8,3456]{1,0:T(8,128)}, u32[]{:S(2)}) copy-start(f32[8,3456]{1,0:T(8,128)} %get-tuple-element.59) | copy-start | bytes 331780
  311.6 7.1 %copy-start.6 = (bf16[384,1536]{1,0:T(8,128)(2,1)S(1)}, bf16[384,1536]{1,0:T(8,128)(2,1)}, u32[]{:S(2)}) copy-start(bf16[384,1536]{1,0:T(8,128)(2,1)} %get-tuple-element.60) | copy-start | bytes 3538948
  311.6 9.5 %copy-start.5 = (bf16[192,6528]{1,0:T(8,128)(2,1)S(1)}, bf16[192,6528]{1,0:T(8,128)(2,1)}, u32[]{:S(2)}) copy-start(bf16[192,6528]{1,0:T(8,128)(2,1)} %get-tuple-element.58) | copy-start | bytes 7520260
  317.4 3.7 %copy-start.4 = (bf16[192,6448]{1,0:T(8,128)(2,1)S(1)}, bf16[192,6448]{1,0:T(8,128)(2,1)}, u32[]{:S(2)}) copy-start(bf16[192,6448]{1,0:T(8,128)(2,1)} %param.15) | copy-start | bytes 7428100
  321.1 2.9 copy-start.8

commit v7 on v6

--- a/solution.py
+++ b/solution.py
@@ -1394,12 +1394,12 @@
         remote(total, full.at[s], send2.at[k], recv2.at[k], (at.w, s)).wait_recv()
 
 
-def last_kernel(hid, d_gate, d_u, d_dt, w_main, w_com, gate_sum, small,
-                back_sum, in_sum, sums_out,
+def last_kernel(hid, d_gate, d_u, d_dt, w_main, w_com, gate_sum, own, cot, small, gain_ref,
+                hidden_grad, in_sum, sums_out,
                 hid_v, dp_v, w_v,
                 b_diag, b_sib, b_far, b_own, from_sib, pass_sib, from_far,
                 part_v, mside, mlow, mhigh, macc, mown, csib, cown, cacc, cside, clow, chigh, cfar, csum,
-                sgot, stotal, sfull, gate_v, *sems):
+                sgot, stotal, sfull, gate_v, own_v, cot_v, *sems):
     at = Place()
     sems = list(sems)
     take = lambda n: [sems.pop(0) for _ in range(n)]
@@ -1432,7 +1432,11 @@
         )
     hid_load = pltpu.make_async_copy(hid, hid_v, load[4])
     soon, later = weights + loads[0] + loads[1], [hid_load] + loads[2] + loads[3]
-    for copy in soon + later:
+    ends_loads = [
+        pltpu.make_async_copy(own, own_v, load[5].at[0]),
+        pltpu.make_async_copy(cot, cot_v, load[5].at[1]),
+    ]
+    for copy in soon + later + ends_loads:
         copy.start()
     gate_slot = lambda s: in_sum.at[:, pl.ds(pl.multiple_of(s * wide, 128), wide)]
     x_slot = lambda s: in_sum.at[:, pl.ds(pl.multiple_of(E + s * wide, 128), wide)]
@@ -1553,13 +1557,22 @@
     csum[...] = cacc[at.z]
     far_copy = remote(csum, cfar, cx[2], cx[3], at.far)
     far_copy.start()
+    for copy in ends_loads:
+        copy.wait()
     for k, p in enumerate(parts):
         to_sib[k].wait_recv()
         to_far[k].wait_recv()
 
         def body(i, _):
             r = pl.ds(pl.multiple_of(k * rows + i * 32, 32), 32)
-            back_sum[r, :] = b_own[r, :].astype(f32) + from_sib[r, :].astype(f32) + from_far[r, :].astype(f32)
+            total = b_own[r, :].astype(f32) + from_sib[r, :].astype(f32) + from_far[r, :].astype(f32)
+            back, wide_own = total * gain_ref[...], own_v[r, :].astype(f32)
+            depth = wide_own.shape[1]
+            scale = lax.rsqrt(jnp.sum(wide_own * wide_own, axis=1, keepdims=True) / depth + eps)
+            along = jnp.sum(back * wide_own, axis=1, keepdims=True) / depth
+            hidden_grad[r, :] = (
+                cot_v[r, :].astype(f32) + scale * back - wide_own * (scale * scale * scale * along)
+            )
             return 0
 
         lax.fori_loop(0, rows // 32, body, 0)
@@ -1596,7 +1609,7 @@
     remote(csum, got, cx[4], cx[5], at.sib).wait_recv()
 
 
-def finish_last(hid, d_gate, d_u, d_dt, w_main, w_com, gate_sum, small):
+def finish_last(hid, d_gate, d_u, d_dt, w_main, w_com, gate_sum, own, cot, small, gain):
     length, depth = hid.shape
     piece, shard, half = length // 4, depth // 8, depth // 16
     wide = d_gate.shape[1]
@@ -1604,7 +1617,7 @@
     shards4 = lambda cuts: [dma(3, 4 * cuts), dma(4 * cuts), dma(4 * cuts), dma(4 * cuts)]
     return pl.pallas_call(
         last_kernel,
-        in_specs=[pl.BlockSpec(memory_space=ANY)] * 7 + [pl.BlockSpec(memory_space=pltpu.VMEM)],
+        in_specs=[pl.BlockSpec(memory_space=ANY)] * 9 + [pl.BlockSpec(memory_space=pltpu.VMEM)] * 2,
         out_specs=[
             pl.BlockSpec(memory_space=pltpu.VMEM),
             pl.BlockSpec(memory_space=ANY),
@@ -1624,7 +1637,8 @@
         + [vm((4, half, 384), bf16)] * 4
         + [vm((half, 384), bf16)] * 2
         + [vm((8,) + small.shape, f32), vm(small.shape, f32), vm((4,) + small.shape, f32), vm(gate_sum.shape, bf16)]
-        + [dma(2), dma(4), dma(4), dma(4), dma(), dma()]
+        + [vm((piece, depth), bf16)] * 2
+        + [dma(2), dma(4), dma(4), dma(4), dma(), dma(2)]
         + [dma(3, PARTS), dma(3, PARTS)]
         + shards4(2)
         + shards4(1)
@@ -1637,7 +1651,7 @@
             collective_id=4, has_side_effects=True, vmem_limit_bytes=60 * 2**20
         ),
         name="finish_last",
-    )(hid, d_gate, d_u, d_dt, w_main, w_com, gate_sum, small)
+    )(hid, d_gate, d_u, d_dt, w_main, w_com, gate_sum, own, cot, small, gain)
 
 
 def over_rows(left, right):
@@ -1672,7 +1686,7 @@
     return layer_sum, part, reduce_scattered(gate, "wshard")
 
 
-def finish_plain(hid, d_gate, d_u, d_dt, w_main, w_com, gate_sum, small):
+def finish_plain(hid, d_gate, d_u, d_dt, w_main, w_com, gate_sum, own, cot, small, gain):
     groups, owners = lax.axis_size("seq"), lax.axis_size("wshard")
     wide = d_gate.shape[1]
     rest = jnp.concatenate([d_u, d_dt], axis=1)
@@ -1692,7 +1706,15 @@
     sums = jnp.concatenate(
         [full[i, :, :wide] for i in range(groups)] + [jnp.sum(full[:, :, wide:], axis=0), sum(turned)], axis=1
     )
-    return back_sum, in_sum, sums
+    wide_own = own.astype(f32)
+    own_scale = lax.rsqrt(jnp.mean(wide_own * wide_own, axis=-1, keepdims=True) + eps)
+    b = back_sum * gain
+    hidden_grad = (
+        cot.astype(f32)
+        + own_scale * b
+        - wide_own * (own_scale * own_scale * own_scale) * jnp.mean(b * wide_own, axis=-1, keepdims=True)
+    )
+    return hidden_grad, in_sum, sums
 
 
 def middle_plain(gate, mixed, cot_all, w_out, normed):
@@ -1777,15 +1799,10 @@
     layer_sum, out_sum, gate_sum = got if direct else reduce_first_plain(*more)
     layer_output = own_wide + layer_sum
     finish = finish_last if direct else finish_plain
-    back_sum, in_sum, sums = finish(normed, d_gate, du, ddt, w_main, w_com, gate_sum, small)
-
-    own_scale = lax.rsqrt(jnp.mean(own_wide * own_wide, axis=-1, keepdims=True) + eps)
-    b = back_sum * gain_row
-    hidden_grad = (
-        cot_own.astype(f32)
-        + own_scale * b
-        - own_wide * (own_scale * own_scale * own_scale) * jnp.mean(b * own_wide, axis=-1, keepdims=True)
+    hidden_grad, in_sum, sums = finish(
+        normed, d_gate, du, ddt, w_main, w_com, gate_sum, hidden_own, cot_own, small, gain_row
     )
+
     in_weight_grad = in_sum[:, : 2 * E + 2 * N + H].astype(f32)
     norm_gain_grad = jnp.sum(in_weight_grad * in_weight.astype(f32), axis=1) / norm_gain.astype(f32)
     out_sum = out_sum.astype(f32)

time: 328 us -> 326 us (level)
  other arithmetic: 20.6 us -> 16.4 us
where the time goes in v7:
time: 326 us; the launch traced here: 322 us
  Pallas kernels  293 us (90%)
  other arithmetic  16.4 us (5%)
  local copies, waits for them, and re-layouts  11.9 us (4%)
    pallas_call x1, Pallas kernels, mixer_bwd(): pl.pallas_call(functools.partial(bwd_kernel, traffic), grid=(n,), in_spec...  68.7 us
    pallas_call x1, Pallas kernels, finish_last(): pl.pallas_call(last_kernel, in_specs=[pl.BlockSpec(memory_space=ANY)] * 9...  67.6 us
    pallas_call x1, Pallas kernels, gather_first(): pl.pallas_call(gather_kernel, in_specs=[pl.BlockSpec(memory_space=ANY)] *...  61.5 us
    pallas_call x1, Pallas kernels, mixer_fwd(): pl.pallas_call(functools.partial(fwd_kernel, traffic), grid=(n + 1,), in_...  53.7 us
    pallas_call x1, Pallas kernels, middle(): pl.pallas_call(mid_kernel, in_specs=[pl.BlockSpec(memory_space=ANY)] * 5,...  41.3 us

profile of v7, /device:TPU:0, one launch (start us, length us, event | category | flops | bytes accessed | tf_op | source)
XLA Modules:
  0.0 322.1 jit_solution(1320911899248488570)
XLA Ops:
  0.7 0.8 convert_element_type.46
  1.4 1.3 select_maximum_fusion.par_ref
  2.7 0.8 pad.13
  3.5 1.3 broadcast_in_dim.22.bias_ref
  4.8 0.7 broadcast_in_dim.23
  5.5 0.7 broadcast_in_dim_reshape.3.skip_ref
  6.2 0.7 broadcast_in_dim.26
  7.0 0.9 slice.31
  7.9 0.8 fusion.4.com
  8.6 1.3 constant_dynamic-slice_fusion.1
  10.0 0.9 pad_maximum_fusion.main
  10.8 1.3 broadcast_in_dim.27.seg_ref
  12.1 1.3 fusion.rest_1_
  13.4 61.5 %gather_first.1 = (bf16[4,512,1536]{2,1,0:T(8,128)(2,1)}, bf16[8,192,1536]{2,1,0:T(8,128)(2,1)}, bf16[8,192,384]{2,1,0:T(8,128)(2,1)}) custom-call(bf16[512,1536]{1,0:T(8,128)(2,1)} %bitcast.26, bf16[192,1536]{1,0:T(8,128)(2,1)} %pad_maximum_fusion.main, bf16[192,384]{1,0:T(8,128)(2,1)} %fusion.4.com), custom_call_target="tpu_custom_call" | custom-call | tf_op jit(solution)/shard_map/gather_first/pallas_call | solution.py:725
  74.9 1.3 convert_reduce_fusion
  76.8 53.7 %mixer_forward.1 = (bf16[2048,1024]{1,0:T(8,128)(2,1)}, bf16[2048,128]{1,0:T(8,128)(2,1)}, f32[2048,768]{1,0:T(8,128)}, bf16[2048,1536]{1,0:T(8,128)(2,1)}, bf16...) custom-call(bf16[2048,1536]{1,0:T(8,128)(2,1)} %bitcast.31, ...), custom_call_target="tpu_custom_call" | custom-call | tf_op jit(solution)/shard_map/mixer_forward/pallas_call | solution.py:200
  130.5 41.3 %middle.1 = (bf16[2048,768]{1,0:T(8,128)(2,1)}, bf16[2048,768]{1,0:T(8,128)(2,1)}, bf16[1536,768]{1,0:T(8,128)(2,1)}, bf16[768,1536]{1,0:T(8,128)(2,1)}, bf16[2048,1536]{1,0:T(8,128)(2,1)}) custom-call(f32[2048,768]{1,0:T(8,128)} %get-tuple-element.42.gate, bf16[2048,768]{1,0:T(8,128)(2,1)} %get-tuple-element.43.mixed, bf16[2048,1536]{1,0:T(8,128)(2,1)} %bitcast.35, ...), custom_call_target="tpu_custom_call" | custom-call | tf_op jit(solution)/shard_map/middle/pallas_call | solution.py:1334
  171.8 68.7 %mixer_backward.1 = (bf16[2048,1024]{1,0:T(8,128)(2,1)}, bf16[2048,128]{1,0:T(8,128)(2,1)}, f32[8,1024]{1,0:T(8,128)}, f32[512,1536]{1,0:T(8,128)}, bf16[384,1536]{1,0:T(8,128)(2,1)}, /*index=5*/bf16[192,768]{1,0:T(8,128)(2,1)}) custom-call(bf16[2048,1024]{1,0:T(8,128)(2,1)} %get-tuple-element.39.u_ref.halo_ref, ...), custom_call_target="tpu_custom_call" | custom-call | tf_op jit(solution)/shard_map/mixer_backward/pallas_call | solution.py:418
  240.5 67.6 %finish_last.1 = (f32[512,1536]{1,0:T(8,128)}, bf16[192,6528]{1,0:T(8,128)(2,1)}, f32[8,3456]{1,0:T(8,128)}) custom-call(bf16[2048,1536]{1,0:T(8,128)(2,1)} %get-tuple-element.46.normed.hid, bf16[2048,768]{1,0:T(8,128)(2,1)} %get-tuple-element.52.d_gate, bf16[2048,1024]{1,0:T(8,128)(2,1)} %get-tuple-element.53.d_u, ...), custom_call_target="tpu_custom_call" | custom-call | tf_op jit(solution)/shard_map/finish_last/pallas_call | solution.py:1618
  308.1 4.2 %add_bitcast_fusion = f32[1,512,1536]{2,1,0:T(8,128)} fusion(f32[512,1536]{1,0:T(8,128)} %get-tuple-element.51, bf16[1,512,1536]{2,1,0:T(8,128)(2,1)S(1)} %copy-done), kind=kLoop, calls=%fused_computation.1 | loop fusion | flops 1572864 | bytes 7864320 | tf_op jit(solution)/shard_map/broadcast_in_dim | solution.py:1813
  312.7 0.6 slice_reduce_fusion
  314.0 2.5 convert_multiply_fusion
  316.5 2.9 multiply_reduce_fusion
  320.0 1.7 copy.27
  (20 shorter events, 2.4 us)
Async XLA Ops:
  0.6 11.5 %copy-start.1 = (bf16[384,1536]{1,0:T(8,128)(2,1)S(1)}, bf16[384,1536]{1,0:T(8,128)(2,1)}, u32[]{:S(2)}) copy-start(bf16[384,1536]{1,0:T(8,128)(2,1)} %param.22) | copy-start | bytes 3538948
  240.4 67.6 %copy-start = (bf16[1,512,1536]{2,1,0:T(8,128)(2,1)S(1)}, bf16[1,512,1536]{2,1,0:T(8,128)(2,1)}, u32[]{:S(2)}) copy-start(bf16[1,512,1536]{2,1,0:T(8,128)(2,1)} %param.12) | copy-start | bytes 4718596
  308.0 4.2 %copy-start.6 = (f32[8,3456]{1,0:T(8,128)S(1)}, f32[8,3456]{1,0:T(8,128)}, u32[]{:S(2)}) copy-start(f32[8,3456]{1,0:T(8,128)} %get-tuple-element.59) | copy-start | bytes 331780
  308.0 6.0 %copy-start.5 = (bf16[384,1536]{1,0:T(8,128)(2,1)S(1)}, bf16[384,1536]{1,0:T(8,128)(2,1)}, u32[]{:S(2)}) copy-start(bf16[384,1536]{1,0:T(8,128)(2,1)} %get-tuple-element.60) | copy-start | bytes 3538948
  308.1 8.4 %copy-start.4 = (bf16[192,6528]{1,0:T(8,128)(2,1)S(1)}, bf16[192,6528]{1,0:T(8,128)(2,1)}, u32[]{:S(2)}) copy-start(bf16[192,6528]{1,0:T(8,128)(2,1)} %get-tuple-element.58) | copy-start | bytes 7520260
  312.2 4.3 %copy-start.2 = (bf16[192,6448]{1,0:T(8,128)(2,1)S(1)}, bf16[192,6448]{1,0:T(8,128)(2,1)}, u32[]{:S(2)}) copy-start(bf16[192,6448]{1,0:T(8,128)(2,1)} %param.15) | copy-start | bytes 7428100
  316.5 2.9 copy-start.7
  316.5 3.5 %copy-start.3 = (f32[512,1536]{1,0:T(8,128)S(1)}, f32[512,1536]{1,0:T(8,128)}, u32[]{:S(2)}) copy-start(f32[512,1536]{1,0:T(8,128)} %get-tuple-element.57) | copy-start | bytes 9437188

commit v8 on v7

--- a/solution.py
+++ b/solution.py
@@ -1136,7 +1136,7 @@
                 self.gates.side_copy(g).start()
 
             inner = jnp.where((at.z == 1) | (at.z == 2), 1, 0)
-            g = i - 11 - inner
+            g = i - 12 - inner
 
             @pl.when(g >= 0)
             def _():
@@ -1148,7 +1148,7 @@
                     self.gates.step(k)
                     return 0
 
-                lax.fori_loop(last - 10 - inner, 8, rest, 0)
+                lax.fori_loop(last - 11 - inner, 8, rest, 0)
 
                 self.store.start()
                 self.store_gate.start()

time: 326 us -> 329 us (level)
  Pallas kernels: 293 us -> 297 us
where the time goes in v8:
time: 329 us; the launch traced here: 326 us
  Pallas kernels  297 us (90%)
  other arithmetic  16.4 us (5%)
  local copies, waits for them, and re-layouts  11.9 us (4%)
    pallas_call x1, Pallas kernels, mixer_bwd(): pl.pallas_call(functools.partial(bwd_kernel, traffic), grid=(n,), in_spec...  71 us
    pallas_call x1, Pallas kernels, finish_last(): pl.pallas_call(last_kernel, in_specs=[pl.BlockSpec(memory_space=ANY)] * 9...  69.2 us
    pallas_call x1, Pallas kernels, gather_first(): pl.pallas_call(gather_kernel, in_specs=[pl.BlockSpec(memory_space=ANY)] *...  61.5 us
    pallas_call x1, Pallas kernels, mixer_fwd(): pl.pallas_call(functools.partial(fwd_kernel, traffic), grid=(n + 1,), in_...  53.7 us
    pallas_call x1, Pallas kernels, middle(): pl.pallas_call(mid_kernel, in_specs=[pl.BlockSpec(memory_space=ANY)] * 5,...  41.3 us

profile of v8, /device:TPU:0, one launch (start us, length us, event | category | flops | bytes accessed | tf_op | source)
XLA Modules:
  0.0 326.0 jit_solution(2044430724709870565)
XLA Ops:
  0.7 0.8 convert_element_type.46
  1.4 1.3 select_maximum_fusion.par_ref
  2.7 0.8 pad.13
  3.5 1.3 broadcast_in_dim.22.bias_ref
  4.8 0.7 broadcast_in_dim.23
  5.5 0.7 broadcast_in_dim_reshape.3.skip_ref
  6.2 0.7 broadcast_in_dim.26
  7.0 0.9 slice.31
  7.9 0.8 fusion.4.com
  8.6 1.3 constant_dynamic-slice_fusion.1
  10.0 0.9 pad_maximum_fusion.main
  10.8 1.3 broadcast_in_dim.27.seg_ref
  12.1 1.3 fusion.rest_1_
  13.4 61.5 %gather_first.1 = (bf16[4,512,1536]{2,1,0:T(8,128)(2,1)}, bf16[8,192,1536]{2,1,0:T(8,128)(2,1)}, bf16[8,192,384]{2,1,0:T(8,128)(2,1)}) custom-call(bf16[512,1536]{1,0:T(8,128)(2,1)} %bitcast.26, bf16[192,1536]{1,0:T(8,128)(2,1)} %pad_maximum_fusion.main, bf16[192,384]{1,0:T(8,128)(2,1)} %fusion.4.com), custom_call_target="tpu_custom_call" | custom-call | tf_op jit(solution)/shard_map/gather_first/pallas_call | solution.py:725
  74.9 1.3 convert_reduce_fusion
  76.8 53.7 %mixer_forward.1 = (bf16[2048,1024]{1,0:T(8,128)(2,1)}, bf16[2048,128]{1,0:T(8,128)(2,1)}, f32[2048,768]{1,0:T(8,128)}, bf16[2048,1536]{1,0:T(8,128)(2,1)}, bf16...) custom-call(bf16[2048,1536]{1,0:T(8,128)(2,1)} %bitcast.31, ...), custom_call_target="tpu_custom_call" | custom-call | tf_op jit(solution)/shard_map/mixer_forward/pallas_call | solution.py:200
  130.5 41.3 %middle.1 = (bf16[2048,768]{1,0:T(8,128)(2,1)}, bf16[2048,768]{1,0:T(8,128)(2,1)}, bf16[1536,768]{1,0:T(8,128)(2,1)}, bf16[768,1536]{1,0:T(8,128)(2,1)}, bf16[2048,1536]{1,0:T(8,128)(2,1)}) custom-call(f32[2048,768]{1,0:T(8,128)} %get-tuple-element.42.gate, bf16[2048,768]{1,0:T(8,128)(2,1)} %get-tuple-element.43.mixed, bf16[2048,1536]{1,0:T(8,128)(2,1)} %bitcast.35, ...), custom_call_target="tpu_custom_call" | custom-call | tf_op jit(solution)/shard_map/middle/pallas_call | solution.py:1334
  171.8 71.0 %mixer_backward.1 = (bf16[2048,1024]{1,0:T(8,128)(2,1)}, bf16[2048,128]{1,0:T(8,128)(2,1)}, f32[8,1024]{1,0:T(8,128)}, f32[512,1536]{1,0:T(8,128)}, bf16[384,1536]{1,0:T(8,128)(2,1)}, /*index=5*/bf16[192,768]{1,0:T(8,128)(2,1)}) custom-call(bf16[2048,1024]{1,0:T(8,128)(2,1)} %get-tuple-element.39.u_ref.halo_ref, ...), custom_call_target="tpu_custom_call" | custom-call | tf_op jit(solution)/shard_map/mixer_backward/pallas_call | solution.py:418
  242.8 69.2 %finish_last.1 = (f32[512,1536]{1,0:T(8,128)}, bf16[192,6528]{1,0:T(8,128)(2,1)}, f32[8,3456]{1,0:T(8,128)}) custom-call(bf16[2048,1536]{1,0:T(8,128)(2,1)} %get-tuple-element.46.normed.hid, bf16[2048,768]{1,0:T(8,128)(2,1)} %get-tuple-element.52.d_gate, bf16[2048,1024]{1,0:T(8,128)(2,1)} %get-tuple-element.53.d_u, ...), custom_call_target="tpu_custom_call" | custom-call | tf_op jit(solution)/shard_map/finish_last/pallas_call | solution.py:1618
  312.0 4.2 %add_bitcast_fusion = f32[1,512,1536]{2,1,0:T(8,128)} fusion(f32[512,1536]{1,0:T(8,128)} %get-tuple-element.51, bf16[1,512,1536]{2,1,0:T(8,128)(2,1)S(1)} %copy-done), kind=kLoop, calls=%fused_computation.1 | loop fusion | flops 1572864 | bytes 7864320 | tf_op jit(solution)/shard_map/broadcast_in_dim | solution.py:1813
  316.7 0.6 slice_reduce_fusion
  317.9 2.5 convert_multiply_fusion
  320.4 2.9 multiply_reduce_fusion
  323.9 1.7 copy.27
  (20 shorter events, 2.4 us)
Async XLA Ops:
  0.6 11.5 %copy-start.1 = (bf16[384,1536]{1,0:T(8,128)(2,1)S(1)}, bf16[384,1536]{1,0:T(8,128)(2,1)}, u32[]{:S(2)}) copy-start(bf16[384,1536]{1,0:T(8,128)(2,1)} %param.22) | copy-start | bytes 3538948
  242.7 69.2 %copy-start = (bf16[1,512,1536]{2,1,0:T(8,128)(2,1)S(1)}, bf16[1,512,1536]{2,1,0:T(8,128)(2,1)}, u32[]{:S(2)}) copy-start(bf16[1,512,1536]{2,1,0:T(8,128)(2,1)} %param.12) | copy-start | bytes 4718596
  312.0 4.2 %copy-start.6 = (f32[8,3456]{1,0:T(8,128)S(1)}, f32[8,3456]{1,0:T(8,128)}, u32[]{:S(2)}) copy-start(f32[8,3456]{1,0:T(8,128)} %get-tuple-element.59) | copy-start | bytes 331780
  312.0 6.0 %copy-start.5 = (bf16[384,1536]{1,0:T(8,128)(2,1)S(1)}, bf16[384,1536]{1,0:T(8,128)(2,1)}, u32[]{:S(2)}) copy-start(bf16[384,1536]{1,0:T(8,128)(2,1)} %get-tuple-element.60) | copy-start | bytes 3538948
  312.0 8.4 %copy-start.4 = (bf16[192,6528]{1,0:T(8,128)(2,1)S(1)}, bf16[192,6528]{1,0:T(8,128)(2,1)}, u32[]{:S(2)}) copy-start(bf16[192,6528]{1,0:T(8,128)(2,1)} %get-tuple-element.58) | copy-start | bytes 7520260
  316.1 4.3 %copy-start.2 = (bf16[192,6448]{1,0:T(8,128)(2,1)S(1)}, bf16[192,6448]{1,0:T(8,128)(2,1)}, u32[]{:S(2)}) copy-start(bf16[192,6448]{1,0:T(8,128)(2,1)} %param.15) | copy-start | bytes 7428100
  320.4 2.9 copy-start.7
  320.4 3.5 %copy-start.3 = (f32[512,1536]{1,0:T(8,128)S(1)}, f32[512,1536]{1,0:T(8,128)}, u32[]{:S(2)}) copy-start(f32[512,1536]{1,0:T(8,128)} %get-tuple-element.57) | copy-start | bytes 9437188
